TPU v7x, 512 devices: a whole 4x4x16 slice. The times are simulated.
512 devices in a mesh: expert: 128 (over y_hi, z, x), dp: 4 (over y_lo, core).
Axes of the slice: x: 4, y: 4 (y_hi: 2, y_lo: 2; y = y_hi * 2 + y_lo), z: 16, core: 2. Of those that a mesh axis runs over, the one named last changes fastest.
Arguments:
- tokens: bfloat16 [12288, 2048], P(('expert', 'dp')), may hold values from -6 to 6
- expert_ids: int32 [12288, 8], P(('expert', 'dp')), may hold values from 0 to 127, all different within a row; in each aligned block of 24 rows (0 to 23, 24 to 47, ...) at most 2 rows name the same one
- route_weight: float32 [12288, 8], P(('expert', 'dp')), may hold values from 0.05 to 0.5
- cotangent: bfloat16 [12288, 2048], P(('expert', 'dp')), may hold values from -6 to 6
- holder: int32 [128], replicated, may hold values from 0 to 127, each once
- partner: int32 [128], replicated, may hold values from 0 to 127, as said below
- up_weight: bfloat16 [128, 2048, 768], P('expert', 'dp'), may hold values from -0.125 to 0.125
- down_weight: bfloat16 [128, 768, 2048], P('expert', None, 'dp'), may hold values from -0.21875 to 0.21875
- up_moment: bfloat16 [128, 2048, 768], P('expert', 'dp'), may hold values from -1.796875 to 1.796875
- down_moment: bfloat16 [128, 768, 2048], P('expert', None, 'dp'), may hold values from -1.796875 to 1.796875
Outputs:
- layer_out: bfloat16 [12288, 2048], P(('expert', 'dp'))
- up_moment_new: bfloat16 [128, 2048, 768], P('expert', 'dp')
- down_moment_new: bfloat16 [128, 768, 2048], P('expert', None, 'dp')
Inputs may be any that keep to these rules, and one draw needn't show every extreme that they name: `expert_ids`: each token names 8 different experts; within each device's block of 24 tokens no expert is named by more than 2 tokens, a bound that some block reaches. `holder`: A permutation of the slots. partner[partner[s]] = s for every slot s, and exactly 2 * (32) slots have partner[s] != s.
All inputs are finite; a program needn't handle non-finite values.
Results may differ from a plain program's by a relative error of at most 0.022.
Values may be sent and summed in bfloat16 or wider, within the bound.
No kernel may reach another device: no remote copies, remote signals or barrier semaphores. Data moves between devices by JAX's collectives and lax.ppermute only.
A program may use at most 64 MiB of HBM per device.

v0:
```python
import jax
import jax.numpy as jnp
from jax import lax
from jax.sharding import PartitionSpec as P

MOMENT_DECAY = 0.9


def silu_slope(preact):
    sigmoid_value = jax.nn.sigmoid(preact)
    return sigmoid_value * (1.0 + preact * (1.0 - sigmoid_value))


def swap_slots(arrays, partner, slot_count):
    stacked = jnp.stack([array_item.reshape(slot_count, -1) for array_item in arrays], axis=1)
    spread = lax.all_to_all(stacked, "expert", split_axis=0, concat_axis=0, tiled=True)
    picked = jnp.take(spread, partner, axis=0)
    landed = lax.all_to_all(picked, "expert", split_axis=0, concat_axis=0, tiled=True)
    return [landed[:, member].reshape(array_item.shape) for member, array_item in enumerate(arrays)]


def body(
    tokens,
    expert_ids,
    route_weight,
    cotangent,
    holder,
    partner,
    up_weight,
    down_weight,
    up_moment,
    down_moment,
):
    tok_count, top_count = expert_ids.shape
    n_slots = lax.axis_size("expert")
    n_groups = lax.axis_size("dp")
    capacity = min(tok_count, max(2, 4 * tok_count * top_count // (3 * n_slots)))
    feature_count = tokens.shape[1]
    quarter = feature_count // n_groups
    slot_range = jnp.arange(n_slots, dtype=jnp.int32)
    held_hit = (holder[:, None] == slot_range[None, :]).astype(jnp.int32)
    target = jnp.sum(held_hit * partner[None, :], axis=1)
    swapped = swap_slots([up_weight, down_weight, up_moment, down_moment], partner, n_slots)
    up_weight, down_weight, up_moment, down_moment = (
        swapped[0],
        swapped[1],
        swapped[2],
        swapped[3],
    )
    flat_ids = expert_ids.reshape(-1)
    expert_hit = (flat_ids[:, None] == slot_range[None, :]).astype(jnp.int32)
    destination = jnp.sum(expert_hit * target[None, :], axis=1)
    dest_hit = (destination[:, None] == slot_range[None, :]).astype(jnp.int32)
    position = jnp.sum((jnp.cumsum(dest_hit, axis=0) - 1) * dest_hit, axis=1)
    entry_index = destination * capacity + position
    slots_total = n_slots * capacity
    select = (jnp.arange(slots_total, dtype=jnp.int32)[:, None] == entry_index[None, :]).reshape(
        slots_total, tok_count, top_count
    )
    picked = jnp.sum(select.astype(jnp.float32), axis=2)
    scaled = jnp.sum(jnp.where(select, route_weight[None, :, :], 0.0), axis=2)
    sent_rows = jnp.dot(
        picked.astype(jnp.bfloat16), tokens, preferred_element_type=jnp.float32
    ).astype(jnp.bfloat16)
    sent_grads = jnp.dot(
        scaled,
        cotangent.astype(jnp.float32),
        precision=lax.Precision.HIGHEST,
        preferred_element_type=jnp.float32,
    ).astype(jnp.bfloat16)
    outgoing = jnp.stack([sent_rows, sent_grads], axis=0).reshape(
        1, 2, n_slots, capacity, feature_count
    )
    arrived = lax.all_to_all(
        lax.all_to_all(outgoing, "expert", split_axis=2, concat_axis=2, tiled=True),
        "dp",
        split_axis=4,
        concat_axis=0,
        tiled=True,
    )
    rows_in = arrived[:, 0].reshape(-1, quarter)
    grads_in = arrived[:, 1].reshape(-1, quarter)
    up_local = up_weight[0]
    down_local = down_weight[0]
    pre_part = jnp.dot(rows_in, up_local, preferred_element_type=jnp.float32)
    back_part = lax.dot_general(
        grads_in, down_local, (((1,), (1,)), ((), ())), preferred_element_type=jnp.float32
    )
    preact, back_sum = (
        lax.psum(pre_part.astype(jnp.bfloat16), "dp").astype(jnp.float32),
        lax.psum(back_part.astype(jnp.bfloat16), "dp").astype(jnp.float32),
    )
    hidden = jax.nn.silu(preact).astype(jnp.bfloat16)
    pre_grad = (back_sum * silu_slope(preact)).astype(jnp.bfloat16)
    out_part = jnp.dot(hidden, down_local, preferred_element_type=jnp.float32).astype(jnp.bfloat16)
    up_grad = lax.dot_general(
        rows_in, pre_grad, (((0,), (0,)), ((), ())), preferred_element_type=jnp.float32
    )
    down_grad = lax.dot_general(
        hidden, grads_in, (((0,), (0,)), ((), ())), preferred_element_type=jnp.float32
    )
    returned = lax.all_to_all(
        lax.all_to_all(
            out_part.reshape(n_groups, n_slots, capacity, quarter),
            "expert",
            split_axis=1,
            concat_axis=1,
            tiled=True,
        ),
        "dp",
        split_axis=0,
        concat_axis=3,
        tiled=True,
    )
    layer_out = jnp.dot(
        scaled.T,
        returned.reshape(slots_total, feature_count).astype(jnp.float32),
        precision=lax.Precision.HIGHEST,
        preferred_element_type=jnp.float32,
    ).astype(jnp.bfloat16)
    new_up = (
        MOMENT_DECAY * up_moment.astype(jnp.float32) + (1.0 - MOMENT_DECAY) * up_grad[None]
    ).astype(jnp.bfloat16)
    new_down = (
        MOMENT_DECAY * down_moment.astype(jnp.float32) + (1.0 - MOMENT_DECAY) * down_grad[None]
    ).astype(jnp.bfloat16)
    return (layer_out, new_up, new_down)


def solution(mesh):
    return jax.shard_map(
        body,
        mesh=mesh,
        in_specs=(
            P(("expert", "dp"), None),
            P(("expert", "dp"), None),
            P(("expert", "dp"), None),
            P(("expert", "dp"), None),
            P(),
            P(),
            P("expert", "dp", None),
            P("expert", None, "dp"),
            P("expert", "dp", None),
            P("expert", None, "dp"),
        ),
        out_specs=(P(("expert", "dp"), None), P("expert", "dp", None), P("expert", None, "dp")),
        check_vma=False,
    )
```

profile of v0, /device:TPU:1, one launch (start us, length us, event | category | flops | bytes accessed | tf_op | source)
XLA Modules:
  0.0 699.1 jit_solution(17659588930216302587)
XLA Ops:
  13.7 4.1 pad_maximum_fusion.1
  17.8 23.1 %all-to-all-start = ((bf16[1,2,128,2,2048]{4,3,1,0,2:T(2,128)(2,1)}), bf16[1,2,128,2,2048]{4,3,1,0,2:T(2,128)(2,1)S(1)}, u32[]{:S(2)}, u32[]{:S(2)}) async-start(bf16[1,2,128,2,2048]{4,3,1,0,2:T(2,128)(2,1)} %pad_maximum_fusion.1), calls=%async_computation | async-start | bytes 4194304 | tf_op jit(solution)/shard_map/all_to_all | solution.py:75
  42.7 5.6 stack_reshape.17
  50.2 5.6 stack_reshape.19
  55.7 10.0 %pad_maximum_fusion = bf16[128,4,3072]{2,1,0:T(4,128)(2,1)} fusion(bf16[128,1,3072]{2,1,0:T(2,128)(2,1)} %stack_reshape.19, bf16[128,1,3072]{2,1,0:T(2,128)(2,1)} %stack_reshape.18, bf16[128,1,3072]{2,1,0:T(2,128)(2,1)} %stack_reshape.17, bf16[128,1,3072]{2,1,0:T(2,128)(2,1)} %stack_reshape.16), kind=kLoop, calls=%fused_computation.12 | loop fusion | flops 12582912 | bytes 6291456 | tf_op jit(solution)/shard_map/stack | solution.py:15
  65.7 76.4 %all-to-all-done = bf16[1,2,128,2,2048]{4,3,1,0,2:T(2,128)(2,1)S(1)} async-done(((bf16[1,2,128,2,2048]{4,3,1,0,2:T(2,128)(2,1)}), bf16[1,2,128,2,2048]{4,3,1,0,2:T(2,128)(2,1)S(1)}, u32[]{:S(2)}, u32[]{:S(2)}) %all-to-all-start) | async-done | bytes 2097184 | tf_op jit(solution)/shard_map/all_to_all | solution.py:75
  143.4 7.9 %all-to-all-start.2 = ((bf16[128,4,3072]{2,1,0:T(4,128)(2,1)}), bf16[128,4,3072]{2,1,0:T(4,128)(2,1)S(1)}, u32[]{:S(2)}, u32[]{:S(2)}) async-start(bf16[128,4,3072]{2,1,0:T(4,128)(2,1)} %pad_maximum_fusion), calls=%async_computation.2 | async-start | bytes 6291456 | tf_op jit(solution)/shard_map/all_to_all | solution.py:16
  151.3 8.6 %copy.70 = bf16[1,2,128,2,2048]{2,3,1,0,4:T(2,128)(2,1)} copy(bf16[1,2,128,2,2048]{4,3,1,0,2:T(2,128)(2,1)} %copy-done.2) | data formatting | bytes 4194304 | tf_op jit(solution)/shard_map/all_to_all | solution.py:75
  159.9 133.2 %all-to-all-done.2 = bf16[128,4,3072]{2,1,0:T(4,128)(2,1)S(1)} async-done(((bf16[128,4,3072]{2,1,0:T(4,128)(2,1)}), bf16[128,4,3072]{2,1,0:T(4,128)(2,1)S(1)}, u32[]{:S(2)}, u32[]{:S(2)}) %all-to-all-start.2) | async-done | bytes 3145760 | tf_op jit(solution)/shard_map/all_to_all | solution.py:16
  293.1 11.4 %all-to-all-start.1 = ((bf16[1,2,128,2,2048]{2,3,1,0,4:T(2,128)(2,1)}), bf16[1,2,128,2,2048]{2,3,1,0,4:T(2,128)(2,1)}, u32[]{:S(2)}, u32[]{:S(2)}) async-start(bf16[1,2,128,2,2048]{2,3,1,0,4:T(2,128)(2,1)} %copy.70), calls=%async_computation.1 | async-start | bytes 4194304 | tf_op jit(solution)/shard_map/all_to_all | solution.py:74
  304.5 4.7 gather_fusion
  309.2 5.1 broadcast_select_fusion
  314.4 15.1 %all-to-all-done.1 = bf16[1,2,128,2,2048]{2,3,1,0,4:T(2,128)(2,1)} async-done(((bf16[1,2,128,2,2048]{2,3,1,0,4:T(2,128)(2,1)}), bf16[1,2,128,2,2048]{2,3,1,0,4:T(2,128)(2,1)}, u32[]{:S(2)}, u32[]{:S(2)}) %all-to-all-start.1) | async-done | bytes 2097184 | tf_op jit(solution)/shard_map/all_to_all | solution.py:74
  329.4 6.2 all-to-all-start.3
  339.3 3.7 copy.80
  345.2 3.7 copy.72
  351.2 129.2 %all-to-all-done.3 = bf16[128,4,3072]{2,1,0:T(4,128)(2,1)S(1)} async-done(((bf16[128,4,3072]{2,1,0:T(4,128)(2,1)}), bf16[128,4,3072]{2,1,0:T(4,128)(2,1)S(1)}, u32[]{:S(2)}, u32[]{:S(2)}) %all-to-all-start.3) | async-done | bytes 3145760 | tf_op jit(solution)/shard_map/all_to_all | solution.py:18
  480.5 7.5 %slice_reduce_fusion.1 = (bf16[128,3072]{1,0:T(8,128)(2,1)}, bf16[128,3072]{1,0:T(8,128)(2,1)}) fusion(bf16[128,4,3072]{2,1,0:T(4,128)(2,1)S(1)} %all-to-all-done.3), kind=kLoop, calls=%fused_computation.27 | loop fusion | bytes 3145728 | tf_op jit(solution)/shard_map/slice | solution.py:19
  490.3 2.5 squeeze_reshape_squeeze.7
  492.7 3.7 convolution_convert_fusion.4
  498.7 82.4 %all-reduce.4.cloned.1.call-done = (bf16[1024,768]{1,0:T(8,128)(2,1)}, bf16[1024,768]{1,0:T(8,128)(2,1)}) async-done(((bf16[1024,768]{1,0:T(8,128)(2,1)}, bf16[1024,768]{1,0:T(8,128)(2,1)}), (bf16[1024,768]{1,0:T(8,128)(2,1)}, bf16[1024,768]{1,0:T(8,128)(2,1)})) %all-reduce.4.cloned.1.call-update) | async-done | bytes 3145744 | tf_op jit(solution)/shard_map/psum | solution.py:90
  581.1 3.6 convolution_convert_fusion.5
  587.0 2.9 copy.77
  589.9 19.5 %all-to-all-start.4 = ((bf16[4,128,2,512]{3,2,0,1:T(2,128)(2,1)}), bf16[4,128,2,512]{3,2,0,1:T(2,128)(2,1)}, u32[]{:S(2)}, u32[]{:S(2)}) async-start(bf16[4,128,2,512]{3,2,0,1:T(2,128)(2,1)} %copy.77), calls=%async_computation.4 | async-start | bytes 2097152 | tf_op jit(solution)/shard_map/all_to_all | solution.py:103
  609.4 12.0 %fusion.9 = (f32[128,3072]{1,0:T(8,128)}, f32[128,3072]{1,0:T(8,128)}) fusion(bf16[128,4,3072]{2,1,0:T(4,128)(2,1)S(1)} %all-to-all-done.3), kind=kLoop, calls=%fused_computation.22 | loop fusion | flops 1572864 | bytes 4718592 | tf_op jit(solution)/shard_map/mul | solution.py:125
  621.4 2.7 mul.92
  624.6 4.1 fusion.19
  628.7 36.4 %all-to-all-done.4 = bf16[4,128,2,512]{3,2,0,1:T(2,128)(2,1)} async-done(((bf16[4,128,2,512]{3,2,0,1:T(2,128)(2,1)}), bf16[4,128,2,512]{3,2,0,1:T(2,128)(2,1)}, u32[]{:S(2)}, u32[]{:S(2)}) %all-to-all-start.4) | async-done | bytes 1048608 | tf_op jit(solution)/shard_map/all_to_all | solution.py:103
  665.1 3.0 copy.78
  668.1 7.3 %all-to-all-start.5 = ((bf16[4,128,2,512]{3,2,1,0:T(2,128)(2,1)}), bf16[4,128,2,512]{3,2,1,0:T(2,128)(2,1)S(1)}, u32[]{:S(2)}, u32[]{:S(2)}) async-start(bf16[4,128,2,512]{3,2,1,0:T(2,128)(2,1)} %copy.78), calls=%async_computation.5 | async-start | bytes 2097152 | tf_op jit(solution)/shard_map/all_to_all | solution.py:102
  675.4 4.8 fusion.16
  680.2 8.8 %all-to-all-done.5 = bf16[4,128,2,512]{3,2,1,0:T(2,128)(2,1)S(1)} async-done(((bf16[4,128,2,512]{3,2,1,0:T(2,128)(2,1)}), bf16[4,128,2,512]{3,2,1,0:T(2,128)(2,1)S(1)}, u32[]{:S(2)}, u32[]{:S(2)}) %all-to-all-start.5) | async-done | bytes 1048608 | tf_op jit(solution)/shard_map/all_to_all | solution.py:102
  (60 shorter events, 29.6 us)
Async XLA Ops:
  7.2 3.6 copy-start
  10.0 1.9 copy-start.8
  17.8 23.1 %copy-start.6 = (bf16[1,512,768]{2,1,0:T(8,128)(2,1)S(1)}, bf16[1,512,768]{2,1,0:T(8,128)(2,1)}, u32[]{:S(2)}) copy-start(bf16[1,512,768]{2,1,0:T(8,128)(2,1)} %param.16) | copy-start | bytes 2359300
  17.8 124.3 %all-to-all-start = ((bf16[1,2,128,2,2048]{4,3,1,0,2:T(2,128)(2,1)}), bf16[1,2,128,2,2048]{4,3,1,0,2:T(2,128)(2,1)S(1)}, u32[]{:S(2)}, u32[]{:S(2)}) async-start(bf16[1,2,128,2,2048]{4,3,1,0,2:T(2,128)(2,1)} %pad_maximum_fusion.1), calls=%async_computation | async-start | bytes 4194304 | tf_op jit(solution)/shard_map/all_to_all | solution.py:75
  42.7 5.6 copy-start.7
  142.1 1.4 copy-start.2
  143.4 149.6 %all-to-all-start.2 = ((bf16[128,4,3072]{2,1,0:T(4,128)(2,1)}), bf16[128,4,3072]{2,1,0:T(4,128)(2,1)S(1)}, u32[]{:S(2)}, u32[]{:S(2)}) async-start(bf16[128,4,3072]{2,1,0:T(4,128)(2,1)} %pad_maximum_fusion), calls=%async_computation.2 | async-start | bytes 6291456 | tf_op jit(solution)/shard_map/all_to_all | solution.py:16
  159.8 144.6 %copy-start.9 = (s32[128]{0:T(128)S(1)}, s32[128]{0:T(128)}, u32[]{:S(2)}) copy-start(s32[128]{0:T(128)} %param.15) | copy-start | bytes 1540
  293.1 36.4 %all-to-all-start.1 = ((bf16[1,2,128,2,2048]{2,3,1,0,4:T(2,128)(2,1)}), bf16[1,2,128,2,2048]{2,3,1,0,4:T(2,128)(2,1)}, u32[]{:S(2)}, u32[]{:S(2)}) async-start(bf16[1,2,128,2,2048]{2,3,1,0,4:T(2,128)(2,1)} %copy.70), calls=%async_computation.1 | async-start | bytes 4194304 | tf_op jit(solution)/shard_map/all_to_all | solution.py:74
  329.4 151.0 %all-to-all-start.3 = ((bf16[128,4,3072]{2,1,0:T(4,128)(2,1)}), bf16[128,4,3072]{2,1,0:T(4,128)(2,1)S(1)}, u32[]{:S(2)}, u32[]{:S(2)}) async-start(bf16[128,4,3072]{2,1,0:T(4,128)(2,1)} %broadcast_select_fusion), calls=%async_computation.3 | async-start | bytes 6291456 | tf_op jit(solution)/shard_map/all_to_all | solution.py:18
  335.7 245.4 %all-reduce.4.cloned.1.call-start = ((), (), s32[]{:S(2)}) async-start(), calls=%async_computation.6 | async-start | bytes 6291456 | tf_op jit(solution)/shard_map/psum | solution.py:90
  492.7 3.7 copy-start.4
  492.7 3.7 copy-start.5
  589.9 75.2 %all-to-all-start.4 = ((bf16[4,128,2,512]{3,2,0,1:T(2,128)(2,1)}), bf16[4,128,2,512]{3,2,0,1:T(2,128)(2,1)}, u32[]{:S(2)}, u32[]{:S(2)}) async-start(bf16[4,128,2,512]{3,2,0,1:T(2,128)(2,1)} %copy.77), calls=%async_computation.4 | async-start | bytes 2097152 | tf_op jit(solution)/shard_map/all_to_all | solution.py:103
  621.4 2.7 copy-start.3
  668.1 20.9 %all-to-all-start.5 = ((bf16[4,128,2,512]{3,2,1,0:T(2,128)(2,1)}), bf16[4,128,2,512]{3,2,1,0:T(2,128)(2,1)S(1)}, u32[]{:S(2)}, u32[]{:S(2)}) async-start(bf16[4,128,2,512]{3,2,1,0:T(2,128)(2,1)} %copy.78), calls=%async_computation.5 | async-start | bytes 2097152 | tf_op jit(solution)/shard_map/all_to_all | solution.py:102
  689.0 2.8 copy-start.1
Sparse Core Ops, SparseCore 0:
  498.8 82.2 all-reduce.3
where the time goes:
time: 709 us; the launch traced here: 699 us
  waiting for transfers between devices  482 us (68%)
  starting transfers between devices  75.7 us (11%)
  local copies, waits for them, and re-layouts  73.2 us (10%)
  other arithmetic  32.9 us (5%)
  matrix products  21.1 us (3%)
  between operations  14.7 us (2%)
    all_to_all x1, waiting for transfers between devices, swap_slots(): lax.all_to_all(stacked, 'expert', split_axis=0, concat_axis=0, tiled=True)  133 us
    all_to_all x1, waiting for transfers between devices, swap_slots(): lax.all_to_all(picked, 'expert', split_axis=0, concat_axis=0, tiled=True)  129 us
    psum x1, waiting for transfers between devices, body(): lax.psum(pre_part.astype(jnp.bfloat16), 'dp').astype(jnp.float32)  82.4 us
    all_to_all x1, waiting for transfers between devices, body(): lax.all_to_all(outgoing, 'expert', split_axis=2, concat_axis=2, tiled=True)  76.4 us
    all_to_all x1, waiting for transfers between devices, body(): lax.all_to_all(out_part.reshape(n_groups, n_slots, capacity, quarter), 'e...  36.4 us
    all_to_all x1, starting transfers between devices, body(): lax.all_to_all(outgoing, 'expert', split_axis=2, concat_axis=2, tiled=True)  23.1 us
    all_to_all x1, starting transfers between devices, body(): lax.all_to_all(out_part.reshape(n_groups, n_slots, capacity, quarter), 'e...  19.5 us
    all_to_all x1, waiting for transfers between devices, body(): lax.all_to_all(lax.all_to_all(outgoing, 'expert', split_axis=2, concat_ax...  15.1 us
  transfers between devices with their start and end apart: 7, of which 7 were waited for; matrix products, arithmetic and copies ran while one was open for 12% of the time, Pallas kernels for 0%

commit v1 on v0

v1 whole, which is shorter than its diff:
```python
import jax
import jax.numpy as jnp
from jax import lax
from jax.experimental import pallas as pl
from jax.experimental.pallas import tpu as pltpu
from jax.sharding import Mesh, PartitionSpec as P

MOMENT_DECAY = 0.9
AXES = ("yh", "zh", "zp", "x", "yl", "core")
SLOT_AXES = ("yh", "zh", "zp", "x")
GROUP_AXES = ("yh", "zp", "x")
DP_AXES = ("yl", "core")
BF16 = jnp.bfloat16
F32 = jnp.float32
FLIP = [(0, 1), (1, 0)]
VMEM = pl.BlockSpec(memory_space=pltpu.VMEM)
SMEM = pl.BlockSpec(memory_space=pltpu.SMEM)


def call(kernel, name, out_shape, in_specs, flops, moved):
    outs = jax.tree.map(lambda _: VMEM, out_shape)
    return pl.pallas_call(
        kernel,
        name=name,
        out_shape=out_shape,
        in_specs=in_specs,
        out_specs=outs,
        compiler_params=pltpu.CompilerParams(vmem_limit_bytes=48 * 1024 * 1024),
        cost_estimate=pl.CostEstimate(flops=flops, bytes_accessed=moved, transcendentals=0),
    )


def split3(value):
    high = value.astype(BF16)
    rest = value - high.astype(F32)
    middle = rest.astype(BF16)
    low = (rest - middle.astype(F32)).astype(BF16)
    return high, middle, low


def pack_kernel(tok_ref, cot_ref, ids_ref, weight_ref, holder_ref, out_ref):
    rows, top = ids_ref.shape
    width = tok_ref.shape[1]
    experts = holder_ref.shape[1]
    ids = ids_ref[...]
    weights = weight_ref[...]
    lane = lax.broadcasted_iota(jnp.int32, (rows, experts), 1)
    hits = [(ids[:, k : k + 1] == lane).astype(F32) for k in range(top)]
    hit = sum(hits[1:], hits[0])
    earlier = (
        lax.broadcasted_iota(jnp.int32, (rows, rows), 0)
        > lax.broadcasted_iota(jnp.int32, (rows, rows), 1)
    ).astype(F32)
    before = jnp.dot(earlier, hit, preferred_element_type=F32)
    base = 2.0 * holder_ref[...].astype(F32) + before
    high, middle, low = split3(weights)
    meta_lane = lax.broadcasted_iota(jnp.int32, (rows, 128), 1)
    meta = jnp.zeros((rows, 128), F32)
    for k in range(top):
        code = jnp.sum(hits[k] * base, axis=1, keepdims=True)
        meta = jnp.where(meta_lane == k, code, meta)
        for place, part in enumerate((high, middle, low)):
            meta = jnp.where(
                meta_lane == (place + 1) * top + k, part.astype(F32)[:, k : k + 1], meta
            )
    out_ref[:, :width] = tok_ref[...]
    out_ref[:, width : 2 * width] = cot_ref[...]
    out_ref[:, 2 * width :] = meta.astype(BF16)


def select_kernel(plane_ref, gathered_ref, out_ref, share_ref):
    total = gathered_ref.shape[0]
    targets, quarters, per_target, _ = out_ref.shape
    quarter = out_ref.shape[3] // 2
    width = quarters * quarter
    top = 8
    rows = targets * per_target
    block = total // (per_target // 2)
    plane = plane_ref[0]
    meta = gathered_ref[:, 2 * width :].astype(F32)
    row = lax.broadcasted_iota(jnp.int32, (total, rows), 1)
    token = lax.broadcasted_iota(jnp.int32, (total, rows), 0)
    target = row >> 4
    first = ((row >> 1) & 7) * block
    inside = (token >= first) & (token < first + block)
    slot = (target >> 3) * 64 + plane * 8 + (target & 7)
    wanted = jnp.where(inside, slot * 2 + (row & 1), -1).astype(F32)
    picked = jnp.zeros((total, rows), F32)
    share = jnp.zeros((total, rows), F32)
    for k in range(top):
        match = meta[:, k : k + 1] == wanted
        weight = (
            meta[:, top + k : top + k + 1]
            + meta[:, 2 * top + k : 2 * top + k + 1]
            + meta[:, 3 * top + k : 3 * top + k + 1]
        )
        picked = jnp.where(match, 1.0, picked)
        share = jnp.where(match, weight, share)
    share_ref[...] = share
    picked_t = jnp.transpose(picked).astype(BF16)
    shares_t = split3(jnp.transpose(share))
    for q in range(quarters):
        at = q * quarter
        sent = jnp.dot(
            picked_t, gathered_ref[:, at : at + quarter], preferred_element_type=F32
        ).astype(BF16)
        out_ref[:, q, :, :quarter] = sent.reshape(targets, per_target, quarter)
        cot = gathered_ref[:, width + at : width + at + quarter]
        grads = sum(jnp.dot(part, cot, preferred_element_type=F32) for part in shares_t)
        out_ref[:, q, :, quarter:] = grads.astype(BF16).reshape(targets, per_target, quarter)


def forward_kernel(me_ref, rows_ref, *refs):
    ups, downs, out_ref = refs[:4], refs[4:8], refs[8]
    targets, _, per_target, double = rows_ref.shape
    quarter = double // 2
    count = targets * per_target
    hidden_count = ups[0].shape[1]
    me = me_ref[0]
    preact = jnp.zeros((count, hidden_count), F32)
    back = jnp.zeros((count, hidden_count), F32)
    for j in range(4):
        both = rows_ref[:, me ^ j].reshape(count, double)
        preact = preact + jnp.dot(both[:, :quarter], ups[j][...], preferred_element_type=F32)
        back = back + lax.dot_general(
            both[:, quarter:],
            downs[j][...],
            (((1,), (1,)), ((), ())),
            preferred_element_type=F32,
        )
    sigmoid = 1.0 / (1.0 + jnp.exp(-preact))
    out_ref[:, :hidden_count] = (preact * sigmoid).astype(BF16)
    out_ref[:, hidden_count:] = (back * sigmoid * (1.0 + preact * (1.0 - sigmoid))).astype(BF16)


def expert_out_kernel(me_ref, acts_ref, *refs):
    downs, out_ref = refs[:4], refs[4]
    targets, _, per_target, quarter = out_ref.shape
    hidden = acts_ref[:, : downs[0].shape[0]]
    me = me_ref[0]
    for j in range(4):
        part = jnp.dot(hidden, downs[j][...], preferred_element_type=F32).astype(BF16)
        out_ref[:, me ^ j] = part.reshape(targets, per_target, quarter)


def combine_kernel(share_ref, returned_ref, out_ref):
    targets, quarters, per_target, quarter = returned_ref.shape
    shares = split3(share_ref[...])
    for q in range(quarters):
        rows = returned_ref[:, q].reshape(targets * per_target, quarter)
        mixed = sum(jnp.dot(part, rows, preferred_element_type=F32) for part in shares)
        out_ref[:, q * quarter : (q + 1) * quarter] = mixed.astype(BF16)


def moment_kernel(me_ref, rows_ref, a0, a1, a2, a3, up_ref, down_ref, out_ref):
    acts = (a0, a1, a2, a3)
    me = me_ref[0]
    features, hidden_count = up_ref.shape
    over_rows = (((0,), (0,)), ((), ()))
    up_grad = jnp.zeros((features, hidden_count), F32)
    down_grad = jnp.zeros((hidden_count, features), F32)
    for j in range(4):
        rows = rows_ref[me ^ j].reshape(acts[j].shape[0], 2 * features)
        up_grad = up_grad + lax.dot_general(
            rows[:, :features],
            acts[j][:, hidden_count:],
            over_rows,
            preferred_element_type=F32,
        )
        down_grad = down_grad + lax.dot_general(
            acts[j][:, :hidden_count],
            rows[:, features:],
            over_rows,
            preferred_element_type=F32,
        )
    rest = 1.0 - MOMENT_DECAY
    up = (MOMENT_DECAY * up_ref[...].astype(F32) + rest * up_grad).astype(BF16)
    down = (MOMENT_DECAY * down_ref[...].astype(F32) + rest * down_grad).astype(BF16)
    up = up.reshape(32, 16, hidden_count)
    for j in range(2):
        for c in range(3):
            at = j * 384 + c * 128
            out_ref[j * 32 : (j + 1) * 32, c * 16 : (c + 1) * 16, :] = up[:, :, at : at + 128]
    down = down.reshape(16, 48, features)
    for j in range(4):
        out_ref[64 + j * 16 : 80 + j * 16] = down[:, :, j * 128 : (j + 1) * 128]


def pick_kernel(partner_ref, spread_ref, out_ref):
    def step(slot, carry):
        out_ref[slot] = spread_ref[partner_ref[slot]]
        return carry

    lax.fori_loop(0, out_ref.shape[0], step, 0, unroll=8)


def unpack_kernel(pieces_ref, up_ref, down_ref):
    for j in range(2):
        for c in range(3):
            at = j * 384 + c * 128
            part = pieces_ref[j * 32 : (j + 1) * 32, c * 16 : (c + 1) * 16, :]
            up_ref[:, at : at + 128] = part.reshape(512, 128)
    for j in range(4):
        part = pieces_ref[64 + j * 16 : 80 + j * 16]
        down_ref[:, j * 128 : (j + 1) * 128] = part.reshape(768, 128)


def shape_of(dims, dtype=BF16):
    return jax.ShapeDtypeStruct(dims, dtype)


def body(
    tokens,
    expert_ids,
    route_weight,
    cotangent,
    holder,
    partner,
    up_weight,
    down_weight,
    up_moment,
    down_moment,
):
    plane = lax.axis_index("zh").reshape(1).astype(jnp.int32)
    me = lax.axis_index(DP_AXES).reshape(1).astype(jnp.int32)

    packed = call(pack_kernel, "pack", shape_of((24, 4224)), [VMEM] * 5, 10**6, 4 * 10**5)(
        tokens, cotangent, expert_ids, route_weight, holder.reshape(1, -1)
    )
    gathered = lax.all_gather(packed, "zh", axis=0, tiled=True)

    up0, down0 = up_weight[0], down_weight[0]
    up2, down2 = lax.ppermute(up0, "yl", FLIP), lax.ppermute(down0, "yl", FLIP)
    up1, down1 = lax.ppermute(up0, "core", FLIP), lax.ppermute(down0, "core", FLIP)
    up3, down3 = lax.ppermute(up2, "core", FLIP), lax.ppermute(down2, "core", FLIP)
    ups, downs = (up0, up1, up2, up3), (down0, down1, down2, down3)

    outgoing, share = call(
        select_kernel,
        "select",
        (shape_of((16, 4, 16, 1024)), shape_of((192, 256), F32)),
        [SMEM, VMEM],
        10**9,
        4 * 10**6,
    )(plane, gathered)
    rows = lax.all_to_all(outgoing, GROUP_AXES, split_axis=0, concat_axis=0, tiled=True)
    by_feature = lax.all_to_all(
        rows.transpose(1, 0, 2, 3), DP_AXES, split_axis=0, concat_axis=0, tiled=True
    )

    acts = call(
        forward_kernel,
        "forward",
        shape_of((256, 1536)),
        [SMEM] + [VMEM] * 9,
        16 * 10**8,
        9 * 10**6,
    )(me, rows, *ups, *downs)
    acts2 = lax.ppermute(acts, "yl", FLIP)
    acts1 = lax.ppermute(acts, "core", FLIP)
    acts3 = lax.ppermute(acts2, "core", FLIP)

    expert_out = call(
        expert_out_kernel,
        "expert_out",
        shape_of((16, 4, 16, 512)),
        [SMEM] + [VMEM] * 5,
        8 * 10**8,
        5 * 10**6,
    )(me, acts, *downs)

    pieces = call(
        moment_kernel,
        "moments",
        shape_of((128, 48, 128)),
        [SMEM] + [VMEM] * 7,
        32 * 10**8,
        9 * 10**6,
    )(me, by_feature, acts, acts1, acts2, acts3, up_moment[0], down_moment[0])

    returned = lax.all_to_all(expert_out, GROUP_AXES, split_axis=0, concat_axis=0, tiled=True)
    partial = call(
        combine_kernel, "combine", shape_of((192, 2048)), [VMEM, VMEM], 6 * 10**8, 2 * 10**6
    )(share, returned)
    layer_out = lax.psum_scatter(partial, "zh", scatter_dimension=0, tiled=True)

    spread = lax.all_to_all(pieces, SLOT_AXES, split_axis=0, concat_axis=0, tiled=True)
    chosen = call(
        pick_kernel, "pick", shape_of((128, 48, 128)), [SMEM, VMEM], 0, 3 * 10**6
    )(partner, spread)
    landed = lax.all_to_all(chosen, SLOT_AXES, split_axis=0, concat_axis=0, tiled=True)
    new_up, new_down = call(
        unpack_kernel,
        "unpack",
        (shape_of((512, 768)), shape_of((768, 512))),
        [VMEM],
        0,
        3 * 10**6,
    )(landed)
    return layer_out, new_up[None], new_down[None]


def solution(mesh):
    wide = Mesh(mesh.devices.reshape(2, 8, 2, 4, 2, 2), AXES)
    return jax.shard_map(
        body,
        mesh=wide,
        in_specs=(
            P(AXES, None),
            P(AXES, None),
            P(AXES, None),
            P(AXES, None),
            P(),
            P(),
            P(SLOT_AXES, DP_AXES, None),
            P(SLOT_AXES, None, DP_AXES),
            P(SLOT_AXES, DP_AXES, None),
            P(SLOT_AXES, None, DP_AXES),
        ),
        out_specs=(
            P(AXES, None),
            P(SLOT_AXES, DP_AXES, None),
            P(SLOT_AXES, None, DP_AXES),
        ),
        check_vma=False,
    )
```

time: 709 us -> 434 us (0.61)
  waiting for transfers between devices: 482 us -> 310 us
  local copies, waits for them, and re-layouts: 73.2 us -> 16.9 us
  other arithmetic: 32.9 us -> 0 us
  Pallas kernels: 0 us -> 21.2 us
  matrix products: 21.1 us -> 0 us
  starting transfers between devices: 75.7 us -> 67.9 us
    all_to_all x6 -> x5, waiting for transfers between devices: 399 us -> 176 us  [the longest x1 88.8 us: body(): lax.all_to_all(chosen, SLOT_AXES, split_axis=0, concat_axis=0, tiled=True)]
    psum x1 -> x0, waiting for transfers between devices: 82.4 us -> none  [body(): lax.psum(pre_part.astype(jnp.bfloat16), 'dp').astype(jnp.float32)]
    ppermute x0 -> x9, waiting for transfers between devices: none -> 71 us  [the longest x1 30.1 us: body(): acts2 = lax.ppermute(acts, 'yl', FLIP)]
    all_gather x0 -> x1, waiting for transfers between devices: none -> 62.1 us  [body(): gathered = lax.all_gather(packed, 'zh', axis=0, tiled=True)]
    all_to_all x6 -> x5, starting transfers between devices: 75.4 us -> 38.4 us  [the longest x1 14.8 us: body(): lax.all_to_all(pieces, SLOT_AXES, split_axis=0, concat_axis=0, tiled=True)]
    ppermute x0 -> x9, starting transfers between devices: none -> 29.4 us  [the longest x1 5.1 us: body(): lax.ppermute(up0, 'core', FLIP)]
    another operation x13 -> x0, local copies, waits for them, and re-layouts: 25.6 us -> none  [the longest x4 14.8 us: swap_slots(): jnp.stack([array_item.reshape(slot_count, -1) for array_item in arrays],...]
    pallas_call x0 -> x8, Pallas kernels: none -> 21.2 us  [the longest x1 4.9 us: body(): call(moment_kernel, 'moments', shape_of((128, 48, 128)), [SMEM] + [VMEM]...]
  transfers between devices with their start and end apart: 7 -> 16, of which waited for: 7 -> 8; matrix products, arithmetic and copies ran while one was open for 12% -> 1% of each run, Pallas kernels for 0% -> 3%
where the time goes in v1:
time: 434 us; the launch traced here: 430 us
  waiting for transfers between devices  310 us (71%)
  starting transfers between devices  67.9 us (16%)
  Pallas kernels  21.2 us (5%)
  local copies, waits for them, and re-layouts  16.9 us (4%)
  between operations  14.3 us (3%)
    all_to_all x1, waiting for transfers between devices, body(): lax.all_to_all(chosen, SLOT_AXES, split_axis=0, concat_axis=0, tiled=True)  88.8 us
    all_to_all x1, waiting for transfers between devices, body(): lax.all_to_all(pieces, SLOT_AXES, split_axis=0, concat_axis=0, tiled=True)  73.9 us
    all_gather x1, waiting for transfers between devices, body(): gathered = lax.all_gather(packed, 'zh', axis=0, tiled=True)  62.1 us
    ppermute x1, waiting for transfers between devices, body(): acts2 = lax.ppermute(acts, 'yl', FLIP)  30.1 us
    ppermute x1, waiting for transfers between devices, body(): lax.ppermute(up0, 'yl', FLIP)  27.1 us
    all_to_all x1, starting transfers between devices, body(): lax.all_to_all(pieces, SLOT_AXES, split_axis=0, concat_axis=0, tiled=True)  14.8 us
    all_to_all x1, waiting for transfers between devices, body(): lax.all_to_all(expert_out, GROUP_AXES, split_axis=0, concat_axis=0, tiled...  13.7 us
    unnamed x38, local copies, waits for them, and re-layouts  13.6 us
  transfers between devices with their start and end apart: 16, of which 8 were waited for; matrix products, arithmetic and copies ran while one was open for 1% of the time, Pallas kernels for 3%

profile of v1, /device:TPU:1, one launch (start us, length us, event | category | flops | bytes accessed | tf_op | source)
XLA Modules:
  0.0 429.7 jit_solution(16852566816806211972)
XLA Ops:
  12.3 62.1 %all-gather.2.cloned.1.call-done.gathered_ref = bf16[192,4224]{1,0:T(8,128)(2,1)} async-done(((bf16[24,4224]{1,0:T(8,128)(2,1)}), bf16[192,4224]{1,0:T(8,128)(2,1)}) %all-gather.2.cloned.1.call-update) | async-done | bytes 1622032 | tf_op jit(solution)/shard_map/all_gather | solution.py:230
  74.4 1.4 copy-done.13
  75.8 3.4 select.1
  79.9 7.2 %all-to-all-start = ((bf16[16,4,16,1024]{3,2,1,0:T(8,128)(2,1)}), bf16[16,4,16,1024]{3,2,1,0:T(8,128)(2,1)}, u32[]{:S(2)}, u32[]{:S(2)}) async-start(bf16[16,4,16,1024]{3,2,1,0:T(8,128)(2,1)} %get-tuple-element.8), calls=%async_computation | async-start | bytes 4194304 | tf_op jit(solution)/shard_map/all_to_all | solution.py:246
  87.1 2.0 collective-permute-start.1
  89.1 3.3 collective-permute-start.4
  92.4 5.1 %collective-permute-start = (bf16[512,768]{1,0:T(8,128)(2,1)}, bf16[512,768]{1,0:T(8,128)(2,1)}, u32[]{:S(2)}, u32[]{:S(2)}) collective-permute-start(bf16[512,768]{1,0:T(8,128)(2,1)} %bitcast.3.refs_0_), channel_id=1, source_target_pairs={{0,1},{1,0},{2,3},{3,2},{4,5},{5,4},{6,7},{7,6},{8,9},{9,8},{10,11... | collective-permute-start | bytes 2359304 | tf_op jit(solution)/shard_map/ppermute | solution.py:234
  97.5 1.9 collective-permute-start.3
  99.4 27.1 %collective-permute-done.1.refs_2_ = bf16[512,768]{1,0:T(8,128)(2,1)} collective-permute-done((bf16[512,768]{1,0:T(8,128)(2,1)}, bf16[512,768]{1,0:T(8,128)(2,1)}, u32[]{:S(2)}, u32[]{:S(2)}) %collective-permute-start.1) | collective-permute-done | bytes 786464 | tf_op jit(solution)/shard_map/ppermute | solution.py:233
  126.5 5.0 %collective-permute-start.2 = (bf16[512,768]{1,0:T(8,128)(2,1)}, bf16[512,768]{1,0:T(8,128)(2,1)}, u32[]{:S(2)}, u32[]{:S(2)}) collective-permute-start(bf16[512,768]{1,0:T(8,128)(2,1)} %collective-permute-done.1.refs_2_), channel_id=1, source_target_pairs={{0,1},{1,0},{2,3},{3,2},{4,5},{5,4},{6,7},{7,6},{8,9},{9,8},{10,11... | collective-permute-start | bytes 2359304 | tf_op jit(solution)/shard_map/ppermute | solution.py:235
  131.5 11.8 %collective-permute-done.4.refs_6_.refs_2_ = bf16[768,512]{1,0:T(8,128)(2,1)S(1)} collective-permute-done((bf16[768,512]{1,0:T(8,128)(2,1)S(1)}, bf16[768,512]{1,0:T(8,128)(2,1)S(1)}, u32[]{:S(2)}, u32[]{:S(2)}) %collective-permute-start.4) | collective-permute-done | bytes 786464 | tf_op jit(solution)/shard_map/ppermute | solution.py:233
  143.3 3.6 collective-permute-start.5
  146.9 3.3 copy.21
  150.2 4.5 %all-to-all-start.2 = ((bf16[4,16,16,1024]{3,2,1,0:T(8,128)(2,1)}), bf16[4,16,16,1024]{3,2,1,0:T(8,128)(2,1)}, u32[]{:S(2)}, u32[]{:S(2)}) async-start(bf16[4,16,16,1024]{3,2,1,0:T(8,128)(2,1)} %bitcast.19), calls=%async_computation.3 | async-start | bytes 4194304 | tf_op jit(solution)/shard_map/all_to_all | solution.py:247
  155.7 4.8 %forward.1.acts_ref.a0 = bf16[256,1536]{1,0:T(8,128)(2,1)S(1)} custom-call(s32[1]{0:T(128)} %bitcast.2.me_ref, bf16[16,4,16,1024]{3,2,1,0:T(8,128)(2,1)} %all-to-all-done.rows_ref, bf16[512,768]{1,0:T(8,128)(2,1)} %bitcast.3.refs_0_, bf16[512,768]{1,0:T(8,128)(2,1)} %collective-permute-done.refs_1_, bf16[512,768]{1,0:T(8,128)(2,1)} %collective-permute-done.1.refs_2_, ...), custom_call_target="tpu_custom_call" | custom-call | flops 1600000000 | bytes 9000000 | tf_op jit(solution)/shard_map/forward/pallas_call | solution.py:251
  160.5 3.3 collective-permute-start.7
  163.8 2.4 collective-permute-start.6
  166.3 30.1 %collective-permute-done.7.a2 = bf16[256,1536]{1,0:T(8,128)(2,1)S(1)} collective-permute-done((bf16[256,1536]{1,0:T(8,128)(2,1)S(1)}, bf16[256,1536]{1,0:T(8,128)(2,1)S(1)}, u32[]{:S(2)}, u32[]{:S(2)}) %collective-permute-start.7) | collective-permute-done | bytes 786464 | tf_op jit(solution)/shard_map/ppermute | solution.py:259
  196.4 2.7 collective-permute-start.8
  199.1 2.0 collective-permute-done.8.a3
  201.1 1.1 copy-done.14
  203.4 4.9 %moments.1 = bf16[128,48,128]{2,1,0:T(8,128)(2,1)} custom-call(s32[1]{0:T(128)} %bitcast.2.me_ref, bf16[4,16,16,1024]{3,2,1,0:T(8,128)(2,1)} %all-to-all-done.2.rows_ref, bf16[256,1536]{1,0:T(8,128)(2,1)S(1)} %forward.1.acts_ref.a0, bf16[256,1536]{1,0:T(8,128)(2,1)S(1)} %collective-permute-done.6.a1, bf16[256,1536]{1,0:T(8,128)(2,1)S(1)} %collective-permute-done.7.a2, ...), custom_call_target="tpu_custom_call" | custom-call | flops 3200000000 | bytes 9000000 | tf_op jit(solution)/shard_map/moments/pallas_call | solution.py:272
  209.2 14.8 %all-to-all-start.3 = ((bf16[128,48,128]{2,1,0:T(8,128)(2,1)}), bf16[128,48,128]{2,1,0:T(8,128)(2,1)S(1)}, u32[]{:S(2)}, u32[]{:S(2)}) async-start(bf16[128,48,128]{2,1,0:T(8,128)(2,1)} %moments.1), calls=%async_computation.4 | async-start | bytes 3145728 | tf_op jit(solution)/shard_map/all_to_all | solution.py:287
  227.4 1.9 expert_out.1
  229.3 73.9 %all-to-all-done.3.spread_ref = bf16[128,48,128]{2,1,0:T(8,128)(2,1)S(1)} async-done(((bf16[128,48,128]{2,1,0:T(8,128)(2,1)}), bf16[128,48,128]{2,1,0:T(8,128)(2,1)S(1)}, u32[]{:S(2)}, u32[]{:S(2)}) %all-to-all-start.3) | async-done | bytes 1572896 | tf_op jit(solution)/shard_map/all_to_all | solution.py:287
  303.3 3.7 all-to-all-start.1
  306.9 1.9 pick.1
  308.9 13.7 %all-to-all-done.1.returned_ref = bf16[16,4,16,512]{3,2,1,0:T(8,128)(2,1)S(1)} async-done(((bf16[16,4,16,512]{3,2,1,0:T(8,128)(2,1)}), bf16[16,4,16,512]{3,2,1,0:T(8,128)(2,1)S(1)}, u32[]{:S(2)}, u32[]{:S(2)}) %all-to-all-start.1) | async-done | bytes 1048608 | tf_op jit(solution)/shard_map/all_to_all | solution.py:281
  322.5 8.4 %all-to-all-start.4 = ((bf16[128,48,128]{2,1,0:T(8,128)(2,1)}), bf16[128,48,128]{2,1,0:T(8,128)(2,1)S(1)}, u32[]{:S(2)}, u32[]{:S(2)}) async-start(bf16[128,48,128]{2,1,0:T(8,128)(2,1)} %pick.1), calls=%async_computation.5 | async-start | bytes 3145728 | tf_op jit(solution)/shard_map/all_to_all | solution.py:291
  331.0 1.7 combine.1
  332.7 88.8 %all-to-all-done.4.pieces_ref = bf16[128,48,128]{2,1,0:T(8,128)(2,1)S(1)} async-done(((bf16[128,48,128]{2,1,0:T(8,128)(2,1)}), bf16[128,48,128]{2,1,0:T(8,128)(2,1)S(1)}, u32[]{:S(2)}, u32[]{:S(2)}) %all-to-all-start.4) | async-done | bytes 1572896 | tf_op jit(solution)/shard_map/all_to_all | solution.py:291
  421.5 1.4 unpack.1
  (49 shorter events, 12.2 us)
Async XLA Ops:
  7.2 67.2 %all-gather.2.cloned.1.call-start = ((), (), s32[]{:S(2)}) async-start(), calls=%async_computation.6 | async-start | bytes 1824768 | tf_op jit(solution)/shard_map/all_gather | solution.py:230
  8.7 0.9 copy-start.9
  9.6 0.9 copy-start.10
  74.4 1.4 copy-start.13
  79.9 9.2 %copy-start = (bf16[1,768,512]{2,1,0:T(8,128)(2,1)S(1)}, bf16[1,768,512]{2,1,0:T(8,128)(2,1)}, u32[]{:S(2)}) copy-start(bf16[1,768,512]{2,1,0:T(8,128)(2,1)} %param.17) | copy-start | bytes 2359300
  79.9 67.0 %all-to-all-start = ((bf16[16,4,16,1024]{3,2,1,0:T(8,128)(2,1)}), bf16[16,4,16,1024]{3,2,1,0:T(8,128)(2,1)}, u32[]{:S(2)}, u32[]{:S(2)}) async-start(bf16[16,4,16,1024]{3,2,1,0:T(8,128)(2,1)} %get-tuple-element.8), calls=%async_computation | async-start | bytes 4194304 | tf_op jit(solution)/shard_map/all_to_all | solution.py:246
  87.1 39.5 %collective-permute-start.1 = (bf16[512,768]{1,0:T(8,128)(2,1)}, bf16[512,768]{1,0:T(8,128)(2,1)}, u32[]{:S(2)}, u32[]{:S(2)}) collective-permute-start(bf16[512,768]{1,0:T(8,128)(2,1)} %bitcast.3.refs_0_), channel_id=1, source_target_pairs={{0,2},{2,0},{1,3},{3,1},{4,6},{6,4},{5,7},{7,5},{8,10},{10,8},{9,1... | collective-permute-start | bytes 2359304 | tf_op jit(solution)/shard_map/ppermute | solution.py:233
  89.1 54.2 %collective-permute-start.4 = (bf16[768,512]{1,0:T(8,128)(2,1)S(1)}, bf16[768,512]{1,0:T(8,128)(2,1)S(1)}, u32[]{:S(2)}, u32[]{:S(2)}) collective-permute-start(bf16[768,512]{1,0:T(8,128)(2,1)S(1)} %bitcast.12), channel_id=1, source_target_pairs={{0,2},{2,0},{1,3},{3,1},{4,6},{6,4},{5,7},{7,5},{8,10},{10,8},{9,1... | collective-permute-start | bytes 2359304 | tf_op jit(solution)/shard_map/ppermute | solution.py:233
  92.4 62.3 %collective-permute-start = (bf16[512,768]{1,0:T(8,128)(2,1)}, bf16[512,768]{1,0:T(8,128)(2,1)}, u32[]{:S(2)}, u32[]{:S(2)}) collective-permute-start(bf16[512,768]{1,0:T(8,128)(2,1)} %bitcast.3.refs_0_), channel_id=1, source_target_pairs={{0,1},{1,0},{2,3},{3,2},{4,5},{5,4},{6,7},{7,6},{8,9},{9,8},{10,11... | collective-permute-start | bytes 2359304 | tf_op jit(solution)/shard_map/ppermute | solution.py:234
  97.5 57.2 %collective-permute-start.3 = (bf16[768,512]{1,0:T(8,128)(2,1)S(1)}, bf16[768,512]{1,0:T(8,128)(2,1)S(1)}, u32[]{:S(2)}, u32[]{:S(2)}) collective-permute-start(bf16[768,512]{1,0:T(8,128)(2,1)S(1)} %bitcast.13), channel_id=1, source_target_pairs={{0,1},{1,0},{2,3},{3,2},{4,5},{5,4},{6,7},{7,6},{8,9},{9,8},{10,11... | collective-permute-start | bytes 2359304 | tf_op jit(solution)/shard_map/ppermute | solution.py:234
  126.5 28.2 %collective-permute-start.2 = (bf16[512,768]{1,0:T(8,128)(2,1)}, bf16[512,768]{1,0:T(8,128)(2,1)}, u32[]{:S(2)}, u32[]{:S(2)}) collective-permute-start(bf16[512,768]{1,0:T(8,128)(2,1)} %collective-permute-done.1.refs_2_), channel_id=1, source_target_pairs={{0,1},{1,0},{2,3},{3,2},{4,5},{5,4},{6,7},{7,6},{8,9},{9,8},{10,11... | collective-permute-start | bytes 2359304 | tf_op jit(solution)/shard_map/ppermute | solution.py:235
  143.3 6.9 %copy-start.1 = (bf16[768,512]{1,0:T(8,128)(2,1)}, bf16[768,512]{1,0:T(8,128)(2,1)S(1)}, u32[]{:S(2)}) copy-start(bf16[768,512]{1,0:T(8,128)(2,1)S(1)} %collective-permute-done.4.refs_6_.refs_2_) | copy-start | bytes 2359300
  143.3 11.5 %collective-permute-start.5 = (bf16[768,512]{1,0:T(8,128)(2,1)S(1)}, bf16[768,512]{1,0:T(8,128)(2,1)S(1)}, u32[]{:S(2)}, u32[]{:S(2)}) collective-permute-start(bf16[768,512]{1,0:T(8,128)(2,1)S(1)} %collective-permute-done.4.refs_6_.refs_2_), channel_id=1, source_target_pairs={{0,1},{1,0},{2,3},{3,2},{4,5},{5,4},{6,7},{7,6},{8,9},{9,8},{10,11... | collective-permute-start | bytes 2359304 | tf_op jit(solution)/shard_map/ppermute | solution.py:235
  150.2 48.9 %all-to-all-start.2 = ((bf16[4,16,16,1024]{3,2,1,0:T(8,128)(2,1)}), bf16[4,16,16,1024]{3,2,1,0:T(8,128)(2,1)}, u32[]{:S(2)}, u32[]{:S(2)}) async-start(bf16[4,16,16,1024]{3,2,1,0:T(8,128)(2,1)} %bitcast.19), calls=%async_computation.3 | async-start | bytes 4194304 | tf_op jit(solution)/shard_map/all_to_all | solution.py:247
  154.7 5.8 %copy-start.3 = (bf16[768,512]{1,0:T(8,128)(2,1)}, bf16[768,512]{1,0:T(8,128)(2,1)S(1)}, u32[]{:S(2)}) copy-start(bf16[768,512]{1,0:T(8,128)(2,1)S(1)} %collective-permute-done.3.refs_5_.refs_1_) | copy-start | bytes 2359300
  154.8 1.0 copy-start.5
  160.5 35.8 %collective-permute-start.7 = (bf16[256,1536]{1,0:T(8,128)(2,1)S(1)}, bf16[256,1536]{1,0:T(8,128)(2,1)S(1)}, u32[]{:S(2)}, u32[]{:S(2)}) collective-permute-start(bf16[256,1536]{1,0:T(8,128)(2,1)S(1)} %forward.1.acts_ref.a0), channel_id=1, source_target_pairs={{0,2},{2,0},{1,3},{3,1},{4,6},{6,4},{5,7},{7,5},{8,10},{10,8},{9,1... | collective-permute-start | bytes 2359304 | tf_op jit(solution)/shard_map/ppermute | solution.py:259
  163.8 35.3 %collective-permute-start.6 = (bf16[256,1536]{1,0:T(8,128)(2,1)S(1)}, bf16[256,1536]{1,0:T(8,128)(2,1)S(1)}, u32[]{:S(2)}, u32[]{:S(2)}) collective-permute-start(bf16[256,1536]{1,0:T(8,128)(2,1)S(1)} %forward.1.acts_ref.a0), channel_id=1, source_target_pairs={{0,1},{1,0},{2,3},{3,2},{4,5},{5,4},{6,7},{7,6},{8,9},{9,8},{10,11... | collective-permute-start | bytes 2359304 | tf_op jit(solution)/shard_map/ppermute | solution.py:260
  196.4 4.8 %collective-permute-start.8 = (bf16[256,1536]{1,0:T(8,128)(2,1)S(1)}, bf16[256,1536]{1,0:T(8,128)(2,1)}, u32[]{:S(2)}, u32[]{:S(2)}) collective-permute-start(bf16[256,1536]{1,0:T(8,128)(2,1)S(1)} %collective-permute-done.7.a2), channel_id=1, source_target_pairs={{0,1},{1,0},{2,3},{3,2},{4,5},{5,4},{6,7},{7,6},{8,9},{9,8},{10,11... | collective-permute-start | bytes 2359304 | tf_op jit(solution)/shard_map/ppermute | solution.py:261
  201.1 1.1 copy-start.14
  202.3 1.1 copy-start.15
  208.3 0.9 copy-start.7
  209.2 14.8 %copy-start.2 = (bf16[768,512]{1,0:T(8,128)(2,1)S(1)}, bf16[768,512]{1,0:T(8,128)(2,1)}, u32[]{:S(2)}) copy-start(bf16[768,512]{1,0:T(8,128)(2,1)} %copy-done.1) | copy-start | bytes 2359300
  209.2 94.1 %all-to-all-start.3 = ((bf16[128,48,128]{2,1,0:T(8,128)(2,1)}), bf16[128,48,128]{2,1,0:T(8,128)(2,1)S(1)}, u32[]{:S(2)}, u32[]{:S(2)}) async-start(bf16[128,48,128]{2,1,0:T(8,128)(2,1)} %moments.1), calls=%async_computation.4 | async-start | bytes 3145728 | tf_op jit(solution)/shard_map/all_to_all | solution.py:287
  224.0 1.1 copy-start.4
  225.1 1.1 copy-start.6
  226.2 1.1 copy-start.8
  229.3 77.6 %copy-start.12 = (s32[128]{0:T(128)S(1)}, s32[128]{0:T(128)}, u32[]{:S(2)}) copy-start(s32[128]{0:T(128)} %partner_ref.1) | copy-start | bytes 1540
  303.3 19.3 %all-to-all-start.1 = ((bf16[16,4,16,512]{3,2,1,0:T(8,128)(2,1)}), bf16[16,4,16,512]{3,2,1,0:T(8,128)(2,1)S(1)}, u32[]{:S(2)}, u32[]{:S(2)}) async-start(bf16[16,4,16,512]{3,2,1,0:T(8,128)(2,1)} %expert_out.1), calls=%async_computation.1 | async-start | bytes 2097152 | tf_op jit(solution)/shard_map/all_to_all | solution.py:281
  308.9 22.1 %copy-start.17 = (f32[192,256]{1,0:T(8,128)S(1)}, f32[192,256]{1,0:T(8,128)}, u32[]{:S(2)}) copy-start(f32[192,256]{1,0:T(8,128)} %copy-done.16) | copy-start | bytes 589828
  322.5 98.9 %all-to-all-start.4 = ((bf16[128,48,128]{2,1,0:T(8,128)(2,1)}), bf16[128,48,128]{2,1,0:T(8,128)(2,1)S(1)}, u32[]{:S(2)}, u32[]{:S(2)}) async-start(bf16[128,48,128]{2,1,0:T(8,128)(2,1)} %pick.1), calls=%async_computation.5 | async-start | bytes 3145728 | tf_op jit(solution)/shard_map/all_to_all | solution.py:291
  330.9 92.0 %reduce-scatter.2.cloned.1.call-start = ((), (), s32[]{:S(2)}) async-start(), calls=%async_computation.7 | async-start | bytes 884736 | tf_op jit(solution)/shard_map/reduce_scatter | solution.py:285
  (2 other events, 1.3 us)
Sparse Core Ops, SparseCore 0:
  12.4 61.9 all-gather.1
  335.2 75.3 reduce-scatter.1

commit v2 on v1

--- a/solution.py
+++ b/solution.py
@@ -15,9 +15,10 @@
 FLIP = [(0, 1), (1, 0)]
 VMEM = pl.BlockSpec(memory_space=pltpu.VMEM)
 SMEM = pl.BlockSpec(memory_space=pltpu.SMEM)
-
-
-def call(kernel, name, out_shape, in_specs, flops, moved):
+HBM = pl.BlockSpec(memory_space=pltpu.HBM)
+
+
+def call(kernel, name, out_shape, in_specs, flops, moved, scratch=()):
     outs = jax.tree.map(lambda _: VMEM, out_shape)
     return pl.pallas_call(
         kernel,
@@ -25,7 +26,8 @@
         out_shape=out_shape,
         in_specs=in_specs,
         out_specs=outs,
-        compiler_params=pltpu.CompilerParams(vmem_limit_bytes=48 * 1024 * 1024),
+        scratch_shapes=scratch,
+        compiler_params=pltpu.CompilerParams(vmem_limit_bytes=62 * 1024 * 1024),
         cost_estimate=pl.CostEstimate(flops=flops, bytes_accessed=moved, transcendentals=0),
     )
 
@@ -38,31 +40,43 @@
     return high, middle, low
 
 
+def fetch(pairs, sems):
+    copies = [
+        pltpu.make_async_copy(source, target, sems.at[i]) for i, (source, target) in enumerate(pairs)
+    ]
+    for copy in copies:
+        copy.start()
+    return copies
+
+
 def pack_kernel(tok_ref, cot_ref, ids_ref, weight_ref, holder_ref, out_ref):
-    rows, top = ids_ref.shape
+    top, rows = ids_ref.shape
     width = tok_ref.shape[1]
     experts = holder_ref.shape[1]
-    ids = ids_ref[...]
-    weights = weight_ref[...]
-    lane = lax.broadcasted_iota(jnp.int32, (rows, experts), 1)
+    row_at = lax.broadcasted_iota(jnp.int32, (rows, rows), 0)
+    column_at = lax.broadcasted_iota(jnp.int32, (rows, rows), 1)
+    same = (row_at == column_at).astype(BF16)
+
+    def turned(value):
+        return lax.dot_general(
+            same, value.astype(BF16), (((1,), (1,)), ((), ())), preferred_element_type=F32
+        )
+
+    ids = turned(ids_ref[...].astype(F32))
+    parts = [turned(part) for part in split3(weight_ref[...])]
+    lane = lax.broadcasted_iota(jnp.int32, (rows, experts), 1).astype(F32)
     hits = [(ids[:, k : k + 1] == lane).astype(F32) for k in range(top)]
     hit = sum(hits[1:], hits[0])
-    earlier = (
-        lax.broadcasted_iota(jnp.int32, (rows, rows), 0)
-        > lax.broadcasted_iota(jnp.int32, (rows, rows), 1)
-    ).astype(F32)
-    before = jnp.dot(earlier, hit, preferred_element_type=F32)
+    earlier = (row_at > column_at).astype(BF16)
+    before = jnp.dot(earlier, hit.astype(BF16), preferred_element_type=F32)
     base = 2.0 * holder_ref[...].astype(F32) + before
-    high, middle, low = split3(weights)
     meta_lane = lax.broadcasted_iota(jnp.int32, (rows, 128), 1)
     meta = jnp.zeros((rows, 128), F32)
     for k in range(top):
         code = jnp.sum(hits[k] * base, axis=1, keepdims=True)
         meta = jnp.where(meta_lane == k, code, meta)
-        for place, part in enumerate((high, middle, low)):
-            meta = jnp.where(
-                meta_lane == (place + 1) * top + k, part.astype(F32)[:, k : k + 1], meta
-            )
+        for place, part in enumerate(parts):
+            meta = jnp.where(meta_lane == (place + 1) * top + k, part[:, k : k + 1], meta)
     out_ref[:, :width] = tok_ref[...]
     out_ref[:, width : 2 * width] = cot_ref[...]
     out_ref[:, 2 * width :] = meta.astype(BF16)
@@ -111,22 +125,25 @@
 
 
 def forward_kernel(me_ref, rows_ref, *refs):
-    ups, downs, out_ref = refs[:4], refs[4:8], refs[8]
+    sources, out_ref, ups, downs, sems = refs[:8], refs[8], refs[9], refs[10], refs[11]
+    copies = fetch(
+        [(sources[j + 4 * kind], held.at[j]) for j in range(4) for kind, held in ((0, ups), (1, downs))],
+        sems,
+    )
     targets, _, per_target, double = rows_ref.shape
     quarter = double // 2
     count = targets * per_target
-    hidden_count = ups[0].shape[1]
+    hidden_count = ups.shape[2]
     me = me_ref[0]
     preact = jnp.zeros((count, hidden_count), F32)
     back = jnp.zeros((count, hidden_count), F32)
     for j in range(4):
         both = rows_ref[:, me ^ j].reshape(count, double)
-        preact = preact + jnp.dot(both[:, :quarter], ups[j][...], preferred_element_type=F32)
+        copies[2 * j].wait()
+        preact = preact + jnp.dot(both[:, :quarter], ups[j], preferred_element_type=F32)
+        copies[2 * j + 1].wait()
         back = back + lax.dot_general(
-            both[:, quarter:],
-            downs[j][...],
-            (((1,), (1,)), ((), ())),
-            preferred_element_type=F32,
+            both[:, quarter:], downs[j], (((1,), (1,)), ((), ())), preferred_element_type=F32
         )
     sigmoid = 1.0 / (1.0 + jnp.exp(-preact))
     out_ref[:, :hidden_count] = (preact * sigmoid).astype(BF16)
@@ -134,12 +151,14 @@
 
 
 def expert_out_kernel(me_ref, acts_ref, *refs):
-    downs, out_ref = refs[:4], refs[4]
+    sources, out_ref, downs, sems = refs[:4], refs[4], refs[5], refs[6]
+    copies = fetch([(sources[j], downs.at[j]) for j in range(4)], sems)
     targets, _, per_target, quarter = out_ref.shape
-    hidden = acts_ref[:, : downs[0].shape[0]]
+    hidden = acts_ref[:, : downs.shape[1]]
     me = me_ref[0]
     for j in range(4):
-        part = jnp.dot(hidden, downs[j][...], preferred_element_type=F32).astype(BF16)
+        copies[j].wait()
+        part = jnp.dot(hidden, downs[j], preferred_element_type=F32).astype(BF16)
         out_ref[:, me ^ j] = part.reshape(targets, per_target, quarter)
 
 
@@ -152,7 +171,10 @@
         out_ref[:, q * quarter : (q + 1) * quarter] = mixed.astype(BF16)
 
 
-def moment_kernel(me_ref, rows_ref, a0, a1, a2, a3, up_ref, down_ref, out_ref):
+def moment_kernel(
+    me_ref, rows_ref, a0, a1, a2, a3, up_hbm, down_hbm, out_ref, up_ref, down_ref, sems
+):
+    copies = fetch([(up_hbm, up_ref), (down_hbm, down_ref)], sems)
     acts = (a0, a1, a2, a3)
     me = me_ref[0]
     features, hidden_count = up_ref.shape
@@ -174,6 +196,8 @@
             preferred_element_type=F32,
         )
     rest = 1.0 - MOMENT_DECAY
+    for copy in copies:
+        copy.wait()
     up = (MOMENT_DECAY * up_ref[...].astype(F32) + rest * up_grad).astype(BF16)
     down = (MOMENT_DECAY * down_ref[...].astype(F32) + rest * down_grad).astype(BF16)
     up = up.reshape(32, 16, hidden_count)
@@ -225,7 +249,7 @@
     me = lax.axis_index(DP_AXES).reshape(1).astype(jnp.int32)
 
     packed = call(pack_kernel, "pack", shape_of((24, 4224)), [VMEM] * 5, 10**6, 4 * 10**5)(
-        tokens, cotangent, expert_ids, route_weight, holder.reshape(1, -1)
+        tokens, cotangent, expert_ids.T, route_weight.T, holder.reshape(1, -1)
     )
     gathered = lax.all_gather(packed, "zh", axis=0, tiled=True)
 
@@ -233,6 +257,9 @@
     up2, down2 = lax.ppermute(up0, "yl", FLIP), lax.ppermute(down0, "yl", FLIP)
     up1, down1 = lax.ppermute(up0, "core", FLIP), lax.ppermute(down0, "core", FLIP)
     up3, down3 = lax.ppermute(up2, "core", FLIP), lax.ppermute(down2, "core", FLIP)
+    gathered, up1, up2, up3, down1, down2, down3 = lax.optimization_barrier(
+        (gathered, up1, up2, up3, down1, down2, down3)
+    )
     ups, downs = (up0, up1, up2, up3), (down0, down1, down2, down3)
 
     outgoing, share = call(
@@ -252,36 +279,49 @@
         forward_kernel,
         "forward",
         shape_of((256, 1536)),
-        [SMEM] + [VMEM] * 9,
+        [SMEM, VMEM] + [HBM] * 8,
         16 * 10**8,
         9 * 10**6,
+        (
+            pltpu.VMEM((4, 512, 768), BF16),
+            pltpu.VMEM((4, 768, 512), BF16),
+            pltpu.SemaphoreType.DMA((8,)),
+        ),
     )(me, rows, *ups, *downs)
     acts2 = lax.ppermute(acts, "yl", FLIP)
     acts1 = lax.ppermute(acts, "core", FLIP)
-    acts3 = lax.ppermute(acts2, "core", FLIP)
 
     expert_out = call(
         expert_out_kernel,
         "expert_out",
         shape_of((16, 4, 16, 512)),
-        [SMEM] + [VMEM] * 5,
+        [SMEM, VMEM] + [HBM] * 4,
         8 * 10**8,
         5 * 10**6,
+        (pltpu.VMEM((4, 768, 512), BF16), pltpu.SemaphoreType.DMA((4,))),
     )(me, acts, *downs)
 
+    by_feature, acts2, expert_out = lax.optimization_barrier((by_feature, acts2, expert_out))
+    acts3 = lax.ppermute(acts2, "core", FLIP)
+    returned = lax.all_to_all(expert_out, GROUP_AXES, split_axis=0, concat_axis=0, tiled=True)
+    partial = call(
+        combine_kernel, "combine", shape_of((192, 2048)), [VMEM, VMEM], 6 * 10**8, 2 * 10**6
+    )(share, returned)
     pieces = call(
         moment_kernel,
         "moments",
         shape_of((128, 48, 128)),
-        [SMEM] + [VMEM] * 7,
+        [SMEM] + [VMEM] * 5 + [HBM] * 2,
         32 * 10**8,
         9 * 10**6,
+        (
+            pltpu.VMEM((512, 768), BF16),
+            pltpu.VMEM((768, 512), BF16),
+            pltpu.SemaphoreType.DMA((2,)),
+        ),
     )(me, by_feature, acts, acts1, acts2, acts3, up_moment[0], down_moment[0])
 
-    returned = lax.all_to_all(expert_out, GROUP_AXES, split_axis=0, concat_axis=0, tiled=True)
-    partial = call(
-        combine_kernel, "combine", shape_of((192, 2048)), [VMEM, VMEM], 6 * 10**8, 2 * 10**6
-    )(share, returned)
+    partial, pieces = lax.optimization_barrier((partial, pieces))
     layer_out = lax.psum_scatter(partial, "zh", scatter_dimension=0, tiled=True)
 
     spread = lax.all_to_all(pieces, SLOT_AXES, split_axis=0, concat_axis=0, tiled=True)

time: 434 us -> 393 us (0.906)
  waiting for transfers between devices: 310 us -> 145 us
  blocking collectives: 0 us -> 122 us
  Pallas kernels: 21.2 us -> 33.3 us
  local copies, waits for them, and re-layouts: 16.9 us -> 4.97 us
    all_to_all x0 -> x2, blocking collectives: none -> 122 us  [the longest x1 88.7 us: body(): lax.all_to_all(pieces, SLOT_AXES, split_axis=0, concat_axis=0, tiled=True)]
    all_to_all x2 -> x0, waiting for transfers between devices: 74 us -> none  [the longest x1 73.9 us: body(): lax.all_to_all(pieces, SLOT_AXES, split_axis=0, concat_axis=0, tiled=True)]
    all_gather x1, waiting for transfers between devices: 62.1 us -> 18.4 us  [body(): gathered = lax.all_gather(packed, 'zh', axis=0, tiled=True)]
    ppermute x1, waiting for transfers between devices: 27.1 us -> 0.09 us  [body(): lax.ppermute(up0, 'yl', FLIP)]
    all_to_all x2 -> x0, starting transfers between devices: 21.9 us -> none  [the longest x1 14.8 us: body(): lax.all_to_all(pieces, SLOT_AXES, split_axis=0, concat_axis=0, tiled=True)]
    unnamed x38 -> x20, local copies, waits for them, and re-layouts: 13.6 us -> 3.33 us
    all_to_all x1, waiting for transfers between devices: 13.7 us -> 3.63 us  [body(): lax.all_to_all(expert_out, GROUP_AXES, split_axis=0, concat_axis=0, tiled...]
    ppermute x1, starting transfers between devices: 4.96 us -> 14.8 us  [body(): lax.ppermute(up2, 'core', FLIP)]
  transfers between devices with their start and end apart: 16 -> 14, of which waited for: 8 -> 8; matrix products, arithmetic and copies ran while one was open for 1% -> 0% of each run, Pallas kernels for 3% -> 5%
where the time goes in v2:
time: 393 us; the launch traced here: 388 us
  waiting for transfers between devices  145 us (37%)
  blocking collectives  122 us (31%)
  starting transfers between devices  68.1 us (17%)
  Pallas kernels  33.3 us (8%)
  between operations  14.2 us (4%)
  local copies, waits for them, and re-layouts  4.97 us (1%)
    all_to_all x1, waiting for transfers between devices, body(): lax.all_to_all(chosen, SLOT_AXES, split_axis=0, concat_axis=0, tiled=True)  89.8 us
    all_to_all x1, blocking collectives, body(): lax.all_to_all(pieces, SLOT_AXES, split_axis=0, concat_axis=0, tiled=True)  88.7 us
    all_to_all x1, blocking collectives, body(): lax.all_to_all(outgoing, GROUP_AXES, split_axis=0, concat_axis=0, tiled=T...  33.7 us
    ppermute x1, waiting for transfers between devices, body(): acts2 = lax.ppermute(acts, 'yl', FLIP)  26.5 us
    all_gather x1, waiting for transfers between devices, body(): gathered = lax.all_gather(packed, 'zh', axis=0, tiled=True)  18.4 us
    ppermute x1, starting transfers between devices, body(): lax.ppermute(up2, 'core', FLIP)  14.8 us
    ppermute x1, starting transfers between devices, body(): lax.ppermute(up0, 'core', FLIP)  8.68 us
    all_to_all x1, starting transfers between devices, body(): lax.all_to_all(rows.transpose(1, 0, 2, 3), DP_AXES, split_axis=0, concat_...  8.22 us
  transfers between devices with their start and end apart: 14, of which 8 were waited for; matrix products, arithmetic and copies ran while one was open for 0% of the time, Pallas kernels for 5%

profile of v2, /device:TPU:1, one launch (start us, length us, event | category | flops | bytes accessed | tf_op | source)
XLA Modules:
  0.0 388.4 jit_solution(13662699375536493031)
XLA Ops:
  7.2 2.1 pack.1
  9.3 4.0 %collective-permute-start.1 = (bf16[512,768]{1,0:T(8,128)(2,1)}, bf16[512,768]{1,0:T(8,128)(2,1)}, u32[]{:S(2)}, u32[]{:S(2)}) collective-permute-start(bf16[512,768]{1,0:T(8,128)(2,1)} %bitcast.18), channel_id=1, source_target_pairs={{0,2},{2,0},{1,3},{3,1},{4,6},{6,4},{5,7},{7,5},{8,10},{10,8},{9,1... | collective-permute-start | bytes 2359304 | tf_op jit(solution)/shard_map/ppermute | solution.py:257
  13.4 1.9 collective-permute-start.4
  15.3 8.7 %collective-permute-start = (bf16[512,768]{1,0:T(8,128)(2,1)}, bf16[512,768]{1,0:T(8,128)(2,1)}, u32[]{:S(2)}, u32[]{:S(2)}) collective-permute-start(bf16[512,768]{1,0:T(8,128)(2,1)} %bitcast.19), channel_id=1, source_target_pairs={{0,1},{1,0},{2,3},{3,2},{4,5},{5,4},{6,7},{7,6},{8,9},{9,8},{10,11... | collective-permute-start | bytes 2359304 | tf_op jit(solution)/shard_map/ppermute | solution.py:258
  24.0 1.9 collective-permute-start.3
  26.0 14.8 %collective-permute-start.2 = (bf16[512,768]{1,0:T(8,128)(2,1)}, bf16[512,768]{1,0:T(8,128)(2,1)}, u32[]{:S(2)}, u32[]{:S(2)}) collective-permute-start(bf16[512,768]{1,0:T(8,128)(2,1)} %collective-permute-done.1.refs_2_), channel_id=1, source_target_pairs={{0,1},{1,0},{2,3},{3,2},{4,5},{5,4},{6,7},{7,6},{8,9},{9,8},{10,11... | collective-permute-start | bytes 2359304 | tf_op jit(solution)/shard_map/ppermute | solution.py:259
  40.8 2.1 collective-permute-done.4.refs_6_.refs_2_
  42.9 7.9 %collective-permute-start.5 = (bf16[768,512]{1,0:T(8,128)(2,1)S(1)}, bf16[768,512]{1,0:T(8,128)(2,1)S(1)}, u32[]{:S(2)}, u32[]{:S(2)}) collective-permute-start(bf16[768,512]{1,0:T(8,128)(2,1)S(1)} %collective-permute-done.4.refs_6_.refs_2_), channel_id=1, source_target_pairs={{0,1},{1,0},{2,3},{3,2},{4,5},{5,4},{6,7},{7,6},{8,9},{9,8},{10,11... | collective-permute-start | bytes 2359304 | tf_op jit(solution)/shard_map/ppermute | solution.py:259
  50.9 1.8 collective-permute-done.5.refs_7_.refs_3_
  52.7 0.9 copy-done.4
  53.6 18.4 %all-gather.2.cloned.1.call-done.gathered_ref = bf16[192,4224]{1,0:T(8,128)(2,1)} async-done(((bf16[24,4224]{1,0:T(8,128)(2,1)}), bf16[192,4224]{1,0:T(8,128)(2,1)}) %all-gather.2.cloned.1.call-update) | async-done | bytes 1622032 | tf_op jit(solution)/shard_map/all_gather | solution.py:254
  72.0 4.8 %select.1 = (bf16[16,4,16,1024]{3,2,1,0:T(8,128)(2,1)}, f32[192,256]{1,0:T(8,128)}) custom-call(s32[1]{0:T(128)} %bitcast.plane_ref, bf16[192,4224]{1,0:T(8,128)(2,1)} %all-gather.2.cloned.1.call-done.gathered_ref), custom_call_target="tpu_custom_call" | custom-call | flops 1000000000 | bytes 4000000 | tf_op jit(solution)/shard_map/select/pallas_call | solution.py:265
  76.9 33.7 %all_to_all.25.rows_ref = bf16[16,4,16,1024]{3,2,1,0:T(8,128)(2,1)S(1)} all-to-all(bf16[16,4,16,1024]{3,2,1,0:T(8,128)(2,1)} %get-tuple-element.21), channel_id=1, replica_groups=mesh['yh'=2,'zh'=8,'zp'=2,'x'=4,'yl'=2,'core'=2] {'yh','zp','x'}, dimensions={0} | all-to-all | bytes 4194304 | tf_op jit(solution)/shard_map/all_to_all | solution.py:273
  110.6 1.6 copy.17
  112.5 8.2 %all-to-all-start.1 = ((bf16[4,16,16,1024]{3,2,1,0:T(8,128)(2,1)}), bf16[4,16,16,1024]{3,2,1,0:T(8,128)(2,1)}, u32[]{:S(2)}, u32[]{:S(2)}) async-start(bf16[4,16,16,1024]{3,2,1,0:T(8,128)(2,1)} %bitcast.13), calls=%async_computation.1 | async-start | bytes 4194304 | tf_op jit(solution)/shard_map/all_to_all | solution.py:274
  120.8 7.0 %forward.1.acts_ref.a0 = bf16[256,1536]{1,0:T(8,128)(2,1)} custom-call(s32[1]{0:T(128)} %bitcast.7.me_ref, bf16[16,4,16,1024]{3,2,1,0:T(8,128)(2,1)} %copy-done, bf16[512,768]{1,0:T(8,128)(2,1)} %bitcast.20, bf16[512,768]{1,0:T(8,128)(2,1)} %collective-permute-done.refs_1_, bf16[512,768]{1,0:T(8,128)(2,1)} %collective-permute-done.1.refs_2_, ...), custom_call_target="tpu_custom_call" | custom-call | flops 1600000000 | bytes 9000000 | tf_op jit(solution)/shard_map/forward/pallas_call | solution.py:278
  127.8 3.3 collective-permute-start.6
  131.1 4.8 %expert_out.1 = bf16[16,4,16,512]{3,2,1,0:T(8,128)(2,1)} custom-call(s32[1]{0:T(128)} %bitcast.7.me_ref, bf16[256,1536]{1,0:T(8,128)(2,1)} %forward.1.acts_ref.a0, bf16[768,512]{1,0:T(8,128)(2,1)} %bitcast.17, bf16[768,512]{1,0:T(8,128)(2,1)} %copy-done.3, bf16[768,512]{1,0:T(8,128)(2,1)} %copy-done.2, bf16[768,512]{1,0:T(8,128)(2,1)} %copy-done.4), custom_call_target="tpu_custom_call" | custom-call | flops 800000000 | bytes 5000000 | tf_op jit(solution)/shard_map/expert_out/pallas_call | solution.py:294
  135.9 26.5 %collective-permute-done.6.a2 = bf16[256,1536]{1,0:T(8,128)(2,1)S(1)} collective-permute-done((bf16[256,1536]{1,0:T(8,128)(2,1)}, bf16[256,1536]{1,0:T(8,128)(2,1)S(1)}, u32[]{:S(2)}, u32[]{:S(2)}) %collective-permute-start.6) | collective-permute-done | bytes 786464 | tf_op jit(solution)/shard_map/ppermute | solution.py:291
  162.5 4.4 %all-to-all-start.2 = ((bf16[16,4,16,512]{3,2,1,0:T(8,128)(2,1)}), bf16[16,4,16,512]{3,2,1,0:T(8,128)(2,1)}, u32[]{:S(2)}, u32[]{:S(2)}) async-start(bf16[16,4,16,512]{3,2,1,0:T(8,128)(2,1)} %expert_out.1), calls=%async_computation.2 | async-start | bytes 2097152 | tf_op jit(solution)/shard_map/all_to_all | solution.py:306
  166.8 2.8 collective-permute-start.7
  169.6 1.9 collective-permute-start.8
  171.6 2.2 collective-permute-done.8.a3
  174.7 6.0 %moments.1 = bf16[128,48,128]{2,1,0:T(8,128)(2,1)} custom-call(s32[1]{0:T(128)} %bitcast.7.me_ref, bf16[4,16,16,1024]{3,2,1,0:T(8,128)(2,1)} %all-to-all-done.1.rows_ref, bf16[256,1536]{1,0:T(8,128)(2,1)} %forward.1.acts_ref.a0, bf16[256,1536]{1,0:T(8,128)(2,1)} %copy-done.8, bf16[256,1536]{1,0:T(8,128)(2,1)} %copy-done.7, bf16[256,1536]{1,0:T(8,128)(2,1)} %copy-done.9, ...), custom_call_target="tpu_custom_call" | custom-call | flops 3200000000 | bytes 9000000 | tf_op jit(solution)/shard_map/moments/pallas_call | solution.py:310
  180.7 3.6 all-to-all-done.2.returned_ref
  184.3 3.0 combine.1
  187.3 88.7 %all_to_all.26.spread_ref = bf16[128,48,128]{2,1,0:T(8,128)(2,1)} all-to-all(bf16[128,48,128]{2,1,0:T(8,128)(2,1)S(1)} %copy-done.6), channel_id=1, replica_groups=mesh['yh'=2,'zh'=8,'zp'=2,'x'=4,'yl'=2,'core'=2] {'yh','zh','zp','x'}, dimensions={0} | all-to-all | bytes 3145728 | tf_op jit(solution)/shard_map/all_to_all | solution.py:327
  276.1 2.8 pick.1
  278.8 8.2 %all-to-all-start.4 = ((bf16[128,48,128]{2,1,0:T(8,128)(2,1)}), bf16[128,48,128]{2,1,0:T(8,128)(2,1)S(1)}, u32[]{:S(2)}, u32[]{:S(2)}) async-start(bf16[128,48,128]{2,1,0:T(8,128)(2,1)} %pick.1), calls=%async_computation.5 | async-start | bytes 3145728 | tf_op jit(solution)/shard_map/all_to_all | solution.py:331
  287.8 89.8 %all-to-all-done.4.pieces_ref = bf16[128,48,128]{2,1,0:T(8,128)(2,1)S(1)} async-done(((bf16[128,48,128]{2,1,0:T(8,128)(2,1)}), bf16[128,48,128]{2,1,0:T(8,128)(2,1)S(1)}, u32[]{:S(2)}, u32[]{:S(2)}) %all-to-all-start.4) | async-done | bytes 1572896 | tf_op jit(solution)/shard_map/all_to_all | solution.py:331
  377.6 1.2 copy-done.1
  378.8 2.8 unpack.1
  (29 shorter events, 2.2 us)
Async XLA Ops:
  7.2 64.9 %all-gather.2.cloned.1.call-start = ((), (), s32[]{:S(2)}) async-start(), calls=%async_computation.6 | async-start | bytes 1824768 | tf_op jit(solution)/shard_map/all_gather | solution.py:254
  9.3 16.7 %collective-permute-start.1 = (bf16[512,768]{1,0:T(8,128)(2,1)}, bf16[512,768]{1,0:T(8,128)(2,1)}, u32[]{:S(2)}, u32[]{:S(2)}) collective-permute-start(bf16[512,768]{1,0:T(8,128)(2,1)} %bitcast.18), channel_id=1, source_target_pairs={{0,2},{2,0},{1,3},{3,1},{4,6},{6,4},{5,7},{7,5},{8,10},{10,8},{9,1... | collective-permute-start | bytes 2359304 | tf_op jit(solution)/shard_map/ppermute | solution.py:257
  13.4 29.5 %collective-permute-start.4 = (bf16[768,512]{1,0:T(8,128)(2,1)}, bf16[768,512]{1,0:T(8,128)(2,1)S(1)}, u32[]{:S(2)}, u32[]{:S(2)}) collective-permute-start(bf16[768,512]{1,0:T(8,128)(2,1)} %bitcast.14), channel_id=1, source_target_pairs={{0,2},{2,0},{1,3},{3,1},{4,6},{6,4},{5,7},{7,5},{8,10},{10,8},{9,1... | collective-permute-start | bytes 2359304 | tf_op jit(solution)/shard_map/ppermute | solution.py:257
  15.3 35.5 %collective-permute-start = (bf16[512,768]{1,0:T(8,128)(2,1)}, bf16[512,768]{1,0:T(8,128)(2,1)}, u32[]{:S(2)}, u32[]{:S(2)}) collective-permute-start(bf16[512,768]{1,0:T(8,128)(2,1)} %bitcast.19), channel_id=1, source_target_pairs={{0,1},{1,0},{2,3},{3,2},{4,5},{5,4},{6,7},{7,6},{8,9},{9,8},{10,11... | collective-permute-start | bytes 2359304 | tf_op jit(solution)/shard_map/ppermute | solution.py:258
  24.0 26.9 %collective-permute-start.3 = (bf16[768,512]{1,0:T(8,128)(2,1)}, bf16[768,512]{1,0:T(8,128)(2,1)S(1)}, u32[]{:S(2)}, u32[]{:S(2)}) collective-permute-start(bf16[768,512]{1,0:T(8,128)(2,1)} %bitcast.15), channel_id=1, source_target_pairs={{0,1},{1,0},{2,3},{3,2},{4,5},{5,4},{6,7},{7,6},{8,9},{9,8},{10,11... | collective-permute-start | bytes 2359304 | tf_op jit(solution)/shard_map/ppermute | solution.py:258
  26.0 24.9 %collective-permute-start.2 = (bf16[512,768]{1,0:T(8,128)(2,1)}, bf16[512,768]{1,0:T(8,128)(2,1)}, u32[]{:S(2)}, u32[]{:S(2)}) collective-permute-start(bf16[512,768]{1,0:T(8,128)(2,1)} %collective-permute-done.1.refs_2_), channel_id=1, source_target_pairs={{0,1},{1,0},{2,3},{3,2},{4,5},{5,4},{6,7},{7,6},{8,9},{9,8},{10,11... | collective-permute-start | bytes 2359304 | tf_op jit(solution)/shard_map/ppermute | solution.py:259
  42.9 34.0 %copy-start.2 = (bf16[768,512]{1,0:T(8,128)(2,1)}, bf16[768,512]{1,0:T(8,128)(2,1)S(1)}, u32[]{:S(2)}) copy-start(bf16[768,512]{1,0:T(8,128)(2,1)S(1)} %collective-permute-done.4.refs_6_.refs_2_) | copy-start | bytes 2359300
  42.9 9.8 %collective-permute-start.5 = (bf16[768,512]{1,0:T(8,128)(2,1)S(1)}, bf16[768,512]{1,0:T(8,128)(2,1)S(1)}, u32[]{:S(2)}, u32[]{:S(2)}) collective-permute-start(bf16[768,512]{1,0:T(8,128)(2,1)S(1)} %collective-permute-done.4.refs_6_.refs_2_), channel_id=1, source_target_pairs={{0,1},{1,0},{2,3},{3,2},{4,5},{5,4},{6,7},{7,6},{8,9},{9,8},{10,11... | collective-permute-start | bytes 2359304 | tf_op jit(solution)/shard_map/ppermute | solution.py:259
  50.9 26.0 %copy-start.3 = (bf16[768,512]{1,0:T(8,128)(2,1)}, bf16[768,512]{1,0:T(8,128)(2,1)S(1)}, u32[]{:S(2)}) copy-start(bf16[768,512]{1,0:T(8,128)(2,1)S(1)} %collective-permute-done.3.refs_5_.refs_1_) | copy-start | bytes 2359300
  52.7 0.9 copy-start.4
  110.6 2.0 copy-start
  112.5 49.9 %all-to-all-start.1 = ((bf16[4,16,16,1024]{3,2,1,0:T(8,128)(2,1)}), bf16[4,16,16,1024]{3,2,1,0:T(8,128)(2,1)}, u32[]{:S(2)}, u32[]{:S(2)}) async-start(bf16[4,16,16,1024]{3,2,1,0:T(8,128)(2,1)} %bitcast.13), calls=%async_computation.1 | async-start | bytes 4194304 | tf_op jit(solution)/shard_map/all_to_all | solution.py:274
  127.8 34.6 %collective-permute-start.6 = (bf16[256,1536]{1,0:T(8,128)(2,1)}, bf16[256,1536]{1,0:T(8,128)(2,1)S(1)}, u32[]{:S(2)}, u32[]{:S(2)}) collective-permute-start(bf16[256,1536]{1,0:T(8,128)(2,1)} %forward.1.acts_ref.a0), channel_id=1, source_target_pairs={{0,2},{2,0},{1,3},{3,1},{4,6},{6,4},{5,7},{7,5},{8,10},{10,8},{9,1... | collective-permute-start | bytes 2359304 | tf_op jit(solution)/shard_map/ppermute | solution.py:291
  135.9 30.9 %copy-start.5 = (bf16[256,1536]{1,0:T(8,128)(2,1)S(1)}, bf16[256,1536]{1,0:T(8,128)(2,1)}, u32[]{:S(2)}) copy-start(bf16[256,1536]{1,0:T(8,128)(2,1)} %forward.1.acts_ref.a0) | copy-start | bytes 2359300
  162.5 12.2 %copy-start.7 = (bf16[256,1536]{1,0:T(8,128)(2,1)}, bf16[256,1536]{1,0:T(8,128)(2,1)S(1)}, u32[]{:S(2)}) copy-start(bf16[256,1536]{1,0:T(8,128)(2,1)S(1)} %collective-permute-done.6.a2) | copy-start | bytes 2359300
  162.5 21.9 %all-to-all-start.2 = ((bf16[16,4,16,512]{3,2,1,0:T(8,128)(2,1)}), bf16[16,4,16,512]{3,2,1,0:T(8,128)(2,1)}, u32[]{:S(2)}, u32[]{:S(2)}) async-start(bf16[16,4,16,512]{3,2,1,0:T(8,128)(2,1)} %expert_out.1), calls=%async_computation.2 | async-start | bytes 2097152 | tf_op jit(solution)/shard_map/all_to_all | solution.py:306
  166.8 4.7 %collective-permute-start.7 = (bf16[256,1536]{1,0:T(8,128)(2,1)S(1)}, bf16[256,1536]{1,0:T(8,128)(2,1)S(1)}, u32[]{:S(2)}, u32[]{:S(2)}) collective-permute-start(bf16[256,1536]{1,0:T(8,128)(2,1)S(1)} %copy-done.5), channel_id=1, source_target_pairs={{0,1},{1,0},{2,3},{3,2},{4,5},{5,4},{6,7},{7,6},{8,9},{9,8},{10,11... | collective-permute-start | bytes 2359304 | tf_op jit(solution)/shard_map/ppermute | solution.py:292
  169.6 4.2 %collective-permute-start.8 = (bf16[256,1536]{1,0:T(8,128)(2,1)S(1)}, bf16[256,1536]{1,0:T(8,128)(2,1)S(1)}, u32[]{:S(2)}, u32[]{:S(2)}) collective-permute-start(bf16[256,1536]{1,0:T(8,128)(2,1)S(1)} %collective-permute-done.6.a2), channel_id=1, source_target_pairs={{0,1},{1,0},{2,3},{3,2},{4,5},{5,4},{6,7},{7,6},{8,9},{9,8},{10,11... | collective-permute-start | bytes 2359304 | tf_op jit(solution)/shard_map/ppermute | solution.py:305
  171.6 3.1 copy-start.8
  173.8 0.9 copy-start.9
  180.7 6.7 %copy-start.6 = (bf16[128,48,128]{2,1,0:T(8,128)(2,1)S(1)}, bf16[128,48,128]{2,1,0:T(8,128)(2,1)}, u32[]{:S(2)}) copy-start(bf16[128,48,128]{2,1,0:T(8,128)(2,1)} %moments.1) | copy-start | bytes 4718596
  278.8 98.7 %all-to-all-start.4 = ((bf16[128,48,128]{2,1,0:T(8,128)(2,1)}), bf16[128,48,128]{2,1,0:T(8,128)(2,1)S(1)}, u32[]{:S(2)}, u32[]{:S(2)}) async-start(bf16[128,48,128]{2,1,0:T(8,128)(2,1)} %pick.1), calls=%async_computation.5 | async-start | bytes 3145728 | tf_op jit(solution)/shard_map/all_to_all | solution.py:331
  287.1 94.5 %reduce-scatter.2.cloned.1.call-start = ((), (), s32[]{:S(2)}) async-start(), calls=%async_computation.7 | async-start | bytes 884736 | tf_op jit(solution)/shard_map/reduce_scatter | solution.py:325
  377.6 1.2 copy-start.1
Sparse Core Ops, SparseCore 0:
  10.1 61.9 all-gather.1
  291.3 75.2 reduce-scatter.1

commit v3 on v2

--- a/solution.py
+++ b/solution.py
@@ -18,7 +18,7 @@
 HBM = pl.BlockSpec(memory_space=pltpu.HBM)
 
 
-def call(kernel, name, out_shape, in_specs, flops, moved, scratch=()):
+def call(kernel, name, out_shape, in_specs, flops, moved, scratch=(), grant=62):
     outs = jax.tree.map(lambda _: VMEM, out_shape)
     return pl.pallas_call(
         kernel,
@@ -27,7 +27,7 @@
         in_specs=in_specs,
         out_specs=outs,
         scratch_shapes=scratch,
-        compiler_params=pltpu.CompilerParams(vmem_limit_bytes=62 * 1024 * 1024),
+        compiler_params=pltpu.CompilerParams(vmem_limit_bytes=grant * 1024 * 1024),
         cost_estimate=pl.CostEstimate(flops=flops, bytes_accessed=moved, transcendentals=0),
     )
 
@@ -150,24 +150,31 @@
     out_ref[:, hidden_count:] = (back * sigmoid * (1.0 + preact * (1.0 - sigmoid))).astype(BF16)
 
 
-def expert_out_kernel(me_ref, acts_ref, *refs):
-    sources, out_ref, downs, sems = refs[:4], refs[4], refs[5], refs[6]
+def expert_out_kernel(me_ref, column_ref, acts_ref, *refs):
+    sources, outs = refs[:4], refs[4:20]
+    downs, rows, sems = refs[20:]
     copies = fetch([(sources[j], downs.at[j]) for j in range(4)], sems)
-    targets, _, per_target, quarter = out_ref.shape
+    targets, _, per_target, quarter = rows.shape
     hidden = acts_ref[:, : downs.shape[1]]
-    me = me_ref[0]
+    me, column = me_ref[0], column_ref[0]
     for j in range(4):
         copies[j].wait()
         part = jnp.dot(hidden, downs[j], preferred_element_type=F32).astype(BF16)
-        out_ref[:, me ^ j] = part.reshape(targets, per_target, quarter)
-
-
-def combine_kernel(share_ref, returned_ref, out_ref):
-    targets, quarters, per_target, quarter = returned_ref.shape
+        rows[:, me ^ j] = part.reshape(targets, per_target, quarter)
+    for r in range(targets):
+        outs[r][...] = rows[column ^ r]
+
+
+def combine_kernel(column_ref, share_ref, *refs):
+    returned, out_ref, rows = refs[:16], refs[16], refs[17]
+    targets, quarters, per_target, quarter = rows.shape
+    column = column_ref[0]
+    for r in range(targets):
+        rows[column ^ r] = returned[r][...]
     shares = split3(share_ref[...])
     for q in range(quarters):
-        rows = returned_ref[:, q].reshape(targets * per_target, quarter)
-        mixed = sum(jnp.dot(part, rows, preferred_element_type=F32) for part in shares)
+        part = rows[:, q].reshape(targets * per_target, quarter)
+        mixed = sum(jnp.dot(share, part, preferred_element_type=F32) for share in shares)
         out_ref[:, q * quarter : (q + 1) * quarter] = mixed.astype(BF16)
 
 
@@ -247,6 +254,7 @@
 ):
     plane = lax.axis_index("zh").reshape(1).astype(jnp.int32)
     me = lax.axis_index(DP_AXES).reshape(1).astype(jnp.int32)
+    column = lax.axis_index(GROUP_AXES).reshape(1).astype(jnp.int32)
 
     packed = call(pack_kernel, "pack", shape_of((24, 4224)), [VMEM] * 5, 10**6, 4 * 10**5)(
         tokens, cotangent, expert_ids.T, route_weight.T, holder.reshape(1, -1)
@@ -290,23 +298,24 @@
     )(me, rows, *ups, *downs)
     acts2 = lax.ppermute(acts, "yl", FLIP)
     acts1 = lax.ppermute(acts, "core", FLIP)
-
     expert_out = call(
         expert_out_kernel,
         "expert_out",
-        shape_of((16, 4, 16, 512)),
-        [SMEM, VMEM] + [HBM] * 4,
+        [shape_of((4, 16, 512))] * 16,
+        [SMEM, SMEM, VMEM] + [HBM] * 4,
         8 * 10**8,
         5 * 10**6,
-        (pltpu.VMEM((4, 768, 512), BF16), pltpu.SemaphoreType.DMA((4,))),
-    )(me, acts, *downs)
-
-    by_feature, acts2, expert_out = lax.optimization_barrier((by_feature, acts2, expert_out))
+        (
+            pltpu.VMEM((4, 768, 512), BF16),
+            pltpu.VMEM((16, 4, 16, 512), BF16),
+            pltpu.SemaphoreType.DMA((4,)),
+        ),
+    )(me, column, acts, *downs)
+    by_feature, acts1, acts2, expert_out = lax.optimization_barrier(
+        (by_feature, acts1, acts2, expert_out)
+    )
     acts3 = lax.ppermute(acts2, "core", FLIP)
-    returned = lax.all_to_all(expert_out, GROUP_AXES, split_axis=0, concat_axis=0, tiled=True)
-    partial = call(
-        combine_kernel, "combine", shape_of((192, 2048)), [VMEM, VMEM], 6 * 10**8, 2 * 10**6
-    )(share, returned)
+
     pieces = call(
         moment_kernel,
         "moments",
@@ -321,12 +330,28 @@
         ),
     )(me, by_feature, acts, acts1, acts2, acts3, up_moment[0], down_moment[0])
 
-    partial, pieces = lax.optimization_barrier((partial, pieces))
+    spread = lax.all_to_all(pieces, SLOT_AXES, split_axis=0, concat_axis=0, tiled=True)
+
+    _, expert_out = lax.optimization_barrier((pieces, expert_out))
+    returned = [expert_out[0]] + [
+        lax.ppermute(expert_out[r], GROUP_AXES, [(c, c ^ r) for c in range(16)])
+        for r in range(1, 16)
+    ]
+    partial = call(
+        combine_kernel,
+        "combine",
+        shape_of((192, 2048)),
+        [SMEM, VMEM] + [VMEM] * 16,
+        6 * 10**8,
+        2 * 10**6,
+        (pltpu.VMEM((16, 4, 16, 512), BF16),),
+        16,
+    )(column, share, *returned)
+    spread, partial = lax.optimization_barrier((spread, partial))
     layer_out = lax.psum_scatter(partial, "zh", scatter_dimension=0, tiled=True)
 
-    spread = lax.all_to_all(pieces, SLOT_AXES, split_axis=0, concat_axis=0, tiled=True)
     chosen = call(
-        pick_kernel, "pick", shape_of((128, 48, 128)), [SMEM, VMEM], 0, 3 * 10**6
+        pick_kernel, "pick", shape_of((128, 48, 128)), [SMEM, VMEM], 0, 3 * 10**6, (), 12
     )(partner, spread)
     landed = lax.all_to_all(chosen, SLOT_AXES, split_axis=0, concat_axis=0, tiled=True)
     new_up, new_down = call(
@@ -336,6 +361,8 @@
         [VMEM],
         0,
         3 * 10**6,
+        (),
+        12,
     )(landed)
     return layer_out, new_up[None], new_down[None]
 

time: 393 us -> 413 us (1.051)
  blocking collectives: 122 us -> 33.4 us
  starting transfers between devices: 68.1 us -> 143 us
  waiting for transfers between devices: 145 us -> 183 us
    all_to_all x1 -> x0, blocking collectives: 88.7 us -> none  [body(): lax.all_to_all(pieces, SLOT_AXES, split_axis=0, concat_axis=0, tiled=True)]
    ppermute x0 -> x15, starting transfers between devices: none -> 60.2 us  [body(): lax.ppermute(expert_out[r], GROUP_AXES, [(c, c ^ r) for c in range(16)])]
    ppermute x0 -> x15, waiting for transfers between devices: none -> 44.6 us  [body(): lax.ppermute(expert_out[r], GROUP_AXES, [(c, c ^ r) for c in range(16)])]
    all_to_all x1, starting transfers between devices: 8.2 us -> 17.9 us  [body(): lax.all_to_all(chosen, SLOT_AXES, split_axis=0, concat_axis=0, tiled=True)]
    ppermute x1, starting transfers between devices: 1.92 us -> 8.68 us  [body(): lax.ppermute(down0, 'core', FLIP)]
    ppermute x1, starting transfers between devices: 8.68 us -> 1.92 us  [body(): lax.ppermute(up0, 'core', FLIP)]
    ppermute x1, starting transfers between devices: 7.95 us -> 14.7 us  [body(): lax.ppermute(down2, 'core', FLIP)]
    ppermute x1, starting transfers between devices: 14.8 us -> 8.05 us  [body(): lax.ppermute(up2, 'core', FLIP)]
  transfers between devices with their start and end apart: 14 -> 29, of which waited for: 8 -> 11; matrix products, arithmetic and copies ran while one was open for 0% -> 0% of each run, Pallas kernels for 5% -> 4%
where the time goes in v3:
time: 413 us; the launch traced here: 408 us
  waiting for transfers between devices  183 us (44%)
  starting transfers between devices  143 us (35%)
  blocking collectives  33.4 us (8%)
  Pallas kernels  29.9 us (7%)
  between operations  14.7 us (4%)
    all_to_all x1, waiting for transfers between devices, body(): lax.all_to_all(chosen, SLOT_AXES, split_axis=0, concat_axis=0, tiled=True)  89.1 us
    ppermute x15, starting transfers between devices, body(): lax.ppermute(expert_out[r], GROUP_AXES, [(c, c ^ r) for c in range(16)])  60.2 us
    ppermute x15, waiting for transfers between devices, body(): lax.ppermute(expert_out[r], GROUP_AXES, [(c, c ^ r) for c in range(16)])  44.6 us
    all_to_all x1, blocking collectives, body(): lax.all_to_all(outgoing, GROUP_AXES, split_axis=0, concat_axis=0, tiled=T...  33.4 us
    ppermute x1, waiting for transfers between devices, body(): acts2 = lax.ppermute(acts, 'yl', FLIP)  24.1 us
    all_gather x1, waiting for transfers between devices, body(): gathered = lax.all_gather(packed, 'zh', axis=0, tiled=True)  18.9 us
    all_to_all x1, starting transfers between devices, body(): lax.all_to_all(chosen, SLOT_AXES, split_axis=0, concat_axis=0, tiled=True)  17.9 us
    ppermute x1, starting transfers between devices, body(): lax.ppermute(down2, 'core', FLIP)  14.7 us
  transfers between devices with their start and end apart: 29, of which 11 were waited for; matrix products, arithmetic and copies ran while one was open for 0% of the time, Pallas kernels for 4%

profile of v3, /device:TPU:1, one launch (start us, length us, event | category | flops | bytes accessed | tf_op | source)
XLA Modules:
  0.0 408.0 jit_solution(9224462997237596106)
XLA Ops:
  9.3 4.0 collective-permute-start.4
  15.3 8.7 %collective-permute-start.3 = (bf16[768,512]{1,0:T(8,128)(2,1)}, bf16[768,512]{1,0:T(8,128)(2,1)S(1)}, u32[]{:S(2)}, u32[]{:S(2)}) collective-permute-start(bf16[768,512]{1,0:T(8,128)(2,1)} %bitcast.16), channel_id=1, source_target_pairs={{0,1},{1,0},{2,3},{3,2},{4,5},{5,4},{6,7},{7,6},{8,9},{9,8},{10,11... | collective-permute-start | bytes 2359304 | tf_op jit(solution)/shard_map/ppermute | solution.py:266
  26.0 14.7 %collective-permute-start.5 = (bf16[768,512]{1,0:T(8,128)(2,1)S(1)}, bf16[768,512]{1,0:T(8,128)(2,1)S(1)}, u32[]{:S(2)}, u32[]{:S(2)}) collective-permute-start(bf16[768,512]{1,0:T(8,128)(2,1)S(1)} %collective-permute-done.4.refs_6_.refs_2_), channel_id=1, source_target_pairs={{0,1},{1,0},{2,3},{3,2},{4,5},{5,4},{6,7},{7,6},{8,9},{9,8},{10,11... | collective-permute-start | bytes 2359304 | tf_op jit(solution)/shard_map/ppermute | solution.py:267
  40.7 2.2 collective-permute-done.1.refs_2_
  42.9 8.1 %collective-permute-start.2 = (bf16[512,768]{1,0:T(8,128)(2,1)}, bf16[512,768]{1,0:T(8,128)(2,1)}, u32[]{:S(2)}, u32[]{:S(2)}) collective-permute-start(bf16[512,768]{1,0:T(8,128)(2,1)} %collective-permute-done.1.refs_2_), channel_id=1, source_target_pairs={{0,1},{1,0},{2,3},{3,2},{4,5},{5,4},{6,7},{7,6},{8,9},{9,8},{10,11... | collective-permute-start | bytes 2359304 | tf_op jit(solution)/shard_map/ppermute | solution.py:267
  53.2 18.9 %all-gather.2.cloned.1.call-done.gathered_ref = bf16[192,4224]{1,0:T(8,128)(2,1)} async-done(((bf16[24,4224]{1,0:T(8,128)(2,1)}), bf16[192,4224]{1,0:T(8,128)(2,1)}) %all-gather.2.cloned.1.call-update) | async-done | bytes 1622032 | tf_op jit(solution)/shard_map/all_gather | solution.py:262
  72.1 4.8 %select.1 = (bf16[16,4,16,1024]{3,2,1,0:T(8,128)(2,1)}, f32[192,256]{1,0:T(8,128)}) custom-call(s32[1]{0:T(128)} %bitcast.1.plane_ref, bf16[192,4224]{1,0:T(8,128)(2,1)} %all-gather.2.cloned.1.call-done.gathered_ref), custom_call_target="tpu_custom_call" | custom-call | flops 1000000000 | bytes 4000000 | tf_op jit(solution)/shard_map/select/pallas_call | solution.py:273
  76.9 33.4 %all_to_all.20.rows_ref = bf16[16,4,16,1024]{3,2,1,0:T(8,128)(2,1)S(1)} all-to-all(bf16[16,4,16,1024]{3,2,1,0:T(8,128)(2,1)} %get-tuple-element.68), channel_id=1, replica_groups=mesh['yh'=2,'zh'=8,'zp'=2,'x'=4,'yl'=2,'core'=2] {'yh','zp','x'}, dimensions={0} | all-to-all | bytes 4194304 | tf_op jit(solution)/shard_map/all_to_all | solution.py:281
  112.3 8.4 %all-to-all-start.1 = ((bf16[4,16,16,1024]{3,2,1,0:T(8,128)(2,1)}), bf16[4,16,16,1024]{3,2,1,0:T(8,128)(2,1)}, u32[]{:S(2)}, u32[]{:S(2)}) async-start(bf16[4,16,16,1024]{3,2,1,0:T(8,128)(2,1)} %bitcast.14), calls=%async_computation.1 | async-start | bytes 4194304 | tf_op jit(solution)/shard_map/all_to_all | solution.py:282
  120.7 7.1 %forward.1.acts_ref.a0 = bf16[256,1536]{1,0:T(8,128)(2,1)} custom-call(s32[1]{0:T(128)} %bitcast.me_ref, bf16[16,4,16,1024]{3,2,1,0:T(8,128)(2,1)} %copy-done.3, bf16[512,768]{1,0:T(8,128)(2,1)} %bitcast.21, bf16[512,768]{1,0:T(8,128)(2,1)} %collective-permute-done.refs_1_, bf16[512,768]{1,0:T(8,128)(2,1)} %collective-permute-done.1.refs_2_, ...), custom_call_target="tpu_custom_call" | custom-call | flops 1600000000 | bytes 9000000 | tf_op jit(solution)/shard_map/forward/pallas_call | solution.py:286
  129.8 3.6 collective-permute-start.7
  133.4 4.8 %expert_out.1 = (bf16[4,16,512]{2,1,0:T(8,128)(2,1)}, bf16[4,16,512]{2,1,0:T(8,128)(2,1)}, bf16[4,16,512]{2,1,0:T(8,128)(2,1)}, bf16[4,16,512]{2,1,0:T(8,128)(2,...) custom-call(s32[1]{0:T(128)} %bitcast.me_ref, ...), custom_call_target="tpu_custom_call" | custom-call | flops 800000000 | bytes 5000000 | tf_op jit(solution)/shard_map/expert_out/pallas_call | solution.py:301
  138.2 24.1 %collective-permute-done.7.a2 = bf16[256,1536]{1,0:T(8,128)(2,1)S(1)} collective-permute-done((bf16[256,1536]{1,0:T(8,128)(2,1)}, bf16[256,1536]{1,0:T(8,128)(2,1)S(1)}, u32[]{:S(2)}, u32[]{:S(2)}) %collective-permute-start.7) | collective-permute-done | bytes 786464 | tf_op jit(solution)/shard_map/ppermute | solution.py:299
  162.4 2.8 collective-permute-start.8
  167.9 6.0 %moments.1 = bf16[128,48,128]{2,1,0:T(8,128)(2,1)} custom-call(s32[1]{0:T(128)} %bitcast.me_ref, bf16[4,16,16,1024]{3,2,1,0:T(8,128)(2,1)} %all-to-all-done.1.rows_ref, bf16[256,1536]{1,0:T(8,128)(2,1)} %forward.1.acts_ref.a0, bf16[256,1536]{1,0:T(8,128)(2,1)} %copy-done.7, bf16[256,1536]{1,0:T(8,128)(2,1)} %copy-done.8, bf16[256,1536]{1,0:T(8,128)(2,1)} %copy-done.9, ...), custom_call_target="tpu_custom_call" | custom-call | flops 3200000000 | bytes 9000000 | tf_op jit(solution)/shard_map/moments/pallas_call | solution.py:319
  174.1 9.1 %all-to-all-start.2 = ((bf16[128,48,128]{2,1,0:T(8,128)(2,1)}), bf16[128,48,128]{2,1,0:T(8,128)(2,1)S(1)}, u32[]{:S(2)}, u32[]{:S(2)}) async-start(bf16[128,48,128]{2,1,0:T(8,128)(2,1)} %moments.1), calls=%async_computation.2 | async-start | bytes 3145728 | tf_op jit(solution)/shard_map/all_to_all | solution.py:333
  183.2 4.0 collective-permute-start.10
  187.2 2.8 collective-permute-start.11
  190.0 3.1 collective-permute-start.12
  195.1 5.8 %collective-permute-start.14 = (bf16[4,16,512]{2,1,0:T(8,128)(2,1)S(1)}, bf16[4,16,512]{2,1,0:T(8,128)(2,1)S(1)}, u32[]{:S(2)}, u32[]{:S(2)}) collective-permute-start(bf16[4,16,512]{2,1,0:T(8,128)(2,1)S(1)} %copy-done.20), channel_id=1, source_target_pairs={{0,24},{4,28},{8,16},{12,20},{16,8},{20,12},{24,0},{28,4},{256,280... | collective-permute-start | bytes 196616 | tf_op jit(solution)/shard_map/ppermute | solution.py:337
  200.9 2.8 collective-permute-start.15
  203.7 4.9 %collective-permute-start.16 = (bf16[4,16,512]{2,1,0:T(8,128)(2,1)S(1)}, bf16[4,16,512]{2,1,0:T(8,128)(2,1)S(1)}, u32[]{:S(2)}, u32[]{:S(2)}) collective-permute-start(bf16[4,16,512]{2,1,0:T(8,128)(2,1)S(1)} %copy-done.18), channel_id=1, source_target_pairs={{0,256},{4,260},{8,264},{12,268},{16,272},{20,276},{24,280},{28,28... | collective-permute-start | bytes 196616 | tf_op jit(solution)/shard_map/ppermute | solution.py:337
  208.6 41.2 %collective-permute-done.12.refs_4_ = bf16[4,16,512]{2,1,0:T(8,128)(2,1)S(1)} collective-permute-done((bf16[4,16,512]{2,1,0:T(8,128)(2,1)S(1)}, bf16[4,16,512]{2,1,0:T(8,128)(2,1)S(1)}, u32[]{:S(2)}, u32[]{:S(2)}) %collective-permute-start.12) | collective-permute-done | bytes 65568 | tf_op jit(solution)/shard_map/ppermute | solution.py:337
  249.8 3.7 collective-permute-start.17
  253.8 7.0 %collective-permute-start.18 = (bf16[4,16,512]{2,1,0:T(8,128)(2,1)S(1)}, bf16[4,16,512]{2,1,0:T(8,128)(2,1)S(1)}, u32[]{:S(2)}, u32[]{:S(2)}) collective-permute-start(bf16[4,16,512]{2,1,0:T(8,128)(2,1)S(1)} %copy-done.16), channel_id=1, source_target_pairs={{0,264},{4,268},{8,256},{12,260},{16,280},{20,284},{24,272},{28,27... | collective-permute-start | bytes 196616 | tf_op jit(solution)/shard_map/ppermute | solution.py:337
  260.8 3.9 collective-permute-start.19
  266.9 3.2 collective-permute-start.21
  270.2 7.8 %collective-permute-start.22 = (bf16[4,16,512]{2,1,0:T(8,128)(2,1)S(1)}, bf16[4,16,512]{2,1,0:T(8,128)(2,1)S(1)}, u32[]{:S(2)}, u32[]{:S(2)}) collective-permute-start(bf16[4,16,512]{2,1,0:T(8,128)(2,1)S(1)} %copy-done.12), channel_id=1, source_target_pairs={{0,280},{4,284},{8,272},{12,276},{16,264},{20,268},{24,256},{28,26... | collective-permute-start | bytes 196616 | tf_op jit(solution)/shard_map/ppermute | solution.py:337
  278.0 5.2 %collective-permute-start.23 = (bf16[4,16,512]{2,1,0:T(8,128)(2,1)S(1)}, bf16[4,16,512]{2,1,0:T(8,128)(2,1)S(1)}, u32[]{:S(2)}, u32[]{:S(2)}) collective-permute-start(bf16[4,16,512]{2,1,0:T(8,128)(2,1)S(1)} %copy-done.11), channel_id=1, source_target_pairs={{0,284},{4,280},{8,276},{12,272},{16,268},{20,264},{24,260},{28,25... | collective-permute-start | bytes 196616 | tf_op jit(solution)/shard_map/ppermute | solution.py:337
  285.2 2.6 collective-permute-done.23.refs_15_
  292.0 17.9 %all-to-all-start.3 = ((bf16[128,48,128]{2,1,0:T(8,128)(2,1)}), bf16[128,48,128]{2,1,0:T(8,128)(2,1)S(1)}, u32[]{:S(2)}, u32[]{:S(2)}) async-start(bf16[128,48,128]{2,1,0:T(8,128)(2,1)} %pick.1), calls=%async_computation.4 | async-start | bytes 3145728 | tf_op jit(solution)/shard_map/all_to_all | solution.py:356
  310.6 89.1 %all-to-all-done.3.pieces_ref = bf16[128,48,128]{2,1,0:T(8,128)(2,1)S(1)} async-done(((bf16[128,48,128]{2,1,0:T(8,128)(2,1)}), bf16[128,48,128]{2,1,0:T(8,128)(2,1)S(1)}, u32[]{:S(2)}, u32[]{:S(2)}) %all-to-all-start.3) | async-done | bytes 1572896 | tf_op jit(solution)/shard_map/all_to_all | solution.py:356
  (88 shorter events, 27.7 us)
Async XLA Ops:
  7.2 64.9 %all-gather.2.cloned.1.call-start = ((), (), s32[]{:S(2)}) async-start(), calls=%async_computation.5 | async-start | bytes 1824768 | tf_op jit(solution)/shard_map/all_gather | solution.py:262
  9.3 16.7 %collective-permute-start.4 = (bf16[768,512]{1,0:T(8,128)(2,1)}, bf16[768,512]{1,0:T(8,128)(2,1)S(1)}, u32[]{:S(2)}, u32[]{:S(2)}) collective-permute-start(bf16[768,512]{1,0:T(8,128)(2,1)} %bitcast.15), channel_id=1, source_target_pairs={{0,2},{2,0},{1,3},{3,1},{4,6},{6,4},{5,7},{7,5},{8,10},{10,8},{9,1... | collective-permute-start | bytes 2359304 | tf_op jit(solution)/shard_map/ppermute | solution.py:265
  13.4 29.5 %collective-permute-start.1 = (bf16[512,768]{1,0:T(8,128)(2,1)}, bf16[512,768]{1,0:T(8,128)(2,1)}, u32[]{:S(2)}, u32[]{:S(2)}) collective-permute-start(bf16[512,768]{1,0:T(8,128)(2,1)} %bitcast.19), channel_id=1, source_target_pairs={{0,2},{2,0},{1,3},{3,1},{4,6},{6,4},{5,7},{7,5},{8,10},{10,8},{9,1... | collective-permute-start | bytes 2359304 | tf_op jit(solution)/shard_map/ppermute | solution.py:265
  15.3 35.6 %collective-permute-start.3 = (bf16[768,512]{1,0:T(8,128)(2,1)}, bf16[768,512]{1,0:T(8,128)(2,1)S(1)}, u32[]{:S(2)}, u32[]{:S(2)}) collective-permute-start(bf16[768,512]{1,0:T(8,128)(2,1)} %bitcast.16), channel_id=1, source_target_pairs={{0,1},{1,0},{2,3},{3,2},{4,5},{5,4},{6,7},{7,6},{8,9},{9,8},{10,11... | collective-permute-start | bytes 2359304 | tf_op jit(solution)/shard_map/ppermute | solution.py:266
  24.0 27.0 %collective-permute-start = (bf16[512,768]{1,0:T(8,128)(2,1)}, bf16[512,768]{1,0:T(8,128)(2,1)}, u32[]{:S(2)}, u32[]{:S(2)}) collective-permute-start(bf16[512,768]{1,0:T(8,128)(2,1)} %bitcast.20), channel_id=1, source_target_pairs={{0,1},{1,0},{2,3},{3,2},{4,5},{5,4},{6,7},{7,6},{8,9},{9,8},{10,11... | collective-permute-start | bytes 2359304 | tf_op jit(solution)/shard_map/ppermute | solution.py:266
  26.0 25.0 %collective-permute-start.5 = (bf16[768,512]{1,0:T(8,128)(2,1)S(1)}, bf16[768,512]{1,0:T(8,128)(2,1)S(1)}, u32[]{:S(2)}, u32[]{:S(2)}) collective-permute-start(bf16[768,512]{1,0:T(8,128)(2,1)S(1)} %collective-permute-done.4.refs_6_.refs_2_), channel_id=1, source_target_pairs={{0,1},{1,0},{2,3},{3,2},{4,5},{5,4},{6,7},{7,6},{8,9},{9,8},{10,11... | collective-permute-start | bytes 2359304 | tf_op jit(solution)/shard_map/ppermute | solution.py:267
  42.9 10.3 %collective-permute-start.2 = (bf16[512,768]{1,0:T(8,128)(2,1)}, bf16[512,768]{1,0:T(8,128)(2,1)}, u32[]{:S(2)}, u32[]{:S(2)}) collective-permute-start(bf16[512,768]{1,0:T(8,128)(2,1)} %collective-permute-done.1.refs_2_), channel_id=1, source_target_pairs={{0,1},{1,0},{2,3},{3,2},{4,5},{5,4},{6,7},{7,6},{8,9},{9,8},{10,11... | collective-permute-start | bytes 2359304 | tf_op jit(solution)/shard_map/ppermute | solution.py:267
  112.3 50.0 %all-to-all-start.1 = ((bf16[4,16,16,1024]{3,2,1,0:T(8,128)(2,1)}), bf16[4,16,16,1024]{3,2,1,0:T(8,128)(2,1)}, u32[]{:S(2)}, u32[]{:S(2)}) async-start(bf16[4,16,16,1024]{3,2,1,0:T(8,128)(2,1)} %bitcast.14), calls=%async_computation.1 | async-start | bytes 4194304 | tf_op jit(solution)/shard_map/all_to_all | solution.py:282
  127.8 10.4 %collective-permute-start.6 = (bf16[256,1536]{1,0:T(8,128)(2,1)}, bf16[256,1536]{1,0:T(8,128)(2,1)S(1)}, u32[]{:S(2)}, u32[]{:S(2)}) collective-permute-start(bf16[256,1536]{1,0:T(8,128)(2,1)} %forward.1.acts_ref.a0), channel_id=1, source_target_pairs={{0,1},{1,0},{2,3},{3,2},{4,5},{5,4},{6,7},{7,6},{8,9},{9,8},{10,11... | collective-permute-start | bytes 2359304 | tf_op jit(solution)/shard_map/ppermute | solution.py:300
  129.8 32.6 %collective-permute-start.7 = (bf16[256,1536]{1,0:T(8,128)(2,1)}, bf16[256,1536]{1,0:T(8,128)(2,1)S(1)}, u32[]{:S(2)}, u32[]{:S(2)}) collective-permute-start(bf16[256,1536]{1,0:T(8,128)(2,1)} %forward.1.acts_ref.a0), channel_id=1, source_target_pairs={{0,2},{2,0},{1,3},{3,1},{4,6},{6,4},{5,7},{7,5},{8,10},{10,8},{9,1... | collective-permute-start | bytes 2359304 | tf_op jit(solution)/shard_map/ppermute | solution.py:299
  162.4 4.7 %collective-permute-start.8 = (bf16[256,1536]{1,0:T(8,128)(2,1)S(1)}, bf16[256,1536]{1,0:T(8,128)(2,1)S(1)}, u32[]{:S(2)}, u32[]{:S(2)}) collective-permute-start(bf16[256,1536]{1,0:T(8,128)(2,1)S(1)} %collective-permute-done.7.a2), channel_id=1, source_target_pairs={{0,1},{1,0},{2,3},{3,2},{4,5},{5,4},{6,7},{7,6},{8,9},{9,8},{10,11... | collective-permute-start | bytes 2359304 | tf_op jit(solution)/shard_map/ppermute | solution.py:317
  174.1 109.2 %copy-start.10 = (bf16[4,16,512]{2,1,0:T(8,128)(2,1)S(1)}, bf16[4,16,512]{2,1,0:T(8,128)(2,1)}, u32[]{:S(2)}) copy-start(bf16[4,16,512]{2,1,0:T(8,128)(2,1)} %get-tuple-element.112) | copy-start | bytes 196612
  174.1 114.2 %copy-start.1 = (bf16[4,16,512]{2,1,0:T(8,128)(2,1)S(1)}, bf16[4,16,512]{2,1,0:T(8,128)(2,1)}, u32[]{:S(2)}) copy-start(bf16[4,16,512]{2,1,0:T(8,128)(2,1)} %get-tuple-element.111.refs_0_) | copy-start | bytes 196612
  174.1 114.2 %copy-start.2 = (f32[192,256]{1,0:T(8,128)S(1)}, f32[192,256]{1,0:T(8,128)}, u32[]{:S(2)}) copy-start(f32[192,256]{1,0:T(8,128)} %get-tuple-element.94.share_ref) | copy-start | bytes 589828
  174.1 115.9 %all-to-all-start.2 = ((bf16[128,48,128]{2,1,0:T(8,128)(2,1)}), bf16[128,48,128]{2,1,0:T(8,128)(2,1)S(1)}, u32[]{:S(2)}, u32[]{:S(2)}) async-start(bf16[128,48,128]{2,1,0:T(8,128)(2,1)} %moments.1), calls=%async_computation.2 | async-start | bytes 3145728 | tf_op jit(solution)/shard_map/all_to_all | solution.py:333
  183.2 17.6 %collective-permute-start.10 = (bf16[4,16,512]{2,1,0:T(8,128)(2,1)S(1)}, bf16[4,16,512]{2,1,0:T(8,128)(2,1)S(1)}, u32[]{:S(2)}, u32[]{:S(2)}) collective-permute-start(bf16[4,16,512]{2,1,0:T(8,128)(2,1)S(1)} %copy-done.24), channel_id=1, source_target_pairs={{0,8},{4,12},{8,0},{12,4},{16,24},{20,28},{24,16},{28,20},{256,264... | collective-permute-start | bytes 196616 | tf_op jit(solution)/shard_map/ppermute | solution.py:337
  187.2 16.5 %collective-permute-start.11 = (bf16[4,16,512]{2,1,0:T(8,128)(2,1)S(1)}, bf16[4,16,512]{2,1,0:T(8,128)(2,1)S(1)}, u32[]{:S(2)}, u32[]{:S(2)}) collective-permute-start(bf16[4,16,512]{2,1,0:T(8,128)(2,1)S(1)} %copy-done.23), channel_id=1, source_target_pairs={{0,12},{4,8},{8,4},{12,0},{16,28},{20,24},{24,20},{28,16},{256,268... | collective-permute-start | bytes 196616 | tf_op jit(solution)/shard_map/ppermute | solution.py:337
  190.0 59.8 %collective-permute-start.12 = (bf16[4,16,512]{2,1,0:T(8,128)(2,1)S(1)}, bf16[4,16,512]{2,1,0:T(8,128)(2,1)S(1)}, u32[]{:S(2)}, u32[]{:S(2)}) collective-permute-start(bf16[4,16,512]{2,1,0:T(8,128)(2,1)S(1)} %copy-done.22), channel_id=1, source_target_pairs={{0,16},{4,20},{8,24},{12,28},{16,0},{20,4},{24,8},{28,12},{256,272... | collective-permute-start | bytes 196616 | tf_op jit(solution)/shard_map/ppermute | solution.py:337
  193.1 60.6 %collective-permute-start.13 = (bf16[4,16,512]{2,1,0:T(8,128)(2,1)S(1)}, bf16[4,16,512]{2,1,0:T(8,128)(2,1)S(1)}, u32[]{:S(2)}, u32[]{:S(2)}) collective-permute-start(bf16[4,16,512]{2,1,0:T(8,128)(2,1)S(1)} %copy-done.21), channel_id=1, source_target_pairs={{0,20},{4,16},{8,28},{12,24},{16,4},{20,0},{24,12},{28,8},{256,276... | collective-permute-start | bytes 196616 | tf_op jit(solution)/shard_map/ppermute | solution.py:337
  195.1 65.7 %collective-permute-start.14 = (bf16[4,16,512]{2,1,0:T(8,128)(2,1)S(1)}, bf16[4,16,512]{2,1,0:T(8,128)(2,1)S(1)}, u32[]{:S(2)}, u32[]{:S(2)}) collective-permute-start(bf16[4,16,512]{2,1,0:T(8,128)(2,1)S(1)} %copy-done.20), channel_id=1, source_target_pairs={{0,24},{4,28},{8,16},{12,20},{16,8},{20,12},{24,0},{28,4},{256,280... | collective-permute-start | bytes 196616 | tf_op jit(solution)/shard_map/ppermute | solution.py:337
  200.9 63.9 %collective-permute-start.15 = (bf16[4,16,512]{2,1,0:T(8,128)(2,1)S(1)}, bf16[4,16,512]{2,1,0:T(8,128)(2,1)S(1)}, u32[]{:S(2)}, u32[]{:S(2)}) collective-permute-start(bf16[4,16,512]{2,1,0:T(8,128)(2,1)S(1)} %copy-done.19), channel_id=1, source_target_pairs={{0,28},{4,24},{8,20},{12,16},{16,12},{20,8},{24,4},{28,0},{256,284... | collective-permute-start | bytes 196616 | tf_op jit(solution)/shard_map/ppermute | solution.py:337
  203.7 63.2 %collective-permute-start.16 = (bf16[4,16,512]{2,1,0:T(8,128)(2,1)S(1)}, bf16[4,16,512]{2,1,0:T(8,128)(2,1)S(1)}, u32[]{:S(2)}, u32[]{:S(2)}) collective-permute-start(bf16[4,16,512]{2,1,0:T(8,128)(2,1)S(1)} %copy-done.18), channel_id=1, source_target_pairs={{0,256},{4,260},{8,264},{12,268},{16,272},{20,276},{24,280},{28,28... | collective-permute-start | bytes 196616 | tf_op jit(solution)/shard_map/ppermute | solution.py:337
  249.8 20.3 %collective-permute-start.17 = (bf16[4,16,512]{2,1,0:T(8,128)(2,1)S(1)}, bf16[4,16,512]{2,1,0:T(8,128)(2,1)S(1)}, u32[]{:S(2)}, u32[]{:S(2)}) collective-permute-start(bf16[4,16,512]{2,1,0:T(8,128)(2,1)S(1)} %copy-done.17), channel_id=1, source_target_pairs={{0,260},{4,256},{8,268},{12,264},{16,276},{20,272},{24,284},{28,28... | collective-permute-start | bytes 196616 | tf_op jit(solution)/shard_map/ppermute | solution.py:337
  253.8 24.2 %collective-permute-start.18 = (bf16[4,16,512]{2,1,0:T(8,128)(2,1)S(1)}, bf16[4,16,512]{2,1,0:T(8,128)(2,1)S(1)}, u32[]{:S(2)}, u32[]{:S(2)}) collective-permute-start(bf16[4,16,512]{2,1,0:T(8,128)(2,1)S(1)} %copy-done.16), channel_id=1, source_target_pairs={{0,264},{4,268},{8,256},{12,260},{16,280},{20,284},{24,272},{28,27... | collective-permute-start | bytes 196616 | tf_op jit(solution)/shard_map/ppermute | solution.py:337
  260.8 22.4 %collective-permute-start.19 = (bf16[4,16,512]{2,1,0:T(8,128)(2,1)S(1)}, bf16[4,16,512]{2,1,0:T(8,128)(2,1)S(1)}, u32[]{:S(2)}, u32[]{:S(2)}) collective-permute-start(bf16[4,16,512]{2,1,0:T(8,128)(2,1)S(1)} %copy-done.15), channel_id=1, source_target_pairs={{0,268},{4,264},{8,260},{12,256},{16,284},{20,280},{24,276},{28,27... | collective-permute-start | bytes 196616 | tf_op jit(solution)/shard_map/ppermute | solution.py:337
  264.8 20.4 %collective-permute-start.20 = (bf16[4,16,512]{2,1,0:T(8,128)(2,1)S(1)}, bf16[4,16,512]{2,1,0:T(8,128)(2,1)S(1)}, u32[]{:S(2)}, u32[]{:S(2)}) collective-permute-start(bf16[4,16,512]{2,1,0:T(8,128)(2,1)S(1)} %copy-done.14), channel_id=1, source_target_pairs={{0,272},{4,276},{8,280},{12,284},{16,256},{20,260},{24,264},{28,26... | collective-permute-start | bytes 196616 | tf_op jit(solution)/shard_map/ppermute | solution.py:337
  266.9 18.3 %collective-permute-start.21 = (bf16[4,16,512]{2,1,0:T(8,128)(2,1)S(1)}, bf16[4,16,512]{2,1,0:T(8,128)(2,1)S(1)}, u32[]{:S(2)}, u32[]{:S(2)}) collective-permute-start(bf16[4,16,512]{2,1,0:T(8,128)(2,1)S(1)} %copy-done.13), channel_id=1, source_target_pairs={{0,276},{4,272},{8,284},{12,280},{16,260},{20,256},{24,268},{28,26... | collective-permute-start | bytes 196616 | tf_op jit(solution)/shard_map/ppermute | solution.py:337
  270.2 15.0 %collective-permute-start.22 = (bf16[4,16,512]{2,1,0:T(8,128)(2,1)S(1)}, bf16[4,16,512]{2,1,0:T(8,128)(2,1)S(1)}, u32[]{:S(2)}, u32[]{:S(2)}) collective-permute-start(bf16[4,16,512]{2,1,0:T(8,128)(2,1)S(1)} %copy-done.12), channel_id=1, source_target_pairs={{0,280},{4,284},{8,272},{12,276},{16,264},{20,268},{24,256},{28,26... | collective-permute-start | bytes 196616 | tf_op jit(solution)/shard_map/ppermute | solution.py:337
  278.0 9.8 %collective-permute-start.23 = (bf16[4,16,512]{2,1,0:T(8,128)(2,1)S(1)}, bf16[4,16,512]{2,1,0:T(8,128)(2,1)S(1)}, u32[]{:S(2)}, u32[]{:S(2)}) collective-permute-start(bf16[4,16,512]{2,1,0:T(8,128)(2,1)S(1)} %copy-done.11), channel_id=1, source_target_pairs={{0,284},{4,280},{8,276},{12,272},{16,268},{20,264},{24,260},{28,25... | collective-permute-start | bytes 196616 | tf_op jit(solution)/shard_map/ppermute | solution.py:337
  283.3 5.0 %collective-permute-start.9 = (bf16[4,16,512]{2,1,0:T(8,128)(2,1)S(1)}, bf16[4,16,512]{2,1,0:T(8,128)(2,1)S(1)}, u32[]{:S(2)}, u32[]{:S(2)}) collective-permute-start(bf16[4,16,512]{2,1,0:T(8,128)(2,1)S(1)} %copy-done.10), channel_id=1, source_target_pairs={{0,4},{4,0},{8,12},{12,8},{16,20},{20,16},{24,28},{28,24},{256,260... | collective-permute-start | bytes 196616 | tf_op jit(solution)/shard_map/ppermute | solution.py:337
  292.0 107.8 %all-to-all-start.3 = ((bf16[128,48,128]{2,1,0:T(8,128)(2,1)}), bf16[128,48,128]{2,1,0:T(8,128)(2,1)S(1)}, u32[]{:S(2)}, u32[]{:S(2)}) async-start(bf16[128,48,128]{2,1,0:T(8,128)(2,1)} %pick.1), calls=%async_computation.4 | async-start | bytes 3145728 | tf_op jit(solution)/shard_map/all_to_all | solution.py:356
  309.9 91.3 %reduce-scatter.2.cloned.1.call-start = ((), (), s32[]{:S(2)}) async-start(), calls=%async_computation.6 | async-start | bytes 884736 | tf_op jit(solution)/shard_map/reduce_scatter | solution.py:351
  (22 other events, 984.1 us)
Sparse Core Ops, SparseCore 0:
  10.1 61.9 all-gather.1
  314.1 76.2 reduce-scatter.1

commit v4 on v2

--- a/solution.py
+++ b/solution.py
@@ -18,7 +18,7 @@
 HBM = pl.BlockSpec(memory_space=pltpu.HBM)
 
 
-def call(kernel, name, out_shape, in_specs, flops, moved, scratch=()):
+def call(kernel, name, out_shape, in_specs, flops, moved, scratch=(), grant=62):
     outs = jax.tree.map(lambda _: VMEM, out_shape)
     return pl.pallas_call(
         kernel,
@@ -27,7 +27,7 @@
         in_specs=in_specs,
         out_specs=outs,
         scratch_shapes=scratch,
-        compiler_params=pltpu.CompilerParams(vmem_limit_bytes=62 * 1024 * 1024),
+        compiler_params=pltpu.CompilerParams(vmem_limit_bytes=grant * 1024 * 1024),
         cost_estimate=pl.CostEstimate(flops=flops, bytes_accessed=moved, transcendentals=0),
     )
 
@@ -301,11 +301,13 @@
         (pltpu.VMEM((4, 768, 512), BF16), pltpu.SemaphoreType.DMA((4,))),
     )(me, acts, *downs)
 
-    by_feature, acts2, expert_out = lax.optimization_barrier((by_feature, acts2, expert_out))
+    by_feature, acts1, acts2, expert_out = lax.optimization_barrier(
+        (by_feature, acts1, acts2, expert_out)
+    )
     acts3 = lax.ppermute(acts2, "core", FLIP)
     returned = lax.all_to_all(expert_out, GROUP_AXES, split_axis=0, concat_axis=0, tiled=True)
     partial = call(
-        combine_kernel, "combine", shape_of((192, 2048)), [VMEM, VMEM], 6 * 10**8, 2 * 10**6
+        combine_kernel, "combine", shape_of((192, 2048)), [VMEM, VMEM], 6 * 10**8, 2 * 10**6, (), 12
     )(share, returned)
     pieces = call(
         moment_kernel,
@@ -321,12 +323,12 @@
         ),
     )(me, by_feature, acts, acts1, acts2, acts3, up_moment[0], down_moment[0])
 
-    partial, pieces = lax.optimization_barrier((partial, pieces))
     layer_out = lax.psum_scatter(partial, "zh", scatter_dimension=0, tiled=True)
 
     spread = lax.all_to_all(pieces, SLOT_AXES, split_axis=0, concat_axis=0, tiled=True)
+    spread, layer_out = lax.optimization_barrier((spread, layer_out))
     chosen = call(
-        pick_kernel, "pick", shape_of((128, 48, 128)), [SMEM, VMEM], 0, 3 * 10**6
+        pick_kernel, "pick", shape_of((128, 48, 128)), [SMEM, VMEM], 0, 3 * 10**6, (), 12
     )(partner, spread)
     landed = lax.all_to_all(chosen, SLOT_AXES, split_axis=0, concat_axis=0, tiled=True)
     new_up, new_down = call(
@@ -336,6 +338,8 @@
         [VMEM],
         0,
         3 * 10**6,
+        (),
+        12,
     )(landed)
     return layer_out, new_up[None], new_down[None]
 

time: 393 us -> 384 us (0.977)
  Pallas kernels: 33.3 us -> 28.6 us
  blocking collectives: 122 us -> 118 us
    all_to_all x1, waiting for transfers between devices: 89.8 us -> 10.6 us  [body(): lax.all_to_all(pieces, SLOT_AXES, split_axis=0, concat_axis=0, tiled=True)]
    reduce_scatter x1, waiting for transfers between devices: 0.01 us -> 78.3 us  [body(): layer_out = lax.psum_scatter(partial, 'zh', scatter_dimension=0, tiled=True)]
    all_to_all x1, blocking collectives: 88.7 us -> 84.6 us  [body(): lax.all_to_all(chosen, SLOT_AXES, split_axis=0, concat_axis=0, tiled=True)]
  transfers between devices with their start and end apart: 14 -> 14, of which waited for: 8 -> 9; matrix products, arithmetic and copies ran while one was open for 0% -> 0% of each run, Pallas kernels for 5% -> 5%
where the time goes in v4:
time: 384 us; the launch traced here: 377 us
  waiting for transfers between devices  143 us (37%)
  blocking collectives  118 us (31%)
  starting transfers between devices  68.4 us (18%)
  Pallas kernels  28.6 us (7%)
  between operations  14.2 us (4%)
  local copies, waits for them, and re-layouts  4.66 us (1%)
    all_to_all x1, blocking collectives, body(): lax.all_to_all(chosen, SLOT_AXES, split_axis=0, concat_axis=0, tiled=True)  84.6 us
    reduce_scatter x1, waiting for transfers between devices, body(): layer_out = lax.psum_scatter(partial, 'zh', scatter_dimension=0, tiled=True)  78.3 us
    all_to_all x1, blocking collectives, body(): lax.all_to_all(outgoing, GROUP_AXES, split_axis=0, concat_axis=0, tiled=T...  33.7 us
    ppermute x1, waiting for transfers between devices, body(): acts2 = lax.ppermute(acts, 'yl', FLIP)  24 us
    all_gather x1, waiting for transfers between devices, body(): gathered = lax.all_gather(packed, 'zh', axis=0, tiled=True)  18.4 us
    ppermute x1, starting transfers between devices, body(): lax.ppermute(up2, 'core', FLIP)  14.8 us
    all_to_all x1, waiting for transfers between devices, body(): lax.all_to_all(pieces, SLOT_AXES, split_axis=0, concat_axis=0, tiled=True)  10.6 us
    ppermute x1, starting transfers between devices, body(): lax.ppermute(up0, 'core', FLIP)  8.68 us
  transfers between devices with their start and end apart: 14, of which 9 were waited for; matrix products, arithmetic and copies ran while one was open for 0% of the time, Pallas kernels for 5%

profile of v4, /device:TPU:1, one launch (start us, length us, event | category | flops | bytes accessed | tf_op | source)
XLA Modules:
  0.0 377.3 jit_solution(5907802703439504898)
XLA Ops:
  7.2 2.1 pack.1
  9.3 4.0 %collective-permute-start.1 = (bf16[512,768]{1,0:T(8,128)(2,1)}, bf16[512,768]{1,0:T(8,128)(2,1)}, u32[]{:S(2)}, u32[]{:S(2)}) collective-permute-start(bf16[512,768]{1,0:T(8,128)(2,1)} %bitcast.18), channel_id=1, source_target_pairs={{0,2},{2,0},{1,3},{3,1},{4,6},{6,4},{5,7},{7,5},{8,10},{10,8},{9,1... | collective-permute-start | bytes 2359304 | tf_op jit(solution)/shard_map/ppermute | solution.py:257
  13.4 1.9 collective-permute-start.4
  15.3 8.7 %collective-permute-start = (bf16[512,768]{1,0:T(8,128)(2,1)}, bf16[512,768]{1,0:T(8,128)(2,1)}, u32[]{:S(2)}, u32[]{:S(2)}) collective-permute-start(bf16[512,768]{1,0:T(8,128)(2,1)} %bitcast.19), channel_id=1, source_target_pairs={{0,1},{1,0},{2,3},{3,2},{4,5},{5,4},{6,7},{7,6},{8,9},{9,8},{10,11... | collective-permute-start | bytes 2359304 | tf_op jit(solution)/shard_map/ppermute | solution.py:258
  24.0 1.9 collective-permute-start.3
  26.0 14.8 %collective-permute-start.2 = (bf16[512,768]{1,0:T(8,128)(2,1)}, bf16[512,768]{1,0:T(8,128)(2,1)}, u32[]{:S(2)}, u32[]{:S(2)}) collective-permute-start(bf16[512,768]{1,0:T(8,128)(2,1)} %collective-permute-done.1.refs_2_), channel_id=1, source_target_pairs={{0,1},{1,0},{2,3},{3,2},{4,5},{5,4},{6,7},{7,6},{8,9},{9,8},{10,11... | collective-permute-start | bytes 2359304 | tf_op jit(solution)/shard_map/ppermute | solution.py:259
  40.8 2.1 collective-permute-done.4.refs_6_.refs_2_
  42.9 7.9 %collective-permute-start.5 = (bf16[768,512]{1,0:T(8,128)(2,1)S(1)}, bf16[768,512]{1,0:T(8,128)(2,1)S(1)}, u32[]{:S(2)}, u32[]{:S(2)}) collective-permute-start(bf16[768,512]{1,0:T(8,128)(2,1)S(1)} %collective-permute-done.4.refs_6_.refs_2_), channel_id=1, source_target_pairs={{0,1},{1,0},{2,3},{3,2},{4,5},{5,4},{6,7},{7,6},{8,9},{9,8},{10,11... | collective-permute-start | bytes 2359304 | tf_op jit(solution)/shard_map/ppermute | solution.py:259
  50.9 1.8 collective-permute-done.5.refs_7_.refs_3_
  52.7 0.9 copy-done.5
  53.6 18.4 %all-gather.2.cloned.1.call-done.gathered_ref = bf16[192,4224]{1,0:T(8,128)(2,1)} async-done(((bf16[24,4224]{1,0:T(8,128)(2,1)}), bf16[192,4224]{1,0:T(8,128)(2,1)}) %all-gather.2.cloned.1.call-update) | async-done | bytes 1622032 | tf_op jit(solution)/shard_map/all_gather | solution.py:254
  72.0 4.8 %select.1 = (bf16[16,4,16,1024]{3,2,1,0:T(8,128)(2,1)}, f32[192,256]{1,0:T(8,128)}) custom-call(s32[1]{0:T(128)} %bitcast.1.plane_ref, bf16[192,4224]{1,0:T(8,128)(2,1)} %all-gather.2.cloned.1.call-done.gathered_ref), custom_call_target="tpu_custom_call" | custom-call | flops 1000000000 | bytes 4000000 | tf_op jit(solution)/shard_map/select/pallas_call | solution.py:265
  76.9 33.7 %all_to_all.25.rows_ref = bf16[16,4,16,1024]{3,2,1,0:T(8,128)(2,1)S(1)} all-to-all(bf16[16,4,16,1024]{3,2,1,0:T(8,128)(2,1)} %get-tuple-element.21), channel_id=1, replica_groups=mesh['yh'=2,'zh'=8,'zp'=2,'x'=4,'yl'=2,'core'=2] {'yh','zp','x'}, dimensions={0} | all-to-all | bytes 4194304 | tf_op jit(solution)/shard_map/all_to_all | solution.py:273
  110.5 1.6 copy.17
  112.5 8.2 %all-to-all-start.1 = ((bf16[4,16,16,1024]{3,2,1,0:T(8,128)(2,1)}), bf16[4,16,16,1024]{3,2,1,0:T(8,128)(2,1)}, u32[]{:S(2)}, u32[]{:S(2)}) async-start(bf16[4,16,16,1024]{3,2,1,0:T(8,128)(2,1)} %bitcast.13), calls=%async_computation.1 | async-start | bytes 4194304 | tf_op jit(solution)/shard_map/all_to_all | solution.py:274
  120.7 7.0 %forward.1.acts_ref.a0 = bf16[256,1536]{1,0:T(8,128)(2,1)} custom-call(s32[1]{0:T(128)} %bitcast.me_ref, bf16[16,4,16,1024]{3,2,1,0:T(8,128)(2,1)} %copy-done.2, bf16[512,768]{1,0:T(8,128)(2,1)} %bitcast.20, bf16[512,768]{1,0:T(8,128)(2,1)} %collective-permute-done.refs_1_, bf16[512,768]{1,0:T(8,128)(2,1)} %collective-permute-done.1.refs_2_, ...), custom_call_target="tpu_custom_call" | custom-call | flops 1600000000 | bytes 9000000 | tf_op jit(solution)/shard_map/forward/pallas_call | solution.py:278
  127.8 3.3 collective-permute-start.7
  131.1 2.5 collective-permute-start.6
  133.6 4.8 %expert_out.1 = bf16[16,4,16,512]{3,2,1,0:T(8,128)(2,1)} custom-call(s32[1]{0:T(128)} %bitcast.me_ref, bf16[256,1536]{1,0:T(8,128)(2,1)} %forward.1.acts_ref.a0, bf16[768,512]{1,0:T(8,128)(2,1)} %bitcast.17, bf16[768,512]{1,0:T(8,128)(2,1)} %copy-done.4, bf16[768,512]{1,0:T(8,128)(2,1)} %copy-done.3, bf16[768,512]{1,0:T(8,128)(2,1)} %copy-done.5), custom_call_target="tpu_custom_call" | custom-call | flops 800000000 | bytes 5000000 | tf_op jit(solution)/shard_map/expert_out/pallas_call | solution.py:294
  138.4 24.0 %collective-permute-done.7.a2 = bf16[256,1536]{1,0:T(8,128)(2,1)S(1)} collective-permute-done((bf16[256,1536]{1,0:T(8,128)(2,1)}, bf16[256,1536]{1,0:T(8,128)(2,1)S(1)}, u32[]{:S(2)}, u32[]{:S(2)}) %collective-permute-start.7) | collective-permute-done | bytes 786464 | tf_op jit(solution)/shard_map/ppermute | solution.py:291
  162.4 0.9 copy-done.7
  163.3 3.7 all-to-all-start.3
  167.0 2.8 collective-permute-start.8
  169.8 1.9 collective-permute-done.8.a3
  172.5 6.0 %moments.1 = bf16[128,48,128]{2,1,0:T(8,128)(2,1)} custom-call(s32[1]{0:T(128)} %bitcast.me_ref, bf16[4,16,16,1024]{3,2,1,0:T(8,128)(2,1)} %all-to-all-done.1.rows_ref, bf16[256,1536]{1,0:T(8,128)(2,1)} %forward.1.acts_ref.a0, bf16[256,1536]{1,0:T(8,128)(2,1)} %copy-done.7, bf16[256,1536]{1,0:T(8,128)(2,1)} %copy-done.6, bf16[256,1536]{1,0:T(8,128)(2,1)} %copy-done.8, ...), custom_call_target="tpu_custom_call" | custom-call | flops 3200000000 | bytes 9000000 | tf_op jit(solution)/shard_map/moments/pallas_call | solution.py:312
  178.5 5.9 %all-to-all-done.3.returned_ref = bf16[16,4,16,512]{3,2,1,0:T(8,128)(2,1)S(1)} async-done(((bf16[16,4,16,512]{3,2,1,0:T(8,128)(2,1)}), bf16[16,4,16,512]{3,2,1,0:T(8,128)(2,1)S(1)}, u32[]{:S(2)}, u32[]{:S(2)}) %all-to-all-start.3) | async-done | bytes 1048608 | tf_op jit(solution)/shard_map/all_to_all | solution.py:308
  184.4 8.5 %all-to-all-start.2 = ((bf16[128,48,128]{2,1,0:T(8,128)(2,1)}), bf16[128,48,128]{2,1,0:T(8,128)(2,1)S(1)}, u32[]{:S(2)}, u32[]{:S(2)}) async-start(bf16[128,48,128]{2,1,0:T(8,128)(2,1)} %moments.1), calls=%async_computation.2 | async-start | bytes 3145728 | tf_op jit(solution)/shard_map/all_to_all | solution.py:328
  193.0 1.7 combine.1
  194.7 78.3 %reduce-scatter.2.cloned.1.call-done = bf16[24,2048]{1,0:T(8,128)(2,1)} async-done(((bf16[192,2048]{1,0:T(8,128)(2,1)}), bf16[24,2048]{1,0:T(8,128)(2,1)}) %reduce-scatter.2.cloned.1.call-update) | async-done | bytes 98320 | tf_op jit(solution)/shard_map/reduce_scatter | solution.py:326
  273.1 10.6 %all-to-all-done.2.spread_ref = bf16[128,48,128]{2,1,0:T(8,128)(2,1)S(1)} async-done(((bf16[128,48,128]{2,1,0:T(8,128)(2,1)}), bf16[128,48,128]{2,1,0:T(8,128)(2,1)S(1)}, u32[]{:S(2)}, u32[]{:S(2)}) %all-to-all-start.2) | async-done | bytes 1572896 | tf_op jit(solution)/shard_map/all_to_all | solution.py:328
  284.5 84.6 %all_to_all.26.pieces_ref = bf16[128,48,128]{2,1,0:T(8,128)(2,1)S(1)} all-to-all(bf16[128,48,128]{2,1,0:T(8,128)(2,1)S(1)} %pick.1), channel_id=1, replica_groups=mesh['yh'=2,'zh'=8,'zp'=2,'x'=4,'yl'=2,'core'=2] {'yh','zh','zp','x'}, dimensions={0} | all-to-all | bytes 3145728 | tf_op jit(solution)/shard_map/all_to_all | solution.py:333
  369.1 1.4 unpack.1
  (27 shorter events, 2.2 us)
Async XLA Ops:
  7.2 64.9 %all-gather.2.cloned.1.call-start = ((), (), s32[]{:S(2)}) async-start(), calls=%async_computation.6 | async-start | bytes 1824768 | tf_op jit(solution)/shard_map/all_gather | solution.py:254
  9.3 16.7 %collective-permute-start.1 = (bf16[512,768]{1,0:T(8,128)(2,1)}, bf16[512,768]{1,0:T(8,128)(2,1)}, u32[]{:S(2)}, u32[]{:S(2)}) collective-permute-start(bf16[512,768]{1,0:T(8,128)(2,1)} %bitcast.18), channel_id=1, source_target_pairs={{0,2},{2,0},{1,3},{3,1},{4,6},{6,4},{5,7},{7,5},{8,10},{10,8},{9,1... | collective-permute-start | bytes 2359304 | tf_op jit(solution)/shard_map/ppermute | solution.py:257
  13.4 29.5 %collective-permute-start.4 = (bf16[768,512]{1,0:T(8,128)(2,1)}, bf16[768,512]{1,0:T(8,128)(2,1)S(1)}, u32[]{:S(2)}, u32[]{:S(2)}) collective-permute-start(bf16[768,512]{1,0:T(8,128)(2,1)} %bitcast.14), channel_id=1, source_target_pairs={{0,2},{2,0},{1,3},{3,1},{4,6},{6,4},{5,7},{7,5},{8,10},{10,8},{9,1... | collective-permute-start | bytes 2359304 | tf_op jit(solution)/shard_map/ppermute | solution.py:257
  15.3 35.5 %collective-permute-start = (bf16[512,768]{1,0:T(8,128)(2,1)}, bf16[512,768]{1,0:T(8,128)(2,1)}, u32[]{:S(2)}, u32[]{:S(2)}) collective-permute-start(bf16[512,768]{1,0:T(8,128)(2,1)} %bitcast.19), channel_id=1, source_target_pairs={{0,1},{1,0},{2,3},{3,2},{4,5},{5,4},{6,7},{7,6},{8,9},{9,8},{10,11... | collective-permute-start | bytes 2359304 | tf_op jit(solution)/shard_map/ppermute | solution.py:258
  24.0 26.9 %collective-permute-start.3 = (bf16[768,512]{1,0:T(8,128)(2,1)}, bf16[768,512]{1,0:T(8,128)(2,1)S(1)}, u32[]{:S(2)}, u32[]{:S(2)}) collective-permute-start(bf16[768,512]{1,0:T(8,128)(2,1)} %bitcast.15), channel_id=1, source_target_pairs={{0,1},{1,0},{2,3},{3,2},{4,5},{5,4},{6,7},{7,6},{8,9},{9,8},{10,11... | collective-permute-start | bytes 2359304 | tf_op jit(solution)/shard_map/ppermute | solution.py:258
  26.0 24.9 %collective-permute-start.2 = (bf16[512,768]{1,0:T(8,128)(2,1)}, bf16[512,768]{1,0:T(8,128)(2,1)}, u32[]{:S(2)}, u32[]{:S(2)}) collective-permute-start(bf16[512,768]{1,0:T(8,128)(2,1)} %collective-permute-done.1.refs_2_), channel_id=1, source_target_pairs={{0,1},{1,0},{2,3},{3,2},{4,5},{5,4},{6,7},{7,6},{8,9},{9,8},{10,11... | collective-permute-start | bytes 2359304 | tf_op jit(solution)/shard_map/ppermute | solution.py:259
  42.9 34.0 %copy-start.3 = (bf16[768,512]{1,0:T(8,128)(2,1)}, bf16[768,512]{1,0:T(8,128)(2,1)S(1)}, u32[]{:S(2)}) copy-start(bf16[768,512]{1,0:T(8,128)(2,1)S(1)} %collective-permute-done.4.refs_6_.refs_2_) | copy-start | bytes 2359300
  42.9 9.8 %collective-permute-start.5 = (bf16[768,512]{1,0:T(8,128)(2,1)S(1)}, bf16[768,512]{1,0:T(8,128)(2,1)S(1)}, u32[]{:S(2)}, u32[]{:S(2)}) collective-permute-start(bf16[768,512]{1,0:T(8,128)(2,1)S(1)} %collective-permute-done.4.refs_6_.refs_2_), channel_id=1, source_target_pairs={{0,1},{1,0},{2,3},{3,2},{4,5},{5,4},{6,7},{7,6},{8,9},{9,8},{10,11... | collective-permute-start | bytes 2359304 | tf_op jit(solution)/shard_map/ppermute | solution.py:259
  50.9 26.0 %copy-start.4 = (bf16[768,512]{1,0:T(8,128)(2,1)}, bf16[768,512]{1,0:T(8,128)(2,1)S(1)}, u32[]{:S(2)}) copy-start(bf16[768,512]{1,0:T(8,128)(2,1)S(1)} %collective-permute-done.3.refs_5_.refs_1_) | copy-start | bytes 2359300
  52.7 0.9 copy-start.5
  110.5 2.0 copy-start.2
  112.5 49.9 %all-to-all-start.1 = ((bf16[4,16,16,1024]{3,2,1,0:T(8,128)(2,1)}), bf16[4,16,16,1024]{3,2,1,0:T(8,128)(2,1)}, u32[]{:S(2)}, u32[]{:S(2)}) async-start(bf16[4,16,16,1024]{3,2,1,0:T(8,128)(2,1)} %bitcast.13), calls=%async_computation.1 | async-start | bytes 4194304 | tf_op jit(solution)/shard_map/all_to_all | solution.py:274
  127.8 34.6 %collective-permute-start.7 = (bf16[256,1536]{1,0:T(8,128)(2,1)}, bf16[256,1536]{1,0:T(8,128)(2,1)S(1)}, u32[]{:S(2)}, u32[]{:S(2)}) collective-permute-start(bf16[256,1536]{1,0:T(8,128)(2,1)} %forward.1.acts_ref.a0), channel_id=1, source_target_pairs={{0,2},{2,0},{1,3},{3,1},{4,6},{6,4},{5,7},{7,5},{8,10},{10,8},{9,1... | collective-permute-start | bytes 2359304 | tf_op jit(solution)/shard_map/ppermute | solution.py:291
  131.1 31.3 %collective-permute-start.6 = (bf16[256,1536]{1,0:T(8,128)(2,1)}, bf16[256,1536]{1,0:T(8,128)(2,1)S(1)}, u32[]{:S(2)}, u32[]{:S(2)}) collective-permute-start(bf16[256,1536]{1,0:T(8,128)(2,1)} %forward.1.acts_ref.a0), channel_id=1, source_target_pairs={{0,1},{1,0},{2,3},{3,2},{4,5},{5,4},{6,7},{7,6},{8,9},{9,8},{10,11... | collective-permute-start | bytes 2359304 | tf_op jit(solution)/shard_map/ppermute | solution.py:292
  162.4 10.1 %copy-start.6 = (bf16[256,1536]{1,0:T(8,128)(2,1)}, bf16[256,1536]{1,0:T(8,128)(2,1)S(1)}, u32[]{:S(2)}) copy-start(bf16[256,1536]{1,0:T(8,128)(2,1)S(1)} %collective-permute-done.7.a2) | copy-start | bytes 2359300
  162.4 0.9 copy-start.7
  163.3 21.1 %all-to-all-start.3 = ((bf16[16,4,16,512]{3,2,1,0:T(8,128)(2,1)}), bf16[16,4,16,512]{3,2,1,0:T(8,128)(2,1)S(1)}, u32[]{:S(2)}, u32[]{:S(2)}) async-start(bf16[16,4,16,512]{3,2,1,0:T(8,128)(2,1)} %expert_out.1), calls=%async_computation.3 | async-start | bytes 2097152 | tf_op jit(solution)/shard_map/all_to_all | solution.py:308
  167.0 4.7 %collective-permute-start.8 = (bf16[256,1536]{1,0:T(8,128)(2,1)S(1)}, bf16[256,1536]{1,0:T(8,128)(2,1)S(1)}, u32[]{:S(2)}, u32[]{:S(2)}) collective-permute-start(bf16[256,1536]{1,0:T(8,128)(2,1)S(1)} %collective-permute-done.7.a2), channel_id=1, source_target_pairs={{0,1},{1,0},{2,3},{3,2},{4,5},{5,4},{6,7},{7,6},{8,9},{9,8},{10,11... | collective-permute-start | bytes 2359304 | tf_op jit(solution)/shard_map/ppermute | solution.py:307
  171.7 0.9 copy-start.8
  178.5 14.5 %copy-start.1 = (f32[192,256]{1,0:T(8,128)S(1)}, f32[192,256]{1,0:T(8,128)}, u32[]{:S(2)}) copy-start(f32[192,256]{1,0:T(8,128)} %get-tuple-element.31.share_ref) | copy-start | bytes 589828
  184.4 99.3 %all-to-all-start.2 = ((bf16[128,48,128]{2,1,0:T(8,128)(2,1)}), bf16[128,48,128]{2,1,0:T(8,128)(2,1)S(1)}, u32[]{:S(2)}, u32[]{:S(2)}) async-start(bf16[128,48,128]{2,1,0:T(8,128)(2,1)} %moments.1), calls=%async_computation.2 | async-start | bytes 3145728 | tf_op jit(solution)/shard_map/all_to_all | solution.py:328
  193.0 90.8 %copy-start = (s32[128]{0:T(128)S(1)}, s32[128]{0:T(128)}, u32[]{:S(2)}) copy-start(s32[128]{0:T(128)} %partner_ref.1) | copy-start | bytes 1540
  193.0 80.1 %reduce-scatter.2.cloned.1.call-start = ((), (), s32[]{:S(2)}) async-start(), calls=%async_computation.7 | async-start | bytes 884736 | tf_op jit(solution)/shard_map/reduce_scatter | solution.py:326
Sparse Core Ops, SparseCore 0:
  10.1 61.9 all-gather.1
  197.2 75.8 reduce-scatter.1

commit v5 on v4

--- a/solution.py
+++ b/solution.py
@@ -84,8 +84,7 @@
 
 def select_kernel(plane_ref, gathered_ref, out_ref, share_ref):
     total = gathered_ref.shape[0]
-    targets, quarters, per_target, _ = out_ref.shape
-    quarter = out_ref.shape[3] // 2
+    targets, quarters, per_target, quarter = out_ref.shape
     width = quarters * quarter
     top = 8
     rows = targets * per_target
@@ -112,49 +111,59 @@
         share = jnp.where(match, weight, share)
     share_ref[...] = share
     picked_t = jnp.transpose(picked).astype(BF16)
-    shares_t = split3(jnp.transpose(share))
     for q in range(quarters):
-        at = q * quarter
-        sent = jnp.dot(
-            picked_t, gathered_ref[:, at : at + quarter], preferred_element_type=F32
-        ).astype(BF16)
-        out_ref[:, q, :, :quarter] = sent.reshape(targets, per_target, quarter)
-        cot = gathered_ref[:, width + at : width + at + quarter]
+        tok = gathered_ref[:, q * quarter : (q + 1) * quarter]
+        sent = jnp.dot(picked_t, tok, preferred_element_type=F32).astype(BF16)
+        out_ref[:, q] = sent.reshape(targets, per_target, quarter)
+
+
+def scale_kernel(share_ref, gathered_ref, out_ref):
+    targets, quarters, per_target, quarter = out_ref.shape
+    width = quarters * quarter
+    shares_t = split3(jnp.transpose(share_ref[...]))
+    for q in range(quarters):
+        cot = gathered_ref[:, width + q * quarter : width + (q + 1) * quarter]
         grads = sum(jnp.dot(part, cot, preferred_element_type=F32) for part in shares_t)
-        out_ref[:, q, :, quarter:] = grads.astype(BF16).reshape(targets, per_target, quarter)
-
-
-def forward_kernel(me_ref, rows_ref, *refs):
-    sources, out_ref, ups, downs, sems = refs[:8], refs[8], refs[9], refs[10], refs[11]
-    copies = fetch(
-        [(sources[j + 4 * kind], held.at[j]) for j in range(4) for kind, held in ((0, ups), (1, downs))],
-        sems,
-    )
-    targets, _, per_target, double = rows_ref.shape
-    quarter = double // 2
+        out_ref[:, q] = grads.astype(BF16).reshape(targets, per_target, quarter)
+
+
+def hidden_kernel(me_ref, rows_ref, *refs):
+    sources, hidden_ref, slope_ref, ups, sems = refs[:4], refs[4], refs[5], refs[6], refs[7]
+    copies = fetch([(sources[j], ups.at[j]) for j in range(4)], sems)
+    targets, _, per_target, quarter = rows_ref.shape
     count = targets * per_target
-    hidden_count = ups.shape[2]
     me = me_ref[0]
-    preact = jnp.zeros((count, hidden_count), F32)
-    back = jnp.zeros((count, hidden_count), F32)
-    for j in range(4):
-        both = rows_ref[:, me ^ j].reshape(count, double)
-        copies[2 * j].wait()
-        preact = preact + jnp.dot(both[:, :quarter], ups[j], preferred_element_type=F32)
-        copies[2 * j + 1].wait()
+    preact = jnp.zeros((count, ups.shape[2]), F32)
+    for j in range(4):
+        part = rows_ref[:, me ^ j].reshape(count, quarter)
+        copies[j].wait()
+        preact = preact + jnp.dot(part, ups[j], preferred_element_type=F32)
+    sigmoid = 1.0 / (1.0 + jnp.exp(-preact))
+    hidden_ref[...] = (preact * sigmoid).astype(BF16)
+    slope_ref[...] = sigmoid * (1.0 + preact * (1.0 - sigmoid))
+
+
+def back_kernel(me_ref, rows_ref, slope_ref, *refs):
+    sources, out_ref, downs, sems = refs[:4], refs[4], refs[5], refs[6]
+    copies = fetch([(sources[j], downs.at[j]) for j in range(4)], sems)
+    targets, _, per_target, quarter = rows_ref.shape
+    count = targets * per_target
+    me = me_ref[0]
+    back = jnp.zeros(slope_ref.shape, F32)
+    for j in range(4):
+        part = rows_ref[:, me ^ j].reshape(count, quarter)
+        copies[j].wait()
         back = back + lax.dot_general(
-            both[:, quarter:], downs[j], (((1,), (1,)), ((), ())), preferred_element_type=F32
+            part, downs[j], (((1,), (1,)), ((), ())), preferred_element_type=F32
         )
-    sigmoid = 1.0 / (1.0 + jnp.exp(-preact))
-    out_ref[:, :hidden_count] = (preact * sigmoid).astype(BF16)
-    out_ref[:, hidden_count:] = (back * sigmoid * (1.0 + preact * (1.0 - sigmoid))).astype(BF16)
-
-
-def expert_out_kernel(me_ref, acts_ref, *refs):
+    out_ref[...] = (back * slope_ref[...]).astype(BF16)
+
+
+def expert_out_kernel(me_ref, hidden_ref, *refs):
     sources, out_ref, downs, sems = refs[:4], refs[4], refs[5], refs[6]
     copies = fetch([(sources[j], downs.at[j]) for j in range(4)], sems)
     targets, _, per_target, quarter = out_ref.shape
-    hidden = acts_ref[:, : downs.shape[1]]
+    hidden = hidden_ref[...]
     me = me_ref[0]
     for j in range(4):
         copies[j].wait()
@@ -172,25 +181,25 @@
 
 
 def moment_kernel(
-    me_ref, rows_ref, a0, a1, a2, a3, up_hbm, down_hbm, out_ref, up_ref, down_ref, sems
+    me_ref, rows_ref, h0, h1, h2, h3, g0, g1, g2, g3, up_hbm, down_hbm, out_ref, up_ref, down_ref, sems
 ):
     copies = fetch([(up_hbm, up_ref), (down_hbm, down_ref)], sems)
-    acts = (a0, a1, a2, a3)
+    hiddens, pre_grads = (h0, h1, h2, h3), (g0, g1, g2, g3)
     me = me_ref[0]
     features, hidden_count = up_ref.shape
     over_rows = (((0,), (0,)), ((), ()))
     up_grad = jnp.zeros((features, hidden_count), F32)
     down_grad = jnp.zeros((hidden_count, features), F32)
     for j in range(4):
-        rows = rows_ref[me ^ j].reshape(acts[j].shape[0], 2 * features)
+        rows = rows_ref[me ^ j].reshape(hiddens[j].shape[0], 2 * features)
         up_grad = up_grad + lax.dot_general(
             rows[:, :features],
-            acts[j][:, hidden_count:],
+            pre_grads[j][...],
             over_rows,
             preferred_element_type=F32,
         )
         down_grad = down_grad + lax.dot_general(
-            acts[j][:, :hidden_count],
+            hiddens[j][...],
             rows[:, features:],
             over_rows,
             preferred_element_type=F32,
@@ -262,35 +271,33 @@
     )
     ups, downs = (up0, up1, up2, up3), (down0, down1, down2, down3)
 
-    outgoing, share = call(
+    tokens_out, share = call(
         select_kernel,
         "select",
-        (shape_of((16, 4, 16, 1024)), shape_of((192, 256), F32)),
+        (shape_of((16, 4, 16, 512)), shape_of((192, 256), F32)),
         [SMEM, VMEM],
-        10**9,
-        4 * 10**6,
+        3 * 10**8,
+        3 * 10**6,
     )(plane, gathered)
-    rows = lax.all_to_all(outgoing, GROUP_AXES, split_axis=0, concat_axis=0, tiled=True)
-    by_feature = lax.all_to_all(
-        rows.transpose(1, 0, 2, 3), DP_AXES, split_axis=0, concat_axis=0, tiled=True
-    )
-
-    acts = call(
-        forward_kernel,
-        "forward",
-        shape_of((256, 1536)),
-        [SMEM, VMEM] + [HBM] * 8,
-        16 * 10**8,
-        9 * 10**6,
-        (
-            pltpu.VMEM((4, 512, 768), BF16),
-            pltpu.VMEM((4, 768, 512), BF16),
-            pltpu.SemaphoreType.DMA((8,)),
-        ),
-    )(me, rows, *ups, *downs)
-    acts2 = lax.ppermute(acts, "yl", FLIP)
-    acts1 = lax.ppermute(acts, "core", FLIP)
-
+    grads_out = call(
+        scale_kernel, "scale", shape_of((16, 4, 16, 512)), [VMEM, VMEM], 7 * 10**8, 3 * 10**6
+    )(share, gathered)
+    token_rows = lax.all_to_all(tokens_out, GROUP_AXES, split_axis=0, concat_axis=0, tiled=True)
+    grads_out, token_rows = lax.optimization_barrier((grads_out, token_rows))
+    grad_rows = lax.all_to_all(grads_out, GROUP_AXES, split_axis=0, concat_axis=0, tiled=True)
+
+    down_scratch = (pltpu.VMEM((4, 768, 512), BF16), pltpu.SemaphoreType.DMA((4,)))
+    hidden, slope = call(
+        hidden_kernel,
+        "hidden",
+        (shape_of((256, 768)), shape_of((256, 768), F32)),
+        [SMEM, VMEM] + [HBM] * 4,
+        8 * 10**8,
+        5 * 10**6,
+        (pltpu.VMEM((4, 512, 768), BF16), pltpu.SemaphoreType.DMA((4,))),
+    )(me, token_rows, *ups)
+    hidden2 = lax.ppermute(hidden, "yl", FLIP)
+    hidden1 = lax.ppermute(hidden, "core", FLIP)
     expert_out = call(
         expert_out_kernel,
         "expert_out",
@@ -298,22 +305,43 @@
         [SMEM, VMEM] + [HBM] * 4,
         8 * 10**8,
         5 * 10**6,
-        (pltpu.VMEM((4, 768, 512), BF16), pltpu.SemaphoreType.DMA((4,))),
-    )(me, acts, *downs)
-
-    by_feature, acts1, acts2, expert_out = lax.optimization_barrier(
-        (by_feature, acts1, acts2, expert_out)
-    )
-    acts3 = lax.ppermute(acts2, "core", FLIP)
+        down_scratch,
+    )(me, hidden, *downs)
+
+    grad_rows, hidden1, hidden2, expert_out = lax.optimization_barrier(
+        (grad_rows, hidden1, hidden2, expert_out)
+    )
     returned = lax.all_to_all(expert_out, GROUP_AXES, split_axis=0, concat_axis=0, tiled=True)
+    pre_grad = call(
+        back_kernel,
+        "back",
+        shape_of((256, 768)),
+        [SMEM, VMEM, VMEM] + [HBM] * 4,
+        8 * 10**8,
+        5 * 10**6,
+        down_scratch,
+    )(me, grad_rows, slope, *downs)
+    pre_grad2 = lax.ppermute(pre_grad, "yl", FLIP)
+    pre_grad1 = lax.ppermute(pre_grad, "core", FLIP)
+    both = jnp.concatenate([token_rows, grad_rows], axis=-1).transpose(1, 0, 2, 3)
+
+    both, returned, pre_grad1, pre_grad2 = lax.optimization_barrier(
+        (both, returned, pre_grad1, pre_grad2)
+    )
+    by_feature = lax.all_to_all(both, DP_AXES, split_axis=0, concat_axis=0, tiled=True)
+    hidden3 = lax.ppermute(hidden2, "core", FLIP)
+    pre_grad3 = lax.ppermute(pre_grad2, "core", FLIP)
     partial = call(
         combine_kernel, "combine", shape_of((192, 2048)), [VMEM, VMEM], 6 * 10**8, 2 * 10**6, (), 12
     )(share, returned)
+    by_feature, _ = lax.optimization_barrier((by_feature, partial))
+    layer_out = lax.psum_scatter(partial, "zh", scatter_dimension=0, tiled=True)
+
     pieces = call(
         moment_kernel,
         "moments",
         shape_of((128, 48, 128)),
-        [SMEM] + [VMEM] * 5 + [HBM] * 2,
+        [SMEM] + [VMEM] * 9 + [HBM] * 2,
         32 * 10**8,
         9 * 10**6,
         (
@@ -321,12 +349,22 @@
             pltpu.VMEM((768, 512), BF16),
             pltpu.SemaphoreType.DMA((2,)),
         ),
-    )(me, by_feature, acts, acts1, acts2, acts3, up_moment[0], down_moment[0])
-
-    layer_out = lax.psum_scatter(partial, "zh", scatter_dimension=0, tiled=True)
-
+    )(
+        me,
+        by_feature,
+        hidden,
+        hidden1,
+        hidden2,
+        hidden3,
+        pre_grad,
+        pre_grad1,
+        pre_grad2,
+        pre_grad3,
+        up_moment[0],
+        down_moment[0],
+    )
+    pieces, layer_out = lax.optimization_barrier((pieces, layer_out))
     spread = lax.all_to_all(pieces, SLOT_AXES, split_axis=0, concat_axis=0, tiled=True)
-    spread, layer_out = lax.optimization_barrier((spread, layer_out))
     chosen = call(
         pick_kernel, "pick", shape_of((128, 48, 128)), [SMEM, VMEM], 0, 3 * 10**6, (), 12
     )(partner, spread)

time: 384 us -> 394 us (1.026)
  waiting for transfers between devices: 143 us -> 82.2 us
  blocking collectives: 118 us -> 172 us
  starting transfers between devices: 68.4 us -> 81.3 us
  Pallas kernels: 28.6 us -> 33.7 us
    reduce_scatter x1, waiting for transfers between devices: 78.3 us -> 15.5 us  [body(): layer_out = lax.psum_scatter(partial, 'zh', scatter_dimension=0, tiled=True)]
    all_to_all x1, blocking collectives: 33.7 us -> 88 us  [body(): lax.all_to_all(pieces, SLOT_AXES, split_axis=0, concat_axis=0, tiled=True)]
    all_to_all x2 -> x3, waiting for transfers between devices: 10.6 us -> 31.6 us  [the longest x1 18.9 us: body(): lax.all_to_all(both, DP_AXES, split_axis=0, concat_axis=0, tiled=True)]
    ppermute x3 -> x6, waiting for transfers between devices: 25.9 us -> 11 us  [the longest x1 7.35 us: body(): pre_grad2 = lax.ppermute(pre_grad, 'yl', FLIP)]
    ppermute x3 -> x6, starting transfers between devices: 8.63 us -> 17.3 us  [the longest x1 5.31 us: body(): hidden1 = lax.ppermute(hidden, 'core', FLIP)]
    all_to_all x1, waiting for transfers between devices: 5.89 us -> 0.01 us  [body(): lax.all_to_all(expert_out, GROUP_AXES, split_axis=0, concat_axis=0, tiled...]
    pallas_call x2 -> x4, Pallas kernels: 11.9 us -> 17.1 us  [the longest x1 5.11 us: body(): call(hidden_kernel, 'hidden', (shape_of((256, 768)), shape_of((256, 768),...]
    all_to_all x1, starting transfers between devices: 3.65 us -> 8.21 us  [body(): lax.all_to_all(expert_out, GROUP_AXES, split_axis=0, concat_axis=0, tiled...]
  transfers between devices with their start and end apart: 14 -> 18, of which waited for: 9 -> 9; matrix products, arithmetic and copies ran while one was open for 0% -> 1% of each run, Pallas kernels for 5% -> 7%
where the time goes in v5:
time: 394 us; the launch traced here: 388 us
  blocking collectives  172 us (44%)
  waiting for transfers between devices  82.2 us (21%)
  starting transfers between devices  81.3 us (21%)
  Pallas kernels  33.7 us (9%)
  between operations  14.3 us (4%)
    all_to_all x1, blocking collectives, body(): lax.all_to_all(pieces, SLOT_AXES, split_axis=0, concat_axis=0, tiled=True)  88 us
    all_to_all x1, blocking collectives, body(): lax.all_to_all(chosen, SLOT_AXES, split_axis=0, concat_axis=0, tiled=True)  83.7 us
    all_gather x1, waiting for transfers between devices, body(): gathered = lax.all_gather(packed, 'zh', axis=0, tiled=True)  20 us
    all_to_all x1, waiting for transfers between devices, body(): lax.all_to_all(both, DP_AXES, split_axis=0, concat_axis=0, tiled=True)  18.9 us
    reduce_scatter x1, waiting for transfers between devices, body(): layer_out = lax.psum_scatter(partial, 'zh', scatter_dimension=0, tiled=True)  15.5 us
    ppermute x1, starting transfers between devices, body(): lax.ppermute(up2, 'core', FLIP)  14.7 us
    all_to_all x1, waiting for transfers between devices, body(): lax.all_to_all(tokens_out, GROUP_AXES, split_axis=0, concat_axis=0, tiled...  12.7 us
    ppermute x1, starting transfers between devices, body(): lax.ppermute(up0, 'core', FLIP)  8.68 us
  transfers between devices with their start and end apart: 18, of which 9 were waited for; matrix products, arithmetic and copies ran while one was open for 1% of the time, Pallas kernels for 7%

profile of v5, /device:TPU:1, one launch (start us, length us, event | category | flops | bytes accessed | tf_op | source)
XLA Modules:
  0.0 388.2 jit_solution(1153006547352534106)
XLA Ops:
  7.2 2.1 pack.1
  9.3 4.0 %collective-permute-start.1 = (bf16[512,768]{1,0:T(8,128)(2,1)}, bf16[512,768]{1,0:T(8,128)(2,1)S(1)}, u32[]{:S(2)}, u32[]{:S(2)}) collective-permute-start(bf16[512,768]{1,0:T(8,128)(2,1)} %bitcast.17), channel_id=1, source_target_pairs={{0,2},{2,0},{1,3},{3,1},{4,6},{6,4},{5,7},{7,5},{8,10},{10,8},{9,1... | collective-permute-start | bytes 2359304 | tf_op jit(solution)/shard_map/ppermute | solution.py:266
  13.4 1.9 collective-permute-start.4
  15.3 8.7 %collective-permute-start = (bf16[512,768]{1,0:T(8,128)(2,1)}, bf16[512,768]{1,0:T(8,128)(2,1)}, u32[]{:S(2)}, u32[]{:S(2)}) collective-permute-start(bf16[512,768]{1,0:T(8,128)(2,1)} %bitcast.18), channel_id=1, source_target_pairs={{0,1},{1,0},{2,3},{3,2},{4,5},{5,4},{6,7},{7,6},{8,9},{9,8},{10,11... | collective-permute-start | bytes 2359304 | tf_op jit(solution)/shard_map/ppermute | solution.py:267
  24.0 1.9 collective-permute-start.3
  26.0 14.7 %collective-permute-start.2 = (bf16[512,768]{1,0:T(8,128)(2,1)S(1)}, bf16[512,768]{1,0:T(8,128)(2,1)}, u32[]{:S(2)}, u32[]{:S(2)}) collective-permute-start(bf16[512,768]{1,0:T(8,128)(2,1)S(1)} %collective-permute-done.1.refs_2_), channel_id=1, source_target_pairs={{0,1},{1,0},{2,3},{3,2},{4,5},{5,4},{6,7},{7,6},{8,9},{9,8},{10,11... | collective-permute-start | bytes 2359304 | tf_op jit(solution)/shard_map/ppermute | solution.py:268
  40.7 2.2 collective-permute-done.4.refs_2_
  42.9 7.9 %collective-permute-start.5 = (bf16[768,512]{1,0:T(8,128)(2,1)S(1)}, bf16[768,512]{1,0:T(8,128)(2,1)S(1)}, u32[]{:S(2)}, u32[]{:S(2)}) collective-permute-start(bf16[768,512]{1,0:T(8,128)(2,1)S(1)} %collective-permute-done.4.refs_2_), channel_id=1, source_target_pairs={{0,1},{1,0},{2,3},{3,2},{4,5},{5,4},{6,7},{7,6},{8,9},{9,8},{10,11... | collective-permute-start | bytes 2359304 | tf_op jit(solution)/shard_map/ppermute | solution.py:268
  52.7 20.0 %all-gather.2.cloned.1.call-done.gathered_ref = bf16[192,4224]{1,0:T(8,128)(2,1)} async-done(((bf16[24,4224]{1,0:T(8,128)(2,1)}), bf16[192,4224]{1,0:T(8,128)(2,1)}) %all-gather.2.cloned.1.call-update) | async-done | bytes 1622032 | tf_op jit(solution)/shard_map/all_gather | solution.py:263
  72.7 3.4 select.1
  76.1 6.9 %all-to-all-start = ((bf16[16,4,16,512]{3,2,1,0:T(8,128)(2,1)}), bf16[16,4,16,512]{3,2,1,0:T(8,128)(2,1)S(1)}, u32[]{:S(2)}, u32[]{:S(2)}) async-start(bf16[16,4,16,512]{3,2,1,0:T(8,128)(2,1)} %get-tuple-element.31), calls=%async_computation | async-start | bytes 2097152 | tf_op jit(solution)/shard_map/all_to_all | solution.py:285
  83.0 3.6 scale.1
  86.6 12.7 %all-to-all-done.rows_ref = bf16[16,4,16,512]{3,2,1,0:T(8,128)(2,1)S(1)} async-done(((bf16[16,4,16,512]{3,2,1,0:T(8,128)(2,1)}), bf16[16,4,16,512]{3,2,1,0:T(8,128)(2,1)S(1)}, u32[]{:S(2)}, u32[]{:S(2)}) %all-to-all-start) | async-done | bytes 1048608 | tf_op jit(solution)/shard_map/all_to_all | solution.py:285
  99.3 4.3 %all-to-all-start.1 = ((bf16[16,4,16,512]{3,2,1,0:T(8,128)(2,1)}), bf16[16,4,16,512]{3,2,1,0:T(8,128)(2,1)}, u32[]{:S(2)}, u32[]{:S(2)}) async-start(bf16[16,4,16,512]{3,2,1,0:T(8,128)(2,1)} %scale.1), calls=%async_computation.1 | async-start | bytes 2097152 | tf_op jit(solution)/shard_map/all_to_all | solution.py:287
  103.6 5.1 %hidden.1 = (bf16[256,768]{1,0:T(8,128)(2,1)}, f32[256,768]{1,0:T(8,128)}) custom-call(s32[1]{0:T(128)} %bitcast.me_ref, bf16[16,4,16,512]{3,2,1,0:T(8,128)(2,1)} %copy-done.2, bf16[512,768]{1,0:T(8,128)(2,1)} %bitcast.19, bf16[512,768]{1,0:T(8,128)(2,1)} %collective-permute-done.refs_1_, bf16[512,768]{1,0:T(8,128)(2,1)} %copy-done.6, ...), custom_call_target="tpu_custom_call" | custom-call | flops 800000000 | bytes 5000000 | tf_op jit(solution)/shard_map/hidden/pallas_call | solution.py:290
  110.7 5.3 %collective-permute-start.6 = (bf16[256,768]{1,0:T(8,128)(2,1)}, bf16[256,768]{1,0:T(8,128)(2,1)S(1)}, u32[]{:S(2)}, u32[]{:S(2)}) collective-permute-start(bf16[256,768]{1,0:T(8,128)(2,1)} %get-tuple-element.37.hidden_ref.h0), channel_id=1, source_target_pairs={{0,1},{1,0},{2,3},{3,2},{4,5},{5,4},{6,7},{7,6},{8,9},{9,8},{10,11... | collective-permute-start | bytes 1179656 | tf_op jit(solution)/shard_map/ppermute | solution.py:300
  116.0 4.7 %expert_out.1 = bf16[16,4,16,512]{3,2,1,0:T(8,128)(2,1)} custom-call(s32[1]{0:T(128)} %bitcast.me_ref, bf16[256,768]{1,0:T(8,128)(2,1)} %get-tuple-element.37.hidden_ref.h0, bf16[768,512]{1,0:T(8,128)(2,1)} %bitcast.15, bf16[768,512]{1,0:T(8,128)(2,1)} %copy-done.4, bf16[768,512]{1,0:T(8,128)(2,1)} %copy-done.3, bf16[768,512]{1,0:T(8,128)(2,1)} %copy-done.5), custom_call_target="tpu_custom_call" | custom-call | flops 800000000 | bytes 5000000 | tf_op jit(solution)/shard_map/expert_out/pallas_call | solution.py:301
  120.7 3.6 collective-permute-done.7.h2
  124.3 8.2 %all-to-all-start.2 = ((bf16[16,4,16,512]{3,2,1,0:T(8,128)(2,1)}), bf16[16,4,16,512]{3,2,1,0:T(8,128)(2,1)S(1)}, u32[]{:S(2)}, u32[]{:S(2)}) async-start(bf16[16,4,16,512]{3,2,1,0:T(8,128)(2,1)} %expert_out.1), calls=%async_computation.2 | async-start | bytes 2097152 | tf_op jit(solution)/shard_map/all_to_all | solution.py:314
  132.5 5.1 %back.1.g0 = bf16[256,768]{1,0:T(8,128)(2,1)} custom-call(s32[1]{0:T(128)} %bitcast.me_ref, bf16[16,4,16,512]{3,2,1,0:T(8,128)(2,1)} %all-to-all-done.1.rows_ref, f32[256,768]{1,0:T(8,128)} %get-tuple-element.43.slope_ref, bf16[768,512]{1,0:T(8,128)(2,1)} %bitcast.16, bf16[768,512]{1,0:T(8,128)(2,1)} %copy-done.4, bf16[768,512]{1,0:T(8,128)(2,1)} %copy-done.3, ...), custom_call_target="tpu_custom_call" | custom-call | flops 800000000 | bytes 5000000 | tf_op jit(solution)/shard_map/back/pallas_call | solution.py:315
  137.6 2.4 collective-permute-start.9
  140.0 3.3 collective-permute-start.8
  143.3 3.2 copy_bitcast_fusion
  146.5 7.4 %collective-permute-done.9.g2 = bf16[256,768]{1,0:T(8,128)(2,1)S(1)} collective-permute-done((bf16[256,768]{1,0:T(8,128)(2,1)}, bf16[256,768]{1,0:T(8,128)(2,1)S(1)}, u32[]{:S(2)}, u32[]{:S(2)}) %collective-permute-start.9) | collective-permute-done | bytes 393248 | tf_op jit(solution)/shard_map/ppermute | solution.py:324
  154.7 5.4 %all-to-all-start.3 = ((bf16[4,16,16,1024]{3,2,1,0:T(8,128)(2,1)}), bf16[4,16,16,1024]{3,2,1,0:T(8,128)(2,1)}, u32[]{:S(2)}, u32[]{:S(2)}) async-start(bf16[4,16,16,1024]{3,2,1,0:T(8,128)(2,1)} %copy_bitcast_fusion), calls=%async_computation.3 | async-start | bytes 4194304 | tf_op jit(solution)/shard_map/all_to_all | solution.py:331
  161.8 2.0 collective-permute-start.10
  163.8 2.3 collective-permute-start.11
  166.1 18.9 %all-to-all-done.3.rows_ref = bf16[4,16,16,1024]{3,2,1,0:T(8,128)(2,1)} async-done(((bf16[4,16,16,1024]{3,2,1,0:T(8,128)(2,1)}), bf16[4,16,16,1024]{3,2,1,0:T(8,128)(2,1)}, u32[]{:S(2)}, u32[]{:S(2)}) %all-to-all-start.3) | async-done | bytes 2097184 | tf_op jit(solution)/shard_map/all_to_all | solution.py:331
  185.9 6.0 %moments.1 = bf16[128,48,128]{2,1,0:T(8,128)(2,1)} custom-call(s32[1]{0:T(128)} %bitcast.me_ref, bf16[4,16,16,1024]{3,2,1,0:T(8,128)(2,1)} %all-to-all-done.3.rows_ref, bf16[256,768]{1,0:T(8,128)(2,1)} %get-tuple-element.37.hidden_ref.h0, bf16[256,768]{1,0:T(8,128)(2,1)} %copy-done.8, bf16[256,768]{1,0:T(8,128)(2,1)} %copy-done.7, ...), custom_call_target="tpu_custom_call" | custom-call | flops 3200000000 | bytes 9000000 | tf_op jit(solution)/shard_map/moments/pallas_call | solution.py:340
  191.9 15.5 %reduce-scatter.2.cloned.1.call-done = bf16[24,2048]{1,0:T(8,128)(2,1)} async-done(((bf16[192,2048]{1,0:T(8,128)(2,1)}), bf16[24,2048]{1,0:T(8,128)(2,1)}) %reduce-scatter.2.cloned.1.call-update) | async-done | bytes 98320 | tf_op jit(solution)/shard_map/reduce_scatter | solution.py:338
  207.5 88.0 %all_to_all.30.spread_ref = bf16[128,48,128]{2,1,0:T(8,128)(2,1)S(1)} all-to-all(bf16[128,48,128]{2,1,0:T(8,128)(2,1)} %moments.1), channel_id=1, replica_groups=mesh['yh'=2,'zh'=8,'zp'=2,'x'=4,'yl'=2,'core'=2] {'yh','zh','zp','x'}, dimensions={0} | all-to-all | bytes 3145728 | tf_op jit(solution)/shard_map/all_to_all | solution.py:367
  296.3 83.7 %all_to_all.31.pieces_ref = bf16[128,48,128]{2,1,0:T(8,128)(2,1)S(1)} all-to-all(bf16[128,48,128]{2,1,0:T(8,128)(2,1)S(1)} %pick.1), channel_id=1, replica_groups=mesh['yh'=2,'zh'=8,'zp'=2,'x'=4,'yl'=2,'core'=2] {'yh','zh','zp','x'}, dimensions={0} | all-to-all | bytes 3145728 | tf_op jit(solution)/shard_map/all_to_all | solution.py:371
  (45 shorter events, 9.5 us)
Async XLA Ops:
  7.2 65.5 %all-gather.2.cloned.1.call-start = ((), (), s32[]{:S(2)}) async-start(), calls=%async_computation.7 | async-start | bytes 1824768 | tf_op jit(solution)/shard_map/all_gather | solution.py:263
  9.3 16.7 %collective-permute-start.1 = (bf16[512,768]{1,0:T(8,128)(2,1)}, bf16[512,768]{1,0:T(8,128)(2,1)S(1)}, u32[]{:S(2)}, u32[]{:S(2)}) collective-permute-start(bf16[512,768]{1,0:T(8,128)(2,1)} %bitcast.17), channel_id=1, source_target_pairs={{0,2},{2,0},{1,3},{3,1},{4,6},{6,4},{5,7},{7,5},{8,10},{10,8},{9,1... | collective-permute-start | bytes 2359304 | tf_op jit(solution)/shard_map/ppermute | solution.py:266
  13.4 29.5 %collective-permute-start.4 = (bf16[768,512]{1,0:T(8,128)(2,1)}, bf16[768,512]{1,0:T(8,128)(2,1)S(1)}, u32[]{:S(2)}, u32[]{:S(2)}) collective-permute-start(bf16[768,512]{1,0:T(8,128)(2,1)} %bitcast.13), channel_id=1, source_target_pairs={{0,2},{2,0},{1,3},{3,1},{4,6},{6,4},{5,7},{7,5},{8,10},{10,8},{9,1... | collective-permute-start | bytes 2359304 | tf_op jit(solution)/shard_map/ppermute | solution.py:266
  15.3 35.5 %collective-permute-start = (bf16[512,768]{1,0:T(8,128)(2,1)}, bf16[512,768]{1,0:T(8,128)(2,1)}, u32[]{:S(2)}, u32[]{:S(2)}) collective-permute-start(bf16[512,768]{1,0:T(8,128)(2,1)} %bitcast.18), channel_id=1, source_target_pairs={{0,1},{1,0},{2,3},{3,2},{4,5},{5,4},{6,7},{7,6},{8,9},{9,8},{10,11... | collective-permute-start | bytes 2359304 | tf_op jit(solution)/shard_map/ppermute | solution.py:267
  24.0 26.9 %collective-permute-start.3 = (bf16[768,512]{1,0:T(8,128)(2,1)}, bf16[768,512]{1,0:T(8,128)(2,1)S(1)}, u32[]{:S(2)}, u32[]{:S(2)}) collective-permute-start(bf16[768,512]{1,0:T(8,128)(2,1)} %bitcast.14), channel_id=1, source_target_pairs={{0,1},{1,0},{2,3},{3,2},{4,5},{5,4},{6,7},{7,6},{8,9},{9,8},{10,11... | collective-permute-start | bytes 2359304 | tf_op jit(solution)/shard_map/ppermute | solution.py:267
  26.0 50.1 %copy-start.6 = (bf16[512,768]{1,0:T(8,128)(2,1)}, bf16[512,768]{1,0:T(8,128)(2,1)S(1)}, u32[]{:S(2)}) copy-start(bf16[512,768]{1,0:T(8,128)(2,1)S(1)} %collective-permute-done.1.refs_2_) | copy-start | bytes 2359300
  26.0 24.8 %collective-permute-start.2 = (bf16[512,768]{1,0:T(8,128)(2,1)S(1)}, bf16[512,768]{1,0:T(8,128)(2,1)}, u32[]{:S(2)}, u32[]{:S(2)}) collective-permute-start(bf16[512,768]{1,0:T(8,128)(2,1)S(1)} %collective-permute-done.1.refs_2_), channel_id=1, source_target_pairs={{0,1},{1,0},{2,3},{3,2},{4,5},{5,4},{6,7},{7,6},{8,9},{9,8},{10,11... | collective-permute-start | bytes 2359304 | tf_op jit(solution)/shard_map/ppermute | solution.py:268
  42.9 43.7 %copy-start.3 = (bf16[768,512]{1,0:T(8,128)(2,1)}, bf16[768,512]{1,0:T(8,128)(2,1)S(1)}, u32[]{:S(2)}) copy-start(bf16[768,512]{1,0:T(8,128)(2,1)S(1)} %collective-permute-done.4.refs_2_) | copy-start | bytes 2359300
  42.9 9.8 %collective-permute-start.5 = (bf16[768,512]{1,0:T(8,128)(2,1)S(1)}, bf16[768,512]{1,0:T(8,128)(2,1)S(1)}, u32[]{:S(2)}, u32[]{:S(2)}) collective-permute-start(bf16[768,512]{1,0:T(8,128)(2,1)S(1)} %collective-permute-done.4.refs_2_), channel_id=1, source_target_pairs={{0,1},{1,0},{2,3},{3,2},{4,5},{5,4},{6,7},{7,6},{8,9},{9,8},{10,11... | collective-permute-start | bytes 2359304 | tf_op jit(solution)/shard_map/ppermute | solution.py:268
  50.9 1.9 copy-start.4
  52.7 20.0 %copy-start.5 = (bf16[768,512]{1,0:T(8,128)(2,1)}, bf16[768,512]{1,0:T(8,128)(2,1)S(1)}, u32[]{:S(2)}) copy-start(bf16[768,512]{1,0:T(8,128)(2,1)S(1)} %collective-permute-done.5.refs_3_) | copy-start | bytes 2359300
  76.1 23.1 %all-to-all-start = ((bf16[16,4,16,512]{3,2,1,0:T(8,128)(2,1)}), bf16[16,4,16,512]{3,2,1,0:T(8,128)(2,1)S(1)}, u32[]{:S(2)}, u32[]{:S(2)}) async-start(bf16[16,4,16,512]{3,2,1,0:T(8,128)(2,1)} %get-tuple-element.31), calls=%async_computation | async-start | bytes 2097152 | tf_op jit(solution)/shard_map/all_to_all | solution.py:285
  99.3 4.4 %copy-start.2 = (bf16[16,4,16,512]{3,2,1,0:T(8,128)(2,1)}, bf16[16,4,16,512]{3,2,1,0:T(8,128)(2,1)S(1)}, u32[]{:S(2)}) copy-start(bf16[16,4,16,512]{3,2,1,0:T(8,128)(2,1)S(1)} %all-to-all-done.rows_ref) | copy-start | bytes 3145732
  99.3 25.0 %all-to-all-start.1 = ((bf16[16,4,16,512]{3,2,1,0:T(8,128)(2,1)}), bf16[16,4,16,512]{3,2,1,0:T(8,128)(2,1)}, u32[]{:S(2)}, u32[]{:S(2)}) async-start(bf16[16,4,16,512]{3,2,1,0:T(8,128)(2,1)} %scale.1), calls=%async_computation.1 | async-start | bytes 2097152 | tf_op jit(solution)/shard_map/all_to_all | solution.py:287
  108.8 15.5 %collective-permute-start.7 = (bf16[256,768]{1,0:T(8,128)(2,1)}, bf16[256,768]{1,0:T(8,128)(2,1)S(1)}, u32[]{:S(2)}, u32[]{:S(2)}) collective-permute-start(bf16[256,768]{1,0:T(8,128)(2,1)} %get-tuple-element.37.hidden_ref.h0), channel_id=1, source_target_pairs={{0,2},{2,0},{1,3},{3,1},{4,6},{6,4},{5,7},{7,5},{8,10},{10,8},{9,1... | collective-permute-start | bytes 1179656 | tf_op jit(solution)/shard_map/ppermute | solution.py:299
  110.7 13.6 %collective-permute-start.6 = (bf16[256,768]{1,0:T(8,128)(2,1)}, bf16[256,768]{1,0:T(8,128)(2,1)S(1)}, u32[]{:S(2)}, u32[]{:S(2)}) collective-permute-start(bf16[256,768]{1,0:T(8,128)(2,1)} %get-tuple-element.37.hidden_ref.h0), channel_id=1, source_target_pairs={{0,1},{1,0},{2,3},{3,2},{4,5},{5,4},{6,7},{7,6},{8,9},{9,8},{10,11... | collective-permute-start | bytes 1179656 | tf_op jit(solution)/shard_map/ppermute | solution.py:300
  124.3 37.5 %copy-start.7 = (bf16[256,768]{1,0:T(8,128)(2,1)}, bf16[256,768]{1,0:T(8,128)(2,1)S(1)}, u32[]{:S(2)}) copy-start(bf16[256,768]{1,0:T(8,128)(2,1)S(1)} %collective-permute-done.7.h2) | copy-start | bytes 1179652
  124.3 13.3 %copy-start.8 = (bf16[256,768]{1,0:T(8,128)(2,1)}, bf16[256,768]{1,0:T(8,128)(2,1)S(1)}, u32[]{:S(2)}) copy-start(bf16[256,768]{1,0:T(8,128)(2,1)S(1)} %collective-permute-done.6.h1) | copy-start | bytes 1179652
  124.3 29.6 %all-to-all-start.2 = ((bf16[16,4,16,512]{3,2,1,0:T(8,128)(2,1)}), bf16[16,4,16,512]{3,2,1,0:T(8,128)(2,1)S(1)}, u32[]{:S(2)}, u32[]{:S(2)}) async-start(bf16[16,4,16,512]{3,2,1,0:T(8,128)(2,1)} %expert_out.1), calls=%async_computation.2 | async-start | bytes 2097152 | tf_op jit(solution)/shard_map/all_to_all | solution.py:314
  137.6 16.3 %collective-permute-start.9 = (bf16[256,768]{1,0:T(8,128)(2,1)}, bf16[256,768]{1,0:T(8,128)(2,1)S(1)}, u32[]{:S(2)}, u32[]{:S(2)}) collective-permute-start(bf16[256,768]{1,0:T(8,128)(2,1)} %back.1.g0), channel_id=1, source_target_pairs={{0,2},{2,0},{1,3},{3,1},{4,6},{6,4},{5,7},{7,5},{8,10},{10,8},{9,1... | collective-permute-start | bytes 1179656 | tf_op jit(solution)/shard_map/ppermute | solution.py:324
  140.0 13.9 %collective-permute-start.8 = (bf16[256,768]{1,0:T(8,128)(2,1)}, bf16[256,768]{1,0:T(8,128)(2,1)S(1)}, u32[]{:S(2)}, u32[]{:S(2)}) collective-permute-start(bf16[256,768]{1,0:T(8,128)(2,1)} %back.1.g0), channel_id=1, source_target_pairs={{0,1},{1,0},{2,3},{3,2},{4,5},{5,4},{6,7},{7,6},{8,9},{9,8},{10,11... | collective-permute-start | bytes 1179656 | tf_op jit(solution)/shard_map/ppermute | solution.py:325
  146.5 13.5 %copy-start = (f32[192,256]{1,0:T(8,128)S(1)}, f32[192,256]{1,0:T(8,128)}, u32[]{:S(2)}) copy-start(f32[192,256]{1,0:T(8,128)} %get-tuple-element.30.share_ref) | copy-start | bytes 589828
  153.9 9.9 %copy-start.9 = (bf16[256,768]{1,0:T(8,128)(2,1)}, bf16[256,768]{1,0:T(8,128)(2,1)S(1)}, u32[]{:S(2)}) copy-start(bf16[256,768]{1,0:T(8,128)(2,1)S(1)} %collective-permute-done.9.g2) | copy-start | bytes 1179652
  153.9 0.8 copy-start.10
  154.7 30.3 %all-to-all-start.3 = ((bf16[4,16,16,1024]{3,2,1,0:T(8,128)(2,1)}), bf16[4,16,16,1024]{3,2,1,0:T(8,128)(2,1)}, u32[]{:S(2)}, u32[]{:S(2)}) async-start(bf16[4,16,16,1024]{3,2,1,0:T(8,128)(2,1)} %copy_bitcast_fusion), calls=%async_computation.3 | async-start | bytes 4194304 | tf_op jit(solution)/shard_map/all_to_all | solution.py:331
  160.1 47.4 %reduce-scatter.2.cloned.1.call-start = ((), (), s32[]{:S(2)}) async-start(), calls=%async_computation.8 | async-start | bytes 884736 | tf_op jit(solution)/shard_map/reduce_scatter | solution.py:338
  161.8 23.2 %collective-permute-start.10 = (bf16[256,768]{1,0:T(8,128)(2,1)S(1)}, bf16[256,768]{1,0:T(8,128)(2,1)S(1)}, u32[]{:S(2)}, u32[]{:S(2)}) collective-permute-start(bf16[256,768]{1,0:T(8,128)(2,1)S(1)} %collective-permute-done.7.h2), channel_id=1, source_target_pairs={{0,1},{1,0},{2,3},{3,2},{4,5},{5,4},{6,7},{7,6},{8,9},{9,8},{10,11... | collective-permute-start | bytes 1179656 | tf_op jit(solution)/shard_map/ppermute | solution.py:332
  163.8 21.2 %collective-permute-start.11 = (bf16[256,768]{1,0:T(8,128)(2,1)S(1)}, bf16[256,768]{1,0:T(8,128)(2,1)S(1)}, u32[]{:S(2)}, u32[]{:S(2)}) collective-permute-start(bf16[256,768]{1,0:T(8,128)(2,1)S(1)} %collective-permute-done.9.g2), channel_id=1, source_target_pairs={{0,1},{1,0},{2,3},{3,2},{4,5},{5,4},{6,7},{7,6},{8,9},{9,8},{10,11... | collective-permute-start | bytes 1179656 | tf_op jit(solution)/shard_map/ppermute | solution.py:333
  185.0 0.7 copy-start.11
  185.0 0.9 copy-start.12
  191.9 103.6 %copy-start.1 = (s32[128]{0:T(128)S(1)}, s32[128]{0:T(128)}, u32[]{:S(2)}) copy-start(s32[128]{0:T(128)} %partner_ref.1) | copy-start | bytes 1540
Sparse Core Ops, SparseCore 0:
  10.7 62.0 all-gather.1
  164.3 43.1 reduce-scatter.1

commit v6 on v4

--- a/solution.py
+++ b/solution.py
@@ -49,7 +49,7 @@
     return copies
 
 
-def pack_kernel(tok_ref, cot_ref, ids_ref, weight_ref, holder_ref, out_ref):
+def pack_kernel(tok_ref, ids_ref, weight_ref, holder_ref, out_ref):
     top, rows = ids_ref.shape
     width = tok_ref.shape[1]
     experts = holder_ref.shape[1]
@@ -78,11 +78,10 @@
         for place, part in enumerate(parts):
             meta = jnp.where(meta_lane == (place + 1) * top + k, part[:, k : k + 1], meta)
     out_ref[:, :width] = tok_ref[...]
-    out_ref[:, width : 2 * width] = cot_ref[...]
-    out_ref[:, 2 * width :] = meta.astype(BF16)
-
-
-def select_kernel(plane_ref, gathered_ref, out_ref, share_ref):
+    out_ref[:, width:] = meta.astype(BF16)
+
+
+def select_kernel(plane_ref, gathered_ref, cots_ref, out_ref, share_ref):
     total = gathered_ref.shape[0]
     targets, quarters, per_target, _ = out_ref.shape
     quarter = out_ref.shape[3] // 2
@@ -91,7 +90,7 @@
     rows = targets * per_target
     block = total // (per_target // 2)
     plane = plane_ref[0]
-    meta = gathered_ref[:, 2 * width :].astype(F32)
+    meta = gathered_ref[:, width:].astype(F32)
     row = lax.broadcasted_iota(jnp.int32, (total, rows), 1)
     token = lax.broadcasted_iota(jnp.int32, (total, rows), 0)
     target = row >> 4
@@ -119,7 +118,7 @@
             picked_t, gathered_ref[:, at : at + quarter], preferred_element_type=F32
         ).astype(BF16)
         out_ref[:, q, :, :quarter] = sent.reshape(targets, per_target, quarter)
-        cot = gathered_ref[:, width + at : width + at + quarter]
+        cot = cots_ref[:, at : at + quarter]
         grads = sum(jnp.dot(part, cot, preferred_element_type=F32) for part in shares_t)
         out_ref[:, q, :, quarter:] = grads.astype(BF16).reshape(targets, per_target, quarter)
 
@@ -248,17 +247,21 @@
     plane = lax.axis_index("zh").reshape(1).astype(jnp.int32)
     me = lax.axis_index(DP_AXES).reshape(1).astype(jnp.int32)
 
-    packed = call(pack_kernel, "pack", shape_of((24, 4224)), [VMEM] * 5, 10**6, 4 * 10**5)(
-        tokens, cotangent, expert_ids.T, route_weight.T, holder.reshape(1, -1)
+    packed = call(pack_kernel, "pack", shape_of((24, 2176)), [VMEM] * 4, 10**6, 2 * 10**5)(
+        tokens, expert_ids.T, route_weight.T, holder.reshape(1, -1)
+    )
+    copies = jnp.broadcast_to(cotangent[None], (8,) + cotangent.shape)
+    packed, copies, up0, down0 = lax.optimization_barrier(
+        (packed, copies, up_weight[0], down_weight[0])
     )
     gathered = lax.all_gather(packed, "zh", axis=0, tiled=True)
-
-    up0, down0 = up_weight[0], down_weight[0]
+    cots = lax.all_to_all(copies, "zh", split_axis=0, concat_axis=0, tiled=True).reshape(192, 2048)
+
     up2, down2 = lax.ppermute(up0, "yl", FLIP), lax.ppermute(down0, "yl", FLIP)
     up1, down1 = lax.ppermute(up0, "core", FLIP), lax.ppermute(down0, "core", FLIP)
     up3, down3 = lax.ppermute(up2, "core", FLIP), lax.ppermute(down2, "core", FLIP)
-    gathered, up1, up2, up3, down1, down2, down3 = lax.optimization_barrier(
-        (gathered, up1, up2, up3, down1, down2, down3)
+    gathered, cots, up1, up2, up3, down1, down2, down3 = lax.optimization_barrier(
+        (gathered, cots, up1, up2, up3, down1, down2, down3)
     )
     ups, downs = (up0, up1, up2, up3), (down0, down1, down2, down3)
 
@@ -266,10 +269,10 @@
         select_kernel,
         "select",
         (shape_of((16, 4, 16, 1024)), shape_of((192, 256), F32)),
-        [SMEM, VMEM],
+        [SMEM, VMEM, VMEM],
         10**9,
         4 * 10**6,
-    )(plane, gathered)
+    )(plane, gathered, cots)
     rows = lax.all_to_all(outgoing, GROUP_AXES, split_axis=0, concat_axis=0, tiled=True)
     by_feature = lax.all_to_all(
         rows.transpose(1, 0, 2, 3), DP_AXES, split_axis=0, concat_axis=0, tiled=True

time: 384 us -> 415 us (1.081)
  blocking collectives: 118 us -> 152 us
    all_gather x0 -> x1, blocking collectives: none -> 35.9 us  [body(): gathered = lax.all_gather(packed, 'zh', axis=0, tiled=True)]
    all_gather x1 -> x0, waiting for transfers between devices: 18.4 us -> none  [body(): gathered = lax.all_gather(packed, 'zh', axis=0, tiled=True)]
    all_to_all x0 -> x1, starting transfers between devices: none -> 15.6 us  [body(): lax.all_to_all(copies, 'zh', split_axis=0, concat_axis=0, tiled=True)]
    ppermute x1, starting transfers between devices: 14.8 us -> 5.23 us  [body(): lax.ppermute(up2, 'core', FLIP)]
    ppermute x1, waiting for transfers between devices: 2.06 us -> 11.6 us  [body(): lax.ppermute(down0, 'yl', FLIP)]
    ppermute x1, waiting for transfers between devices: 0.09 us -> 9.63 us  [body(): lax.ppermute(up0, 'yl', FLIP)]
    ppermute x1, starting transfers between devices: 8.68 us -> 3.43 us  [body(): lax.ppermute(up0, 'core', FLIP)]
    ppermute x1, starting transfers between devices: 7.95 us -> 3.66 us  [body(): lax.ppermute(down2, 'core', FLIP)]
  transfers between devices with their start and end apart: 14 -> 14, of which waited for: 9 -> 7; matrix products, arithmetic and copies ran while one was open for 0% -> 0% of each run, Pallas kernels for 5% -> 5%
where the time goes in v6:
time: 415 us; the launch traced here: 409 us
  blocking collectives  152 us (37%)
  waiting for transfers between devices  142 us (34%)
  starting transfers between devices  65.3 us (16%)
  Pallas kernels  28.5 us (7%)
  between operations  14.2 us (3%)
  local copies, waits for them, and re-layouts  7.41 us (2%)
    all_to_all x1, blocking collectives, body(): lax.all_to_all(chosen, SLOT_AXES, split_axis=0, concat_axis=0, tiled=True)  85.5 us
    reduce_scatter x1, waiting for transfers between devices, body(): layer_out = lax.psum_scatter(partial, 'zh', scatter_dimension=0, tiled=True)  77.3 us
    all_gather x1, blocking collectives, body(): gathered = lax.all_gather(packed, 'zh', axis=0, tiled=True)  35.9 us
    all_to_all x1, blocking collectives, body(): lax.all_to_all(outgoing, GROUP_AXES, split_axis=0, concat_axis=0, tiled=T...  31 us
    ppermute x1, waiting for transfers between devices, body(): acts2 = lax.ppermute(acts, 'yl', FLIP)  24 us
    all_to_all x1, starting transfers between devices, body(): lax.all_to_all(copies, 'zh', split_axis=0, concat_axis=0, tiled=True)  15.6 us
    ppermute x1, waiting for transfers between devices, body(): lax.ppermute(down0, 'yl', FLIP)  11.6 us
    all_to_all x1, waiting for transfers between devices, body(): lax.all_to_all(pieces, SLOT_AXES, split_axis=0, concat_axis=0, tiled=True)  11.3 us
  transfers between devices with their start and end apart: 14, of which 7 were waited for; matrix products, arithmetic and copies ran while one was open for 0% of the time, Pallas kernels for 5%

profile of v6, /device:TPU:1, one launch (start us, length us, event | category | flops | bytes accessed | tf_op | source)
XLA Modules:
  0.0 409.5 jit_solution(16152146510370893549)
XLA Ops:
  7.2 2.1 pack.1
  9.3 1.9 broadcast_in_dim.12
  11.2 15.6 %all-to-all-start = ((bf16[8,24,2048]{2,1,0:T(8,128)(2,1)}), bf16[8,24,2048]{2,1,0:T(8,128)(2,1)}, u32[]{:S(2)}, u32[]{:S(2)}) async-start(bf16[8,24,2048]{2,1,0:T(8,128)(2,1)} %broadcast_in_dim.12), calls=%async_computation | async-start | bytes 1572864 | tf_op jit(solution)/shard_map/all_to_all | solution.py:258
  26.8 3.2 collective-permute-start.1
  30.0 2.1 collective-permute-start.4
  32.1 3.4 collective-permute-start
  35.5 1.9 collective-permute-start.3
  37.5 9.6 %collective-permute-done.1.refs_2_ = bf16[512,768]{1,0:T(8,128)(2,1)} collective-permute-done((bf16[512,768]{1,0:T(8,128)(2,1)}, bf16[512,768]{1,0:T(8,128)(2,1)}, u32[]{:S(2)}, u32[]{:S(2)}) %collective-permute-start.1) | collective-permute-done | bytes 786464 | tf_op jit(solution)/shard_map/ppermute | solution.py:260
  47.1 5.2 %collective-permute-start.2 = (bf16[512,768]{1,0:T(8,128)(2,1)}, bf16[512,768]{1,0:T(8,128)(2,1)}, u32[]{:S(2)}, u32[]{:S(2)}) collective-permute-start(bf16[512,768]{1,0:T(8,128)(2,1)} %collective-permute-done.1.refs_2_), channel_id=1, source_target_pairs={{0,1},{1,0},{2,3},{3,2},{4,5},{5,4},{6,7},{7,6},{8,9},{9,8},{10,11... | collective-permute-start | bytes 2359304 | tf_op jit(solution)/shard_map/ppermute | solution.py:262
  52.3 11.6 %collective-permute-done.4.refs_6_.refs_2_ = bf16[768,512]{1,0:T(8,128)(2,1)S(1)} collective-permute-done((bf16[768,512]{1,0:T(8,128)(2,1)S(1)}, bf16[768,512]{1,0:T(8,128)(2,1)S(1)}, u32[]{:S(2)}, u32[]{:S(2)}) %collective-permute-start.4) | collective-permute-done | bytes 786464 | tf_op jit(solution)/shard_map/ppermute | solution.py:260
  63.9 3.7 collective-permute-start.5
  67.6 35.9 %all_gather.3.gathered_ref = bf16[192,2176]{1,0:T(8,128)(2,1)} all-gather(bf16[24,2176]{1,0:T(8,128)(2,1)S(1)} %copy-done.6), channel_id=1, replica_groups=mesh['yh'=2,'zh'=8,'zp'=2,'x'=4,'yl'=2,'core'=2] {'zh'}, dimensions={0}, use_global_device_ids=true | all-gather | bytes 940032 | tf_op jit(solution)/shard_map/all_gather | solution.py:257
  104.5 4.8 %select.1 = (bf16[16,4,16,1024]{3,2,1,0:T(8,128)(2,1)}, f32[192,256]{1,0:T(8,128)}) custom-call(s32[1]{0:T(128)} %bitcast.1.plane_ref, bf16[192,2176]{1,0:T(8,128)(2,1)} %all_gather.3.gathered_ref, bf16[192,2048]{1,0:T(8,128)(2,1)} %bitcast.7.cots_ref), custom_call_target="tpu_custom_call" | custom-call | flops 1000000000 | bytes 4000000 | tf_op jit(solution)/shard_map/select/pallas_call | solution.py:268
  109.2 31.0 %all_to_all.30.rows_ref = bf16[16,4,16,1024]{3,2,1,0:T(8,128)(2,1)S(1)} all-to-all(bf16[16,4,16,1024]{3,2,1,0:T(8,128)(2,1)} %get-tuple-element.31), channel_id=1, replica_groups=mesh['yh'=2,'zh'=8,'zp'=2,'x'=4,'yl'=2,'core'=2] {'yh','zp','x'}, dimensions={0} | all-to-all | bytes 4194304 | tf_op jit(solution)/shard_map/all_to_all | solution.py:276
  141.6 1.5 copy.17
  143.1 10.7 %all-to-all-start.2 = ((bf16[4,16,16,1024]{3,2,1,0:T(8,128)(2,1)}), bf16[4,16,16,1024]{3,2,1,0:T(8,128)(2,1)}, u32[]{:S(2)}, u32[]{:S(2)}) async-start(bf16[4,16,16,1024]{3,2,1,0:T(8,128)(2,1)} %bitcast.14), calls=%async_computation.2 | async-start | bytes 4194304 | tf_op jit(solution)/shard_map/all_to_all | solution.py:277
  153.7 7.0 %forward.1.acts_ref.a0 = bf16[256,1536]{1,0:T(8,128)(2,1)} custom-call(s32[1]{0:T(128)} %bitcast.me_ref, bf16[16,4,16,1024]{3,2,1,0:T(8,128)(2,1)} %copy-done.2, bf16[512,768]{1,0:T(8,128)(2,1)} %bitcast.5.refs_0_, bf16[512,768]{1,0:T(8,128)(2,1)} %collective-permute-done.refs_1_, bf16[512,768]{1,0:T(8,128)(2,1)} %collective-permute-done.1.refs_2_, ...), custom_call_target="tpu_custom_call" | custom-call | flops 1600000000 | bytes 9000000 | tf_op jit(solution)/shard_map/forward/pallas_call | solution.py:281
  160.8 3.3 collective-permute-start.7
  164.1 2.5 collective-permute-start.6
  166.6 4.8 %expert_out.1 = bf16[16,4,16,512]{3,2,1,0:T(8,128)(2,1)} custom-call(s32[1]{0:T(128)} %bitcast.me_ref, bf16[256,1536]{1,0:T(8,128)(2,1)} %forward.1.acts_ref.a0, bf16[768,512]{1,0:T(8,128)(2,1)} %bitcast.16, bf16[768,512]{1,0:T(8,128)(2,1)} %copy-done.5, bf16[768,512]{1,0:T(8,128)(2,1)} %copy-done.4, bf16[768,512]{1,0:T(8,128)(2,1)} %collective-permute-done.5.refs_7_.refs_3_), custom_call_target="tpu_custom_call" | custom-call | flops 800000000 | bytes 5000000 | tf_op jit(solution)/shard_map/expert_out/pallas_call | solution.py:297
  171.5 24.0 %collective-permute-done.7.a2 = bf16[256,1536]{1,0:T(8,128)(2,1)S(1)} collective-permute-done((bf16[256,1536]{1,0:T(8,128)(2,1)}, bf16[256,1536]{1,0:T(8,128)(2,1)S(1)}, u32[]{:S(2)}, u32[]{:S(2)}) %collective-permute-start.7) | collective-permute-done | bytes 786464 | tf_op jit(solution)/shard_map/ppermute | solution.py:294
  196.3 3.7 all-to-all-start.4
  200.0 2.8 collective-permute-start.8
  202.8 1.9 collective-permute-done.8.a3
  205.6 6.0 %moments.1 = bf16[128,48,128]{2,1,0:T(8,128)(2,1)} custom-call(s32[1]{0:T(128)} %bitcast.me_ref, bf16[4,16,16,1024]{3,2,1,0:T(8,128)(2,1)} %all-to-all-done.2.rows_ref, bf16[256,1536]{1,0:T(8,128)(2,1)} %forward.1.acts_ref.a0, bf16[256,1536]{1,0:T(8,128)(2,1)} %copy-done.8, bf16[256,1536]{1,0:T(8,128)(2,1)} %copy-done.7, bf16[256,1536]{1,0:T(8,128)(2,1)} %copy-done.9, ...), custom_call_target="tpu_custom_call" | custom-call | flops 3200000000 | bytes 9000000 | tf_op jit(solution)/shard_map/moments/pallas_call | solution.py:315
  211.6 5.9 %all-to-all-done.4.returned_ref = bf16[16,4,16,512]{3,2,1,0:T(8,128)(2,1)S(1)} async-done(((bf16[16,4,16,512]{3,2,1,0:T(8,128)(2,1)}), bf16[16,4,16,512]{3,2,1,0:T(8,128)(2,1)S(1)}, u32[]{:S(2)}, u32[]{:S(2)}) %all-to-all-start.4) | async-done | bytes 1048608 | tf_op jit(solution)/shard_map/all_to_all | solution.py:311
  217.4 7.0 %all-to-all-start.3 = ((bf16[128,48,128]{2,1,0:T(8,128)(2,1)}), bf16[128,48,128]{2,1,0:T(8,128)(2,1)S(1)}, u32[]{:S(2)}, u32[]{:S(2)}) async-start(bf16[128,48,128]{2,1,0:T(8,128)(2,1)} %moments.1), calls=%async_computation.3 | async-start | bytes 3145728 | tf_op jit(solution)/shard_map/all_to_all | solution.py:331
  224.7 1.7 combine.1
  226.4 77.3 %reduce-scatter.2.cloned.1.call-done = bf16[24,2048]{1,0:T(8,128)(2,1)} async-done(((bf16[192,2048]{1,0:T(8,128)(2,1)}), bf16[24,2048]{1,0:T(8,128)(2,1)}) %reduce-scatter.2.cloned.1.call-update) | async-done | bytes 98320 | tf_op jit(solution)/shard_map/reduce_scatter | solution.py:329
  303.7 11.3 %all-to-all-done.3.spread_ref = bf16[128,48,128]{2,1,0:T(8,128)(2,1)S(1)} async-done(((bf16[128,48,128]{2,1,0:T(8,128)(2,1)}), bf16[128,48,128]{2,1,0:T(8,128)(2,1)S(1)}, u32[]{:S(2)}, u32[]{:S(2)}) %all-to-all-start.3) | async-done | bytes 1572896 | tf_op jit(solution)/shard_map/all_to_all | solution.py:331
  315.7 85.5 %all_to_all.31.pieces_ref = bf16[128,48,128]{2,1,0:T(8,128)(2,1)S(1)} all-to-all(bf16[128,48,128]{2,1,0:T(8,128)(2,1)S(1)} %pick.1), channel_id=1, replica_groups=mesh['yh'=2,'zh'=8,'zp'=2,'x'=4,'yl'=2,'core'=2] {'yh','zh','zp','x'}, dimensions={0} | all-to-all | bytes 3145728 | tf_op jit(solution)/shard_map/all_to_all | solution.py:336
  401.2 1.4 unpack.1
  (30 shorter events, 5.1 us)
Async XLA Ops:
  7.2 22.8 %copy-start.3 = (bf16[1,768,512]{2,1,0:T(8,128)(2,1)S(1)}, bf16[1,768,512]{2,1,0:T(8,128)(2,1)}, u32[]{:S(2)}) copy-start(bf16[1,768,512]{2,1,0:T(8,128)(2,1)} %param.17) | copy-start | bytes 2359300
  9.3 58.4 %copy-start.6 = (bf16[24,2176]{1,0:T(8,128)(2,1)S(1)}, bf16[24,2176]{1,0:T(8,128)(2,1)}, u32[]{:S(2)}) copy-start(bf16[24,2176]{1,0:T(8,128)(2,1)} %pack.1) | copy-start | bytes 313348
  11.2 93.3 %all-to-all-start = ((bf16[8,24,2048]{2,1,0:T(8,128)(2,1)}), bf16[8,24,2048]{2,1,0:T(8,128)(2,1)}, u32[]{:S(2)}, u32[]{:S(2)}) async-start(bf16[8,24,2048]{2,1,0:T(8,128)(2,1)} %broadcast_in_dim.12), calls=%async_computation | async-start | bytes 1572864 | tf_op jit(solution)/shard_map/all_to_all | solution.py:258
  26.8 20.3 %collective-permute-start.1 = (bf16[512,768]{1,0:T(8,128)(2,1)}, bf16[512,768]{1,0:T(8,128)(2,1)}, u32[]{:S(2)}, u32[]{:S(2)}) collective-permute-start(bf16[512,768]{1,0:T(8,128)(2,1)} %bitcast.5.refs_0_), channel_id=1, source_target_pairs={{0,2},{2,0},{1,3},{3,1},{4,6},{6,4},{5,7},{7,5},{8,10},{10,8},{9,1... | collective-permute-start | bytes 2359304 | tf_op jit(solution)/shard_map/ppermute | solution.py:260
  30.0 33.9 %collective-permute-start.4 = (bf16[768,512]{1,0:T(8,128)(2,1)S(1)}, bf16[768,512]{1,0:T(8,128)(2,1)S(1)}, u32[]{:S(2)}, u32[]{:S(2)}) collective-permute-start(bf16[768,512]{1,0:T(8,128)(2,1)S(1)} %bitcast.17), channel_id=1, source_target_pairs={{0,2},{2,0},{1,3},{3,1},{4,6},{6,4},{5,7},{7,5},{8,10},{10,8},{9,1... | collective-permute-start | bytes 2359304 | tf_op jit(solution)/shard_map/ppermute | solution.py:260
  32.1 71.5 %collective-permute-start = (bf16[512,768]{1,0:T(8,128)(2,1)}, bf16[512,768]{1,0:T(8,128)(2,1)}, u32[]{:S(2)}, u32[]{:S(2)}) collective-permute-start(bf16[512,768]{1,0:T(8,128)(2,1)} %bitcast.5.refs_0_), channel_id=1, source_target_pairs={{0,1},{1,0},{2,3},{3,2},{4,5},{5,4},{6,7},{7,6},{8,9},{9,8},{10,11... | collective-permute-start | bytes 2359304 | tf_op jit(solution)/shard_map/ppermute | solution.py:261
  35.5 68.0 %collective-permute-start.3 = (bf16[768,512]{1,0:T(8,128)(2,1)S(1)}, bf16[768,512]{1,0:T(8,128)(2,1)S(1)}, u32[]{:S(2)}, u32[]{:S(2)}) collective-permute-start(bf16[768,512]{1,0:T(8,128)(2,1)S(1)} %bitcast.18), channel_id=1, source_target_pairs={{0,1},{1,0},{2,3},{3,2},{4,5},{5,4},{6,7},{7,6},{8,9},{9,8},{10,11... | collective-permute-start | bytes 2359304 | tf_op jit(solution)/shard_map/ppermute | solution.py:261
  47.1 56.5 %collective-permute-start.2 = (bf16[512,768]{1,0:T(8,128)(2,1)}, bf16[512,768]{1,0:T(8,128)(2,1)}, u32[]{:S(2)}, u32[]{:S(2)}) collective-permute-start(bf16[512,768]{1,0:T(8,128)(2,1)} %collective-permute-done.1.refs_2_), channel_id=1, source_target_pairs={{0,1},{1,0},{2,3},{3,2},{4,5},{5,4},{6,7},{7,6},{8,9},{9,8},{10,11... | collective-permute-start | bytes 2359304 | tf_op jit(solution)/shard_map/ppermute | solution.py:262
  63.9 45.3 %copy-start.4 = (bf16[768,512]{1,0:T(8,128)(2,1)}, bf16[768,512]{1,0:T(8,128)(2,1)S(1)}, u32[]{:S(2)}) copy-start(bf16[768,512]{1,0:T(8,128)(2,1)S(1)} %collective-permute-done.4.refs_6_.refs_2_) | copy-start | bytes 2359300
  63.9 39.7 %collective-permute-start.5 = (bf16[768,512]{1,0:T(8,128)(2,1)S(1)}, bf16[768,512]{1,0:T(8,128)(2,1)}, u32[]{:S(2)}, u32[]{:S(2)}) collective-permute-start(bf16[768,512]{1,0:T(8,128)(2,1)S(1)} %collective-permute-done.4.refs_6_.refs_2_), channel_id=1, source_target_pairs={{0,1},{1,0},{2,3},{3,2},{4,5},{5,4},{6,7},{7,6},{8,9},{9,8},{10,11... | collective-permute-start | bytes 2359304 | tf_op jit(solution)/shard_map/ppermute | solution.py:262
  103.6 0.9 copy-start.5
  140.2 1.4 copy-start.2
  143.1 52.4 %all-to-all-start.2 = ((bf16[4,16,16,1024]{3,2,1,0:T(8,128)(2,1)}), bf16[4,16,16,1024]{3,2,1,0:T(8,128)(2,1)}, u32[]{:S(2)}, u32[]{:S(2)}) async-start(bf16[4,16,16,1024]{3,2,1,0:T(8,128)(2,1)} %bitcast.14), calls=%async_computation.2 | async-start | bytes 4194304 | tf_op jit(solution)/shard_map/all_to_all | solution.py:277
  160.8 34.6 %collective-permute-start.7 = (bf16[256,1536]{1,0:T(8,128)(2,1)}, bf16[256,1536]{1,0:T(8,128)(2,1)S(1)}, u32[]{:S(2)}, u32[]{:S(2)}) collective-permute-start(bf16[256,1536]{1,0:T(8,128)(2,1)} %forward.1.acts_ref.a0), channel_id=1, source_target_pairs={{0,2},{2,0},{1,3},{3,1},{4,6},{6,4},{5,7},{7,5},{8,10},{10,8},{9,1... | collective-permute-start | bytes 2359304 | tf_op jit(solution)/shard_map/ppermute | solution.py:294
  164.1 31.3 %collective-permute-start.6 = (bf16[256,1536]{1,0:T(8,128)(2,1)}, bf16[256,1536]{1,0:T(8,128)(2,1)S(1)}, u32[]{:S(2)}, u32[]{:S(2)}) collective-permute-start(bf16[256,1536]{1,0:T(8,128)(2,1)} %forward.1.acts_ref.a0), channel_id=1, source_target_pairs={{0,1},{1,0},{2,3},{3,2},{4,5},{5,4},{6,7},{7,6},{8,9},{9,8},{10,11... | collective-permute-start | bytes 2359304 | tf_op jit(solution)/shard_map/ppermute | solution.py:295
  195.4 10.2 %copy-start.7 = (bf16[256,1536]{1,0:T(8,128)(2,1)}, bf16[256,1536]{1,0:T(8,128)(2,1)S(1)}, u32[]{:S(2)}) copy-start(bf16[256,1536]{1,0:T(8,128)(2,1)S(1)} %collective-permute-done.7.a2) | copy-start | bytes 2359300
  195.4 0.9 copy-start.8
  196.3 21.1 %all-to-all-start.4 = ((bf16[16,4,16,512]{3,2,1,0:T(8,128)(2,1)}), bf16[16,4,16,512]{3,2,1,0:T(8,128)(2,1)S(1)}, u32[]{:S(2)}, u32[]{:S(2)}) async-start(bf16[16,4,16,512]{3,2,1,0:T(8,128)(2,1)} %expert_out.1), calls=%async_computation.4 | async-start | bytes 2097152 | tf_op jit(solution)/shard_map/all_to_all | solution.py:311
  200.0 4.7 %collective-permute-start.8 = (bf16[256,1536]{1,0:T(8,128)(2,1)S(1)}, bf16[256,1536]{1,0:T(8,128)(2,1)S(1)}, u32[]{:S(2)}, u32[]{:S(2)}) collective-permute-start(bf16[256,1536]{1,0:T(8,128)(2,1)S(1)} %collective-permute-done.7.a2), channel_id=1, source_target_pairs={{0,1},{1,0},{2,3},{3,2},{4,5},{5,4},{6,7},{7,6},{8,9},{9,8},{10,11... | collective-permute-start | bytes 2359304 | tf_op jit(solution)/shard_map/ppermute | solution.py:310
  204.7 0.9 copy-start.9
  211.6 13.1 %copy-start.1 = (f32[192,256]{1,0:T(8,128)S(1)}, f32[192,256]{1,0:T(8,128)}, u32[]{:S(2)}) copy-start(f32[192,256]{1,0:T(8,128)} %get-tuple-element.41.share_ref) | copy-start | bytes 589828
  217.4 97.5 %all-to-all-start.3 = ((bf16[128,48,128]{2,1,0:T(8,128)(2,1)}), bf16[128,48,128]{2,1,0:T(8,128)(2,1)S(1)}, u32[]{:S(2)}, u32[]{:S(2)}) async-start(bf16[128,48,128]{2,1,0:T(8,128)(2,1)} %moments.1), calls=%async_computation.3 | async-start | bytes 3145728 | tf_op jit(solution)/shard_map/all_to_all | solution.py:331
  224.4 90.5 %copy-start = (s32[128]{0:T(128)S(1)}, s32[128]{0:T(128)}, u32[]{:S(2)}) copy-start(s32[128]{0:T(128)} %partner_ref.1) | copy-start | bytes 1540
  224.5 79.3 %reduce-scatter.2.cloned.1.call-start = ((), (), s32[]{:S(2)}) async-start(), calls=%async_computation.7 | async-start | bytes 884736 | tf_op jit(solution)/shard_map/reduce_scatter | solution.py:329
Sparse Core Ops, SparseCore 0:
  228.7 74.9 reduce-scatter.1

commit v7 on v4

--- a/solution.py
+++ b/solution.py
@@ -125,7 +125,7 @@
 
 
 def forward_kernel(me_ref, rows_ref, *refs):
-    sources, out_ref, ups, downs, sems = refs[:8], refs[8], refs[9], refs[10], refs[11]
+    sources, hidden_ref, pre_grad_ref, ups, downs, sems = refs[:8], *refs[8:]
     copies = fetch(
         [(sources[j + 4 * kind], held.at[j]) for j in range(4) for kind, held in ((0, ups), (1, downs))],
         sems,
@@ -146,15 +146,15 @@
             both[:, quarter:], downs[j], (((1,), (1,)), ((), ())), preferred_element_type=F32
         )
     sigmoid = 1.0 / (1.0 + jnp.exp(-preact))
-    out_ref[:, :hidden_count] = (preact * sigmoid).astype(BF16)
-    out_ref[:, hidden_count:] = (back * sigmoid * (1.0 + preact * (1.0 - sigmoid))).astype(BF16)
-
-
-def expert_out_kernel(me_ref, acts_ref, *refs):
+    hidden_ref[...] = (preact * sigmoid).astype(BF16)
+    pre_grad_ref[...] = (back * sigmoid * (1.0 + preact * (1.0 - sigmoid))).astype(BF16)
+
+
+def expert_out_kernel(me_ref, hidden_ref, *refs):
     sources, out_ref, downs, sems = refs[:4], refs[4], refs[5], refs[6]
     copies = fetch([(sources[j], downs.at[j]) for j in range(4)], sems)
     targets, _, per_target, quarter = out_ref.shape
-    hidden = acts_ref[:, : downs.shape[1]]
+    hidden = hidden_ref[...]
     me = me_ref[0]
     for j in range(4):
         copies[j].wait()
@@ -172,25 +172,25 @@
 
 
 def moment_kernel(
-    me_ref, rows_ref, a0, a1, a2, a3, up_hbm, down_hbm, out_ref, up_ref, down_ref, sems
+    me_ref, rows_ref, h0, h1, h2, h3, g0, g1, g2, g3, up_hbm, down_hbm, out_ref, up_ref, down_ref, sems
 ):
     copies = fetch([(up_hbm, up_ref), (down_hbm, down_ref)], sems)
-    acts = (a0, a1, a2, a3)
+    hiddens, pre_grads = (h0, h1, h2, h3), (g0, g1, g2, g3)
     me = me_ref[0]
     features, hidden_count = up_ref.shape
     over_rows = (((0,), (0,)), ((), ()))
     up_grad = jnp.zeros((features, hidden_count), F32)
     down_grad = jnp.zeros((hidden_count, features), F32)
     for j in range(4):
-        rows = rows_ref[me ^ j].reshape(acts[j].shape[0], 2 * features)
+        rows = rows_ref[me ^ j].reshape(hiddens[j].shape[0], 2 * features)
         up_grad = up_grad + lax.dot_general(
             rows[:, :features],
-            acts[j][:, hidden_count:],
+            pre_grads[j][...],
             over_rows,
             preferred_element_type=F32,
         )
         down_grad = down_grad + lax.dot_general(
-            acts[j][:, :hidden_count],
+            hiddens[j][...],
             rows[:, features:],
             over_rows,
             preferred_element_type=F32,
@@ -275,10 +275,10 @@
         rows.transpose(1, 0, 2, 3), DP_AXES, split_axis=0, concat_axis=0, tiled=True
     )
 
-    acts = call(
+    hidden, pre_grad = call(
         forward_kernel,
         "forward",
-        shape_of((256, 1536)),
+        (shape_of((256, 768)), shape_of((256, 768))),
         [SMEM, VMEM] + [HBM] * 8,
         16 * 10**8,
         9 * 10**6,
@@ -288,8 +288,10 @@
             pltpu.SemaphoreType.DMA((8,)),
         ),
     )(me, rows, *ups, *downs)
-    acts2 = lax.ppermute(acts, "yl", FLIP)
-    acts1 = lax.ppermute(acts, "core", FLIP)
+    hidden2 = lax.ppermute(hidden, "yl", FLIP)
+    hidden1 = lax.ppermute(hidden, "core", FLIP)
+    pre_grad1 = lax.ppermute(pre_grad, "core", FLIP)
+    pre_grad2 = lax.ppermute(pre_grad, "yl", FLIP)
 
     expert_out = call(
         expert_out_kernel,
@@ -299,12 +301,14 @@
         8 * 10**8,
         5 * 10**6,
         (pltpu.VMEM((4, 768, 512), BF16), pltpu.SemaphoreType.DMA((4,))),
-    )(me, acts, *downs)
-
-    by_feature, acts1, acts2, expert_out = lax.optimization_barrier(
-        (by_feature, acts1, acts2, expert_out)
-    )
-    acts3 = lax.ppermute(acts2, "core", FLIP)
+    )(me, hidden, *downs)
+
+    by_feature, hidden1, hidden2, pre_grad1, expert_out = lax.optimization_barrier(
+        (by_feature, hidden1, hidden2, pre_grad1, expert_out)
+    )
+    hidden3 = lax.ppermute(hidden2, "core", FLIP)
+    pre_grad2, hidden3 = lax.optimization_barrier((pre_grad2, hidden3))
+    pre_grad3 = lax.ppermute(pre_grad2, "core", FLIP)
     returned = lax.all_to_all(expert_out, GROUP_AXES, split_axis=0, concat_axis=0, tiled=True)
     partial = call(
         combine_kernel, "combine", shape_of((192, 2048)), [VMEM, VMEM], 6 * 10**8, 2 * 10**6, (), 12
@@ -313,7 +317,7 @@
         moment_kernel,
         "moments",
         shape_of((128, 48, 128)),
-        [SMEM] + [VMEM] * 5 + [HBM] * 2,
+        [SMEM] + [VMEM] * 9 + [HBM] * 2,
         32 * 10**8,
         9 * 10**6,
         (
@@ -321,7 +325,21 @@
             pltpu.VMEM((768, 512), BF16),
             pltpu.SemaphoreType.DMA((2,)),
         ),
-    )(me, by_feature, acts, acts1, acts2, acts3, up_moment[0], down_moment[0])
+        44,
+    )(
+        me,
+        by_feature,
+        hidden,
+        hidden1,
+        hidden2,
+        hidden3,
+        pre_grad,
+        pre_grad1,
+        pre_grad2,
+        pre_grad3,
+        up_moment[0],
+        down_moment[0],
+    )
 
     layer_out = lax.psum_scatter(partial, "zh", scatter_dimension=0, tiled=True)
 

time: 384 us -> 393 us (1.023)
  starting transfers between devices: 68.4 us -> 81.6 us
    ppermute x3 -> x6, starting transfers between devices: 8.63 us -> 15.5 us  [the longest x1 3.59 us: body(): hidden2 = lax.ppermute(hidden, 'yl', FLIP)]
    all_to_all x1, starting transfers between devices: 8.53 us -> 14.7 us  [body(): lax.all_to_all(pieces, SLOT_AXES, split_axis=0, concat_axis=0, tiled=True)]
    all_to_all x1, waiting for transfers between devices: 5.89 us -> 0.01 us  [body(): lax.all_to_all(expert_out, GROUP_AXES, split_axis=0, concat_axis=0, tiled...]
    all_to_all x1, waiting for transfers between devices: 10.6 us -> 16.2 us  [body(): lax.all_to_all(pieces, SLOT_AXES, split_axis=0, concat_axis=0, tiled=True)]
    ppermute x3 -> x6, waiting for transfers between devices: 25.9 us -> 31 us  [the longest x1 16.1 us: body(): pre_grad2 = lax.ppermute(pre_grad, 'yl', FLIP)]
  transfers between devices with their start and end apart: 14 -> 17, of which waited for: 9 -> 9; matrix products, arithmetic and copies ran while one was open for 0% -> 0% of each run, Pallas kernels for 5% -> 5%
where the time goes in v7:
time: 393 us; the launch traced here: 389 us
  waiting for transfers between devices  146 us (37%)
  blocking collectives  116 us (30%)
  starting transfers between devices  81.6 us (21%)
  Pallas kernels  28 us (7%)
  between operations  14.3 us (4%)
    all_to_all x1, blocking collectives, body(): lax.all_to_all(chosen, SLOT_AXES, split_axis=0, concat_axis=0, tiled=True)  82.7 us
    reduce_scatter x1, waiting for transfers between devices, body(): layer_out = lax.psum_scatter(partial, 'zh', scatter_dimension=0, tiled=True)  76.3 us
    all_to_all x1, blocking collectives, body(): lax.all_to_all(outgoing, GROUP_AXES, split_axis=0, concat_axis=0, tiled=T...  33.7 us
    all_gather x1, waiting for transfers between devices, body(): gathered = lax.all_gather(packed, 'zh', axis=0, tiled=True)  18.4 us
    all_to_all x1, waiting for transfers between devices, body(): lax.all_to_all(pieces, SLOT_AXES, split_axis=0, concat_axis=0, tiled=True)  16.2 us
    ppermute x1, waiting for transfers between devices, body(): pre_grad2 = lax.ppermute(pre_grad, 'yl', FLIP)  16.1 us
    ppermute x1, starting transfers between devices, body(): lax.ppermute(up2, 'core', FLIP)  14.8 us
    all_to_all x1, starting transfers between devices, body(): lax.all_to_all(pieces, SLOT_AXES, split_axis=0, concat_axis=0, tiled=True)  14.7 us
  transfers between devices with their start and end apart: 17, of which 9 were waited for; matrix products, arithmetic and copies ran while one was open for 0% of the time, Pallas kernels for 5%

profile of v7, /device:TPU:1, one launch (start us, length us, event | category | flops | bytes accessed | tf_op | source)
XLA Modules:
  0.0 389.2 jit_solution(10194617884400361928)
XLA Ops:
  7.2 2.1 pack.1
  9.3 4.0 %collective-permute-start.1 = (bf16[512,768]{1,0:T(8,128)(2,1)}, bf16[512,768]{1,0:T(8,128)(2,1)}, u32[]{:S(2)}, u32[]{:S(2)}) collective-permute-start(bf16[512,768]{1,0:T(8,128)(2,1)} %bitcast.20), channel_id=1, source_target_pairs={{0,2},{2,0},{1,3},{3,1},{4,6},{6,4},{5,7},{7,5},{8,10},{10,8},{9,1... | collective-permute-start | bytes 2359304 | tf_op jit(solution)/shard_map/ppermute | solution.py:257
  13.4 1.9 collective-permute-start.4
  15.3 8.7 %collective-permute-start = (bf16[512,768]{1,0:T(8,128)(2,1)}, bf16[512,768]{1,0:T(8,128)(2,1)}, u32[]{:S(2)}, u32[]{:S(2)}) collective-permute-start(bf16[512,768]{1,0:T(8,128)(2,1)} %bitcast.21), channel_id=1, source_target_pairs={{0,1},{1,0},{2,3},{3,2},{4,5},{5,4},{6,7},{7,6},{8,9},{9,8},{10,11... | collective-permute-start | bytes 2359304 | tf_op jit(solution)/shard_map/ppermute | solution.py:258
  24.0 1.9 collective-permute-start.3
  26.0 14.8 %collective-permute-start.2 = (bf16[512,768]{1,0:T(8,128)(2,1)}, bf16[512,768]{1,0:T(8,128)(2,1)}, u32[]{:S(2)}, u32[]{:S(2)}) collective-permute-start(bf16[512,768]{1,0:T(8,128)(2,1)} %collective-permute-done.1.refs_2_), channel_id=1, source_target_pairs={{0,1},{1,0},{2,3},{3,2},{4,5},{5,4},{6,7},{7,6},{8,9},{9,8},{10,11... | collective-permute-start | bytes 2359304 | tf_op jit(solution)/shard_map/ppermute | solution.py:259
  40.8 2.1 collective-permute-done.4.refs_6_.refs_2_
  42.9 7.9 %collective-permute-start.5 = (bf16[768,512]{1,0:T(8,128)(2,1)S(1)}, bf16[768,512]{1,0:T(8,128)(2,1)S(1)}, u32[]{:S(2)}, u32[]{:S(2)}) collective-permute-start(bf16[768,512]{1,0:T(8,128)(2,1)S(1)} %collective-permute-done.4.refs_6_.refs_2_), channel_id=1, source_target_pairs={{0,1},{1,0},{2,3},{3,2},{4,5},{5,4},{6,7},{7,6},{8,9},{9,8},{10,11... | collective-permute-start | bytes 2359304 | tf_op jit(solution)/shard_map/ppermute | solution.py:259
  50.9 1.8 collective-permute-done.5.refs_7_.refs_3_
  53.6 18.4 %all-gather.2.cloned.1.call-done.gathered_ref = bf16[192,4224]{1,0:T(8,128)(2,1)} async-done(((bf16[24,4224]{1,0:T(8,128)(2,1)}), bf16[192,4224]{1,0:T(8,128)(2,1)}) %all-gather.2.cloned.1.call-update) | async-done | bytes 1622032 | tf_op jit(solution)/shard_map/all_gather | solution.py:254
  72.0 4.8 %select.1 = (bf16[16,4,16,1024]{3,2,1,0:T(8,128)(2,1)}, f32[192,256]{1,0:T(8,128)}) custom-call(s32[1]{0:T(128)} %bitcast.1.plane_ref, bf16[192,4224]{1,0:T(8,128)(2,1)} %all-gather.2.cloned.1.call-done.gathered_ref), custom_call_target="tpu_custom_call" | custom-call | flops 1000000000 | bytes 4000000 | tf_op jit(solution)/shard_map/select/pallas_call | solution.py:265
  76.9 33.7 %all_to_all.25.rows_ref = bf16[16,4,16,1024]{3,2,1,0:T(8,128)(2,1)S(1)} all-to-all(bf16[16,4,16,1024]{3,2,1,0:T(8,128)(2,1)} %get-tuple-element.26), channel_id=1, replica_groups=mesh['yh'=2,'zh'=8,'zp'=2,'x'=4,'yl'=2,'core'=2] {'yh','zp','x'}, dimensions={0} | all-to-all | bytes 4194304 | tf_op jit(solution)/shard_map/all_to_all | solution.py:273
  110.5 1.6 copy.17
  112.5 8.2 %all-to-all-start.1 = ((bf16[4,16,16,1024]{3,2,1,0:T(8,128)(2,1)}), bf16[4,16,16,1024]{3,2,1,0:T(8,128)(2,1)}, u32[]{:S(2)}, u32[]{:S(2)}) async-start(bf16[4,16,16,1024]{3,2,1,0:T(8,128)(2,1)} %bitcast.13), calls=%async_computation.1 | async-start | bytes 4194304 | tf_op jit(solution)/shard_map/all_to_all | solution.py:274
  120.7 7.0 %forward.1 = (bf16[256,768]{1,0:T(8,128)(2,1)}, bf16[256,768]{1,0:T(8,128)(2,1)}) custom-call(s32[1]{0:T(128)} %bitcast.me_ref, bf16[16,4,16,1024]{3,2,1,0:T(8,128)(2,1)} %copy-done.6, bf16[512,768]{1,0:T(8,128)(2,1)} %bitcast.22, bf16[512,768]{1,0:T(8,128)(2,1)} %collective-permute-done.refs_1_, bf16[512,768]{1,0:T(8,128)(2,1)} %collective-permute-done.1.refs_2_, ...), custom_call_target="tpu_custom_call" | custom-call | flops 1600000000 | bytes 9000000 | tf_op jit(solution)/shard_map/forward/pallas_call | solution.py:278
  127.8 2.0 collective-permute-start.8
  129.8 3.6 collective-permute-start.7
  133.4 2.4 collective-permute-start.6
  135.7 4.7 %expert_out.1 = bf16[16,4,16,512]{3,2,1,0:T(8,128)(2,1)} custom-call(s32[1]{0:T(128)} %bitcast.me_ref, bf16[256,768]{1,0:T(8,128)(2,1)} %get-tuple-element.33.hidden_ref.h0, bf16[768,512]{1,0:T(8,128)(2,1)} %bitcast.19, bf16[768,512]{1,0:T(8,128)(2,1)} %copy-done.8, bf16[768,512]{1,0:T(8,128)(2,1)} %copy-done.7, bf16[768,512]{1,0:T(8,128)(2,1)} %copy-done.9), custom_call_target="tpu_custom_call" | custom-call | flops 800000000 | bytes 5000000 | tf_op jit(solution)/shard_map/expert_out/pallas_call | solution.py:296
  140.5 13.6 %collective-permute-done.7.h2 = bf16[256,768]{1,0:T(8,128)(2,1)} collective-permute-done((bf16[256,768]{1,0:T(8,128)(2,1)}, bf16[256,768]{1,0:T(8,128)(2,1)}, u32[]{:S(2)}, u32[]{:S(2)}) %collective-permute-start.7) | collective-permute-done | bytes 393248 | tf_op jit(solution)/shard_map/ppermute | solution.py:291
  154.1 3.7 all-to-all-start.3
  157.8 2.2 collective-permute-start.9
  160.0 2.8 collective-permute-start.10
  162.8 16.1 %collective-permute-done.9.g2 = bf16[256,768]{1,0:T(8,128)(2,1)S(1)} collective-permute-done((bf16[256,768]{1,0:T(8,128)(2,1)S(1)}, bf16[256,768]{1,0:T(8,128)(2,1)S(1)}, u32[]{:S(2)}, u32[]{:S(2)}) %collective-permute-start.9) | collective-permute-done | bytes 393248 | tf_op jit(solution)/shard_map/ppermute | solution.py:294
  178.9 2.5 collective-permute-start.11
  182.8 5.5 %moments.1 = bf16[128,48,128]{2,1,0:T(8,128)(2,1)} custom-call(s32[1]{0:T(128)} %bitcast.me_ref, bf16[4,16,16,1024]{3,2,1,0:T(8,128)(2,1)} %all-to-all-done.1.rows_ref, bf16[256,768]{1,0:T(8,128)(2,1)S(1)} %copy-done, bf16[256,768]{1,0:T(8,128)(2,1)} %collective-permute-done.6.h1, bf16[256,768]{1,0:T(8,128)(2,1)} %collective-permute-done.7.h2, ...), custom_call_target="tpu_custom_call" | custom-call | flops 3200000000 | bytes 9000000 | tf_op jit(solution)/shard_map/moments/pallas_call | solution.py:316
  188.3 14.7 %all-to-all-start.2 = ((bf16[128,48,128]{2,1,0:T(8,128)(2,1)}), bf16[128,48,128]{2,1,0:T(8,128)(2,1)S(1)}, u32[]{:S(2)}, u32[]{:S(2)}) async-start(bf16[128,48,128]{2,1,0:T(8,128)(2,1)} %moments.1), calls=%async_computation.2 | async-start | bytes 3145728 | tf_op jit(solution)/shard_map/all_to_all | solution.py:346
  203.3 1.7 combine.1
  205.0 76.3 %reduce-scatter.2.cloned.1.call-done = bf16[24,2048]{1,0:T(8,128)(2,1)} async-done(((bf16[192,2048]{1,0:T(8,128)(2,1)}), bf16[24,2048]{1,0:T(8,128)(2,1)}) %reduce-scatter.2.cloned.1.call-update) | async-done | bytes 98320 | tf_op jit(solution)/shard_map/reduce_scatter | solution.py:344
  281.3 16.2 %all-to-all-done.2.spread_ref = bf16[128,48,128]{2,1,0:T(8,128)(2,1)S(1)} async-done(((bf16[128,48,128]{2,1,0:T(8,128)(2,1)}), bf16[128,48,128]{2,1,0:T(8,128)(2,1)S(1)}, u32[]{:S(2)}, u32[]{:S(2)}) %all-to-all-start.2) | async-done | bytes 1572896 | tf_op jit(solution)/shard_map/all_to_all | solution.py:346
  298.2 82.7 %all_to_all.26.pieces_ref = bf16[128,48,128]{2,1,0:T(8,128)(2,1)S(1)} all-to-all(bf16[128,48,128]{2,1,0:T(8,128)(2,1)S(1)} %pick.1), channel_id=1, replica_groups=mesh['yh'=2,'zh'=8,'zp'=2,'x'=4,'yl'=2,'core'=2] {'yh','zh','zp','x'}, dimensions={0} | all-to-all | bytes 3145728 | tf_op jit(solution)/shard_map/all_to_all | solution.py:351
  381.0 1.4 unpack.1
  (35 shorter events, 3.8 us)
Async XLA Ops:
  7.2 64.9 %all-gather.2.cloned.1.call-start = ((), (), s32[]{:S(2)}) async-start(), calls=%async_computation.6 | async-start | bytes 1824768 | tf_op jit(solution)/shard_map/all_gather | solution.py:254
  9.3 16.7 %collective-permute-start.1 = (bf16[512,768]{1,0:T(8,128)(2,1)}, bf16[512,768]{1,0:T(8,128)(2,1)}, u32[]{:S(2)}, u32[]{:S(2)}) collective-permute-start(bf16[512,768]{1,0:T(8,128)(2,1)} %bitcast.20), channel_id=1, source_target_pairs={{0,2},{2,0},{1,3},{3,1},{4,6},{6,4},{5,7},{7,5},{8,10},{10,8},{9,1... | collective-permute-start | bytes 2359304 | tf_op jit(solution)/shard_map/ppermute | solution.py:257
  13.4 29.5 %collective-permute-start.4 = (bf16[768,512]{1,0:T(8,128)(2,1)}, bf16[768,512]{1,0:T(8,128)(2,1)S(1)}, u32[]{:S(2)}, u32[]{:S(2)}) collective-permute-start(bf16[768,512]{1,0:T(8,128)(2,1)} %bitcast.16), channel_id=1, source_target_pairs={{0,2},{2,0},{1,3},{3,1},{4,6},{6,4},{5,7},{7,5},{8,10},{10,8},{9,1... | collective-permute-start | bytes 2359304 | tf_op jit(solution)/shard_map/ppermute | solution.py:257
  15.3 35.5 %collective-permute-start = (bf16[512,768]{1,0:T(8,128)(2,1)}, bf16[512,768]{1,0:T(8,128)(2,1)}, u32[]{:S(2)}, u32[]{:S(2)}) collective-permute-start(bf16[512,768]{1,0:T(8,128)(2,1)} %bitcast.21), channel_id=1, source_target_pairs={{0,1},{1,0},{2,3},{3,2},{4,5},{5,4},{6,7},{7,6},{8,9},{9,8},{10,11... | collective-permute-start | bytes 2359304 | tf_op jit(solution)/shard_map/ppermute | solution.py:258
  24.0 26.9 %collective-permute-start.3 = (bf16[768,512]{1,0:T(8,128)(2,1)}, bf16[768,512]{1,0:T(8,128)(2,1)S(1)}, u32[]{:S(2)}, u32[]{:S(2)}) collective-permute-start(bf16[768,512]{1,0:T(8,128)(2,1)} %bitcast.17), channel_id=1, source_target_pairs={{0,1},{1,0},{2,3},{3,2},{4,5},{5,4},{6,7},{7,6},{8,9},{9,8},{10,11... | collective-permute-start | bytes 2359304 | tf_op jit(solution)/shard_map/ppermute | solution.py:258
  26.0 24.9 %collective-permute-start.2 = (bf16[512,768]{1,0:T(8,128)(2,1)}, bf16[512,768]{1,0:T(8,128)(2,1)}, u32[]{:S(2)}, u32[]{:S(2)}) collective-permute-start(bf16[512,768]{1,0:T(8,128)(2,1)} %collective-permute-done.1.refs_2_), channel_id=1, source_target_pairs={{0,1},{1,0},{2,3},{3,2},{4,5},{5,4},{6,7},{7,6},{8,9},{9,8},{10,11... | collective-permute-start | bytes 2359304 | tf_op jit(solution)/shard_map/ppermute | solution.py:259
  42.9 34.0 %copy-start.7 = (bf16[768,512]{1,0:T(8,128)(2,1)}, bf16[768,512]{1,0:T(8,128)(2,1)S(1)}, u32[]{:S(2)}) copy-start(bf16[768,512]{1,0:T(8,128)(2,1)S(1)} %collective-permute-done.4.refs_6_.refs_2_) | copy-start | bytes 2359300
  42.9 9.8 %collective-permute-start.5 = (bf16[768,512]{1,0:T(8,128)(2,1)S(1)}, bf16[768,512]{1,0:T(8,128)(2,1)S(1)}, u32[]{:S(2)}, u32[]{:S(2)}) collective-permute-start(bf16[768,512]{1,0:T(8,128)(2,1)S(1)} %collective-permute-done.4.refs_6_.refs_2_), channel_id=1, source_target_pairs={{0,1},{1,0},{2,3},{3,2},{4,5},{5,4},{6,7},{7,6},{8,9},{9,8},{10,11... | collective-permute-start | bytes 2359304 | tf_op jit(solution)/shard_map/ppermute | solution.py:259
  50.9 26.0 %copy-start.8 = (bf16[768,512]{1,0:T(8,128)(2,1)}, bf16[768,512]{1,0:T(8,128)(2,1)S(1)}, u32[]{:S(2)}) copy-start(bf16[768,512]{1,0:T(8,128)(2,1)S(1)} %collective-permute-done.3.refs_5_.refs_1_) | copy-start | bytes 2359300
  52.7 0.9 copy-start.9
  110.5 2.0 copy-start.6
  112.5 41.6 %all-to-all-start.1 = ((bf16[4,16,16,1024]{3,2,1,0:T(8,128)(2,1)}), bf16[4,16,16,1024]{3,2,1,0:T(8,128)(2,1)}, u32[]{:S(2)}, u32[]{:S(2)}) async-start(bf16[4,16,16,1024]{3,2,1,0:T(8,128)(2,1)} %bitcast.13), calls=%async_computation.1 | async-start | bytes 4194304 | tf_op jit(solution)/shard_map/all_to_all | solution.py:274
  127.8 12.7 %collective-permute-start.8 = (bf16[256,768]{1,0:T(8,128)(2,1)}, bf16[256,768]{1,0:T(8,128)(2,1)}, u32[]{:S(2)}, u32[]{:S(2)}) collective-permute-start(bf16[256,768]{1,0:T(8,128)(2,1)} %get-tuple-element.34.g0), channel_id=1, source_target_pairs={{0,1},{1,0},{2,3},{3,2},{4,5},{5,4},{6,7},{7,6},{8,9},{9,8},{10,11... | collective-permute-start | bytes 1179656 | tf_op jit(solution)/shard_map/ppermute | solution.py:293
  129.8 24.3 %collective-permute-start.7 = (bf16[256,768]{1,0:T(8,128)(2,1)}, bf16[256,768]{1,0:T(8,128)(2,1)}, u32[]{:S(2)}, u32[]{:S(2)}) collective-permute-start(bf16[256,768]{1,0:T(8,128)(2,1)} %get-tuple-element.33.hidden_ref.h0), channel_id=1, source_target_pairs={{0,2},{2,0},{1,3},{3,1},{4,6},{6,4},{5,7},{7,5},{8,10},{10,8},{9,1... | collective-permute-start | bytes 1179656 | tf_op jit(solution)/shard_map/ppermute | solution.py:291
  133.4 20.7 %collective-permute-start.6 = (bf16[256,768]{1,0:T(8,128)(2,1)}, bf16[256,768]{1,0:T(8,128)(2,1)}, u32[]{:S(2)}, u32[]{:S(2)}) collective-permute-start(bf16[256,768]{1,0:T(8,128)(2,1)} %get-tuple-element.33.hidden_ref.h0), channel_id=1, source_target_pairs={{0,1},{1,0},{2,3},{3,2},{4,5},{5,4},{6,7},{7,6},{8,9},{9,8},{10,11... | collective-permute-start | bytes 1179656 | tf_op jit(solution)/shard_map/ppermute | solution.py:292
  135.7 22.0 %copy-start.4 = (bf16[256,768]{1,0:T(8,128)(2,1)S(1)}, bf16[256,768]{1,0:T(8,128)(2,1)}, u32[]{:S(2)}) copy-start(bf16[256,768]{1,0:T(8,128)(2,1)} %get-tuple-element.34.g0) | copy-start | bytes 1179652
  140.5 42.4 %copy-start = (bf16[256,768]{1,0:T(8,128)(2,1)S(1)}, bf16[256,768]{1,0:T(8,128)(2,1)}, u32[]{:S(2)}) copy-start(bf16[256,768]{1,0:T(8,128)(2,1)} %get-tuple-element.33.hidden_ref.h0) | copy-start | bytes 1179652
  140.5 42.4 %copy-start.2 = (bf16[1,512,768]{2,1,0:T(8,128)(2,1)S(1)}, bf16[1,512,768]{2,1,0:T(8,128)(2,1)}, u32[]{:S(2)}) copy-start(bf16[1,512,768]{2,1,0:T(8,128)(2,1)} %param.18) | copy-start | bytes 2359300
  140.5 42.3 %copy-start.3 = (bf16[1,768,512]{2,1,0:T(8,128)(2,1)S(1)}, bf16[1,768,512]{2,1,0:T(8,128)(2,1)}, u32[]{:S(2)}) copy-start(bf16[1,768,512]{2,1,0:T(8,128)(2,1)} %param.19) | copy-start | bytes 2359300
  154.1 34.2 %all-to-all-start.3 = ((bf16[16,4,16,512]{3,2,1,0:T(8,128)(2,1)}), bf16[16,4,16,512]{3,2,1,0:T(8,128)(2,1)S(1)}, u32[]{:S(2)}, u32[]{:S(2)}) async-start(bf16[16,4,16,512]{3,2,1,0:T(8,128)(2,1)} %expert_out.1), calls=%async_computation.3 | async-start | bytes 2097152 | tf_op jit(solution)/shard_map/all_to_all | solution.py:312
  157.8 21.2 %collective-permute-start.9 = (bf16[256,768]{1,0:T(8,128)(2,1)S(1)}, bf16[256,768]{1,0:T(8,128)(2,1)S(1)}, u32[]{:S(2)}, u32[]{:S(2)}) collective-permute-start(bf16[256,768]{1,0:T(8,128)(2,1)S(1)} %copy-done.4), channel_id=1, source_target_pairs={{0,2},{2,0},{1,3},{3,1},{4,6},{6,4},{5,7},{7,5},{8,10},{10,8},{9,1... | collective-permute-start | bytes 1179656 | tf_op jit(solution)/shard_map/ppermute | solution.py:294
  160.0 18.9 %collective-permute-start.10 = (bf16[256,768]{1,0:T(8,128)(2,1)}, bf16[256,768]{1,0:T(8,128)(2,1)S(1)}, u32[]{:S(2)}, u32[]{:S(2)}) collective-permute-start(bf16[256,768]{1,0:T(8,128)(2,1)} %collective-permute-done.7.h2), channel_id=1, source_target_pairs={{0,1},{1,0},{2,3},{3,2},{4,5},{5,4},{6,7},{7,6},{8,9},{9,8},{10,11... | collective-permute-start | bytes 1179656 | tf_op jit(solution)/shard_map/ppermute | solution.py:309
  178.9 3.9 collective-permute-start.11
  188.3 15.0 %copy-start.5 = (f32[192,256]{1,0:T(8,128)S(1)}, f32[192,256]{1,0:T(8,128)}, u32[]{:S(2)}) copy-start(f32[192,256]{1,0:T(8,128)} %get-tuple-element.41.share_ref) | copy-start | bytes 589828
  188.3 109.1 %all-to-all-start.2 = ((bf16[128,48,128]{2,1,0:T(8,128)(2,1)}), bf16[128,48,128]{2,1,0:T(8,128)(2,1)S(1)}, u32[]{:S(2)}, u32[]{:S(2)}) async-start(bf16[128,48,128]{2,1,0:T(8,128)(2,1)} %moments.1), calls=%async_computation.2 | async-start | bytes 3145728 | tf_op jit(solution)/shard_map/all_to_all | solution.py:346
  203.1 94.4 %copy-start.1 = (s32[128]{0:T(128)S(1)}, s32[128]{0:T(128)}, u32[]{:S(2)}) copy-start(s32[128]{0:T(128)} %partner_ref.1) | copy-start | bytes 1540
  203.1 78.3 %reduce-scatter.2.cloned.1.call-start = ((), (), s32[]{:S(2)}) async-start(), calls=%async_computation.7 | async-start | bytes 884736 | tf_op jit(solution)/shard_map/reduce_scatter | solution.py:344
Sparse Core Ops, SparseCore 0:
  10.1 61.8 all-gather.1
  207.3 73.9 reduce-scatter.1

commit v8 on v6

--- a/solution.py
+++ b/solution.py
@@ -6,6 +6,7 @@
 from jax.sharding import Mesh, PartitionSpec as P
 
 MOMENT_DECAY = 0.9
+GATHERED_COTS = 640
 AXES = ("yh", "zh", "zp", "x", "yl", "core")
 SLOT_AXES = ("yh", "zh", "zp", "x")
 GROUP_AXES = ("yh", "zp", "x")
@@ -49,7 +50,7 @@
     return copies
 
 
-def pack_kernel(tok_ref, ids_ref, weight_ref, holder_ref, out_ref):
+def pack_kernel(tok_ref, cot_ref, ids_ref, weight_ref, holder_ref, out_ref):
     top, rows = ids_ref.shape
     width = tok_ref.shape[1]
     experts = holder_ref.shape[1]
@@ -78,7 +79,8 @@
         for place, part in enumerate(parts):
             meta = jnp.where(meta_lane == (place + 1) * top + k, part[:, k : k + 1], meta)
     out_ref[:, :width] = tok_ref[...]
-    out_ref[:, width:] = meta.astype(BF16)
+    out_ref[:, width : width + 128] = meta.astype(BF16)
+    out_ref[:, width + 128 :] = cot_ref[:, :GATHERED_COTS]
 
 
 def select_kernel(plane_ref, gathered_ref, cots_ref, out_ref, share_ref):
@@ -90,7 +92,7 @@
     rows = targets * per_target
     block = total // (per_target // 2)
     plane = plane_ref[0]
-    meta = gathered_ref[:, width:].astype(F32)
+    meta = gathered_ref[:, width : width + 128].astype(F32)
     row = lax.broadcasted_iota(jnp.int32, (total, rows), 1)
     token = lax.broadcasted_iota(jnp.int32, (total, rows), 0)
     target = row >> 4
@@ -118,7 +120,10 @@
             picked_t, gathered_ref[:, at : at + quarter], preferred_element_type=F32
         ).astype(BF16)
         out_ref[:, q, :, :quarter] = sent.reshape(targets, per_target, quarter)
-        cot = cots_ref[:, at : at + quarter]
+        cut = min(max(GATHERED_COTS - at, 0), quarter)
+        near = gathered_ref[:, width + 128 + at : width + 128 + at + cut] if cut else None
+        far = cots_ref[:, at + cut - GATHERED_COTS : at + quarter - GATHERED_COTS] if cut < quarter else None
+        cot = near if far is None else far if near is None else jnp.concatenate([near, far], axis=1)
         grads = sum(jnp.dot(part, cot, preferred_element_type=F32) for part in shares_t)
         out_ref[:, q, :, quarter:] = grads.astype(BF16).reshape(targets, per_target, quarter)
 
@@ -247,15 +252,16 @@
     plane = lax.axis_index("zh").reshape(1).astype(jnp.int32)
     me = lax.axis_index(DP_AXES).reshape(1).astype(jnp.int32)
 
-    packed = call(pack_kernel, "pack", shape_of((24, 2176)), [VMEM] * 4, 10**6, 2 * 10**5)(
-        tokens, expert_ids.T, route_weight.T, holder.reshape(1, -1)
-    )
-    copies = jnp.broadcast_to(cotangent[None], (8,) + cotangent.shape)
+    packed = call(pack_kernel, "pack", shape_of((24, 2816)), [VMEM] * 5, 10**6, 2 * 10**5)(
+        tokens, cotangent, expert_ids.T, route_weight.T, holder.reshape(1, -1)
+    )
+    rest = cotangent[:, GATHERED_COTS:]
+    copies = jnp.broadcast_to(rest[None], (8,) + rest.shape)
     packed, copies, up0, down0 = lax.optimization_barrier(
         (packed, copies, up_weight[0], down_weight[0])
     )
     gathered = lax.all_gather(packed, "zh", axis=0, tiled=True)
-    cots = lax.all_to_all(copies, "zh", split_axis=0, concat_axis=0, tiled=True).reshape(192, 2048)
+    cots = lax.all_to_all(copies, "zh", split_axis=0, concat_axis=0, tiled=True).reshape(192, -1)
 
     up2, down2 = lax.ppermute(up0, "yl", FLIP), lax.ppermute(down0, "yl", FLIP)
     up1, down1 = lax.ppermute(up0, "core", FLIP), lax.ppermute(down0, "core", FLIP)

time: 415 us -> 394 us (0.949)
  blocking collectives: 152 us -> 123 us
  waiting for transfers between devices: 142 us -> 156 us
    all_gather x1 -> x0, blocking collectives: 35.9 us -> none  [body(): gathered = lax.all_gather(packed, 'zh', axis=0, tiled=True)]
    all_gather x0 -> x1, waiting for transfers between devices: none -> 11.9 us  [body(): gathered = lax.all_gather(packed, 'zh', axis=0, tiled=True)]
    all_to_all x1, blocking collectives: 31 us -> 37.3 us  [body(): lax.all_to_all(outgoing, GROUP_AXES, split_axis=0, concat_axis=0, tiled=T...]
  transfers between devices with their start and end apart: 14 -> 15, of which waited for: 7 -> 9; matrix products, arithmetic and copies ran while one was open for 0% -> 0% of each run, Pallas kernels for 5% -> 5%
where the time goes in v8:
time: 394 us; the launch traced here: 389 us
  waiting for transfers between devices  156 us (40%)
  blocking collectives  123 us (31%)
  starting transfers between devices  61.8 us (16%)
  Pallas kernels  28.5 us (7%)
  between operations  14.2 us (4%)
  local copies, waits for them, and re-layouts  5.59 us (1%)
    all_to_all x1, blocking collectives, body(): lax.all_to_all(chosen, SLOT_AXES, split_axis=0, concat_axis=0, tiled=True)  85.5 us
    reduce_scatter x1, waiting for transfers between devices, body(): layer_out = lax.psum_scatter(partial, 'zh', scatter_dimension=0, tiled=True)  77.3 us
    all_to_all x1, blocking collectives, body(): lax.all_to_all(outgoing, GROUP_AXES, split_axis=0, concat_axis=0, tiled=T...  37.3 us
    ppermute x1, waiting for transfers between devices, body(): acts2 = lax.ppermute(acts, 'yl', FLIP)  24 us
    all_to_all x1, starting transfers between devices, body(): lax.all_to_all(copies, 'zh', split_axis=0, concat_axis=0, tiled=True)  15.7 us
    all_gather x1, waiting for transfers between devices, body(): gathered = lax.all_gather(packed, 'zh', axis=0, tiled=True)  11.9 us
    ppermute x1, waiting for transfers between devices, body(): lax.ppermute(down0, 'yl', FLIP)  11.6 us
    all_to_all x1, waiting for transfers between devices, body(): lax.all_to_all(pieces, SLOT_AXES, split_axis=0, concat_axis=0, tiled=True)  11.3 us
  transfers between devices with their start and end apart: 15, of which 9 were waited for; matrix products, arithmetic and copies ran while one was open for 0% of the time, Pallas kernels for 5%

profile of v8, /device:TPU:1, one launch (start us, length us, event | category | flops | bytes accessed | tf_op | source)
XLA Modules:
  0.0 388.6 jit_solution(3872384319367260177)
XLA Ops:
  8.2 2.1 pack.1
  11.1 15.7 %all-to-all-start = ((bf16[8,24,1408]{2,1,0:T(8,128)(2,1)}), bf16[8,24,1408]{2,1,0:T(8,128)(2,1)}, u32[]{:S(2)}, u32[]{:S(2)}) async-start(bf16[8,24,1408]{2,1,0:T(8,128)(2,1)} %broadcast_in_dim.12), calls=%async_computation | async-start | bytes 1081344 | tf_op jit(solution)/shard_map/all_to_all | solution.py:264
  26.8 3.2 collective-permute-start.1
  30.0 2.1 collective-permute-start.4
  32.1 3.4 collective-permute-start
  35.5 1.9 collective-permute-start.3
  37.4 9.7 %collective-permute-done.1.refs_2_ = bf16[512,768]{1,0:T(8,128)(2,1)} collective-permute-done((bf16[512,768]{1,0:T(8,128)(2,1)}, bf16[512,768]{1,0:T(8,128)(2,1)}, u32[]{:S(2)}, u32[]{:S(2)}) %collective-permute-start.1) | collective-permute-done | bytes 786464 | tf_op jit(solution)/shard_map/ppermute | solution.py:266
  47.1 5.2 %collective-permute-start.2 = (bf16[512,768]{1,0:T(8,128)(2,1)}, bf16[512,768]{1,0:T(8,128)(2,1)}, u32[]{:S(2)}, u32[]{:S(2)}) collective-permute-start(bf16[512,768]{1,0:T(8,128)(2,1)} %collective-permute-done.1.refs_2_), channel_id=1, source_target_pairs={{0,1},{1,0},{2,3},{3,2},{4,5},{5,4},{6,7},{7,6},{8,9},{9,8},{10,11... | collective-permute-start | bytes 2359304 | tf_op jit(solution)/shard_map/ppermute | solution.py:268
  52.3 11.6 %collective-permute-done.4.refs_6_.refs_2_ = bf16[768,512]{1,0:T(8,128)(2,1)S(1)} collective-permute-done((bf16[768,512]{1,0:T(8,128)(2,1)S(1)}, bf16[768,512]{1,0:T(8,128)(2,1)S(1)}, u32[]{:S(2)}, u32[]{:S(2)}) %collective-permute-start.4) | collective-permute-done | bytes 786464 | tf_op jit(solution)/shard_map/ppermute | solution.py:266
  63.9 3.6 collective-permute-start.5
  67.6 2.0 collective-permute-done.5.refs_7_.refs_3_
  69.6 11.9 %all-gather.2.cloned.1.call-done.gathered_ref = bf16[192,2816]{1,0:T(8,128)(2,1)} async-done(((bf16[24,2816]{1,0:T(8,128)(2,1)}), bf16[192,2816]{1,0:T(8,128)(2,1)}) %all-gather.2.cloned.1.call-update) | async-done | bytes 1081360 | tf_op jit(solution)/shard_map/all_gather | solution.py:263
  81.6 4.8 %select.1 = (bf16[16,4,16,1024]{3,2,1,0:T(8,128)(2,1)}, f32[192,256]{1,0:T(8,128)}) custom-call(s32[1]{0:T(128)} %bitcast.1.plane_ref, bf16[192,2816]{1,0:T(8,128)(2,1)} %all-gather.2.cloned.1.call-done.gathered_ref, bf16[192,1408]{1,0:T(8,128)(2,1)} %bitcast.7.cots_ref), custom_call_target="tpu_custom_call" | custom-call | flops 1000000000 | bytes 4000000 | tf_op jit(solution)/shard_map/select/pallas_call | solution.py:274
  86.3 37.3 %all_to_all.30.rows_ref = bf16[16,4,16,1024]{3,2,1,0:T(8,128)(2,1)S(1)} all-to-all(bf16[16,4,16,1024]{3,2,1,0:T(8,128)(2,1)} %get-tuple-element.31), channel_id=1, replica_groups=mesh['yh'=2,'zh'=8,'zp'=2,'x'=4,'yl'=2,'core'=2] {'yh','zp','x'}, dimensions={0} | all-to-all | bytes 4194304 | tf_op jit(solution)/shard_map/all_to_all | solution.py:282
  123.7 1.6 copy.17
  125.7 6.7 %all-to-all-start.2 = ((bf16[4,16,16,1024]{3,2,1,0:T(8,128)(2,1)}), bf16[4,16,16,1024]{3,2,1,0:T(8,128)(2,1)}, u32[]{:S(2)}, u32[]{:S(2)}) async-start(bf16[4,16,16,1024]{3,2,1,0:T(8,128)(2,1)} %bitcast.14), calls=%async_computation.2 | async-start | bytes 4194304 | tf_op jit(solution)/shard_map/all_to_all | solution.py:283
  132.3 7.0 %forward.1.acts_ref.a0 = bf16[256,1536]{1,0:T(8,128)(2,1)} custom-call(s32[1]{0:T(128)} %bitcast.me_ref, bf16[16,4,16,1024]{3,2,1,0:T(8,128)(2,1)} %copy-done.2, bf16[512,768]{1,0:T(8,128)(2,1)} %bitcast.5.refs_0_, bf16[512,768]{1,0:T(8,128)(2,1)} %collective-permute-done.refs_1_, bf16[512,768]{1,0:T(8,128)(2,1)} %collective-permute-done.1.refs_2_, ...), custom_call_target="tpu_custom_call" | custom-call | flops 1600000000 | bytes 9000000 | tf_op jit(solution)/shard_map/forward/pallas_call | solution.py:287
  139.4 3.3 collective-permute-start.7
  142.7 2.5 collective-permute-start.6
  145.2 4.8 %expert_out.1 = bf16[16,4,16,512]{3,2,1,0:T(8,128)(2,1)} custom-call(s32[1]{0:T(128)} %bitcast.me_ref, bf16[256,1536]{1,0:T(8,128)(2,1)} %forward.1.acts_ref.a0, bf16[768,512]{1,0:T(8,128)(2,1)} %bitcast.16, bf16[768,512]{1,0:T(8,128)(2,1)} %copy-done.5, bf16[768,512]{1,0:T(8,128)(2,1)} %copy-done.4, bf16[768,512]{1,0:T(8,128)(2,1)} %collective-permute-done.5.refs_7_.refs_3_), custom_call_target="tpu_custom_call" | custom-call | flops 800000000 | bytes 5000000 | tf_op jit(solution)/shard_map/expert_out/pallas_call | solution.py:303
  150.0 24.0 %collective-permute-done.7.a2 = bf16[256,1536]{1,0:T(8,128)(2,1)S(1)} collective-permute-done((bf16[256,1536]{1,0:T(8,128)(2,1)}, bf16[256,1536]{1,0:T(8,128)(2,1)S(1)}, u32[]{:S(2)}, u32[]{:S(2)}) %collective-permute-start.7) | collective-permute-done | bytes 786464 | tf_op jit(solution)/shard_map/ppermute | solution.py:300
  174.9 3.7 all-to-all-start.4
  178.6 2.8 collective-permute-start.8
  181.4 1.9 collective-permute-done.8.a3
  184.1 6.0 %moments.1 = bf16[128,48,128]{2,1,0:T(8,128)(2,1)} custom-call(s32[1]{0:T(128)} %bitcast.me_ref, bf16[4,16,16,1024]{3,2,1,0:T(8,128)(2,1)} %all-to-all-done.2.rows_ref, bf16[256,1536]{1,0:T(8,128)(2,1)} %forward.1.acts_ref.a0, bf16[256,1536]{1,0:T(8,128)(2,1)} %copy-done.7, bf16[256,1536]{1,0:T(8,128)(2,1)} %copy-done.6, bf16[256,1536]{1,0:T(8,128)(2,1)} %copy-done.8, ...), custom_call_target="tpu_custom_call" | custom-call | flops 3200000000 | bytes 9000000 | tf_op jit(solution)/shard_map/moments/pallas_call | solution.py:321
  190.1 5.9 %all-to-all-done.4.returned_ref = bf16[16,4,16,512]{3,2,1,0:T(8,128)(2,1)S(1)} async-done(((bf16[16,4,16,512]{3,2,1,0:T(8,128)(2,1)}), bf16[16,4,16,512]{3,2,1,0:T(8,128)(2,1)S(1)}, u32[]{:S(2)}, u32[]{:S(2)}) %all-to-all-start.4) | async-done | bytes 1048608 | tf_op jit(solution)/shard_map/all_to_all | solution.py:317
  196.0 7.5 %all-to-all-start.3 = ((bf16[128,48,128]{2,1,0:T(8,128)(2,1)}), bf16[128,48,128]{2,1,0:T(8,128)(2,1)S(1)}, u32[]{:S(2)}, u32[]{:S(2)}) async-start(bf16[128,48,128]{2,1,0:T(8,128)(2,1)} %moments.1), calls=%async_computation.3 | async-start | bytes 3145728 | tf_op jit(solution)/shard_map/all_to_all | solution.py:337
  203.8 1.7 combine.1
  205.5 77.3 %reduce-scatter.2.cloned.1.call-done = bf16[24,2048]{1,0:T(8,128)(2,1)} async-done(((bf16[192,2048]{1,0:T(8,128)(2,1)}), bf16[24,2048]{1,0:T(8,128)(2,1)}) %reduce-scatter.2.cloned.1.call-update) | async-done | bytes 98320 | tf_op jit(solution)/shard_map/reduce_scatter | solution.py:335
  282.8 11.3 %all-to-all-done.3.spread_ref = bf16[128,48,128]{2,1,0:T(8,128)(2,1)S(1)} async-done(((bf16[128,48,128]{2,1,0:T(8,128)(2,1)}), bf16[128,48,128]{2,1,0:T(8,128)(2,1)S(1)}, u32[]{:S(2)}, u32[]{:S(2)}) %all-to-all-start.3) | async-done | bytes 1572896 | tf_op jit(solution)/shard_map/all_to_all | solution.py:337
  294.8 85.5 %all_to_all.31.pieces_ref = bf16[128,48,128]{2,1,0:T(8,128)(2,1)S(1)} all-to-all(bf16[128,48,128]{2,1,0:T(8,128)(2,1)S(1)} %pick.1), channel_id=1, replica_groups=mesh['yh'=2,'zh'=8,'zp'=2,'x'=4,'yl'=2,'core'=2] {'yh','zh','zp','x'}, dimensions={0} | all-to-all | bytes 3145728 | tf_op jit(solution)/shard_map/all_to_all | solution.py:342
  380.3 1.4 unpack.1
  (31 shorter events, 5.0 us)
Async XLA Ops:
  7.2 22.8 %copy-start.3 = (bf16[1,768,512]{2,1,0:T(8,128)(2,1)S(1)}, bf16[1,768,512]{2,1,0:T(8,128)(2,1)}, u32[]{:S(2)}) copy-start(bf16[1,768,512]{2,1,0:T(8,128)(2,1)} %param.17) | copy-start | bytes 2359300
  7.2 74.4 %all-gather.2.cloned.1.call-start = ((), (), s32[]{:S(2)}) async-start(), calls=%async_computation.7 | async-start | bytes 1216512 | tf_op jit(solution)/shard_map/all_gather | solution.py:263
  11.1 70.4 %all-to-all-start = ((bf16[8,24,1408]{2,1,0:T(8,128)(2,1)}), bf16[8,24,1408]{2,1,0:T(8,128)(2,1)}, u32[]{:S(2)}, u32[]{:S(2)}) async-start(bf16[8,24,1408]{2,1,0:T(8,128)(2,1)} %broadcast_in_dim.12), calls=%async_computation | async-start | bytes 1081344 | tf_op jit(solution)/shard_map/all_to_all | solution.py:264
  26.8 20.3 %collective-permute-start.1 = (bf16[512,768]{1,0:T(8,128)(2,1)}, bf16[512,768]{1,0:T(8,128)(2,1)}, u32[]{:S(2)}, u32[]{:S(2)}) collective-permute-start(bf16[512,768]{1,0:T(8,128)(2,1)} %bitcast.5.refs_0_), channel_id=1, source_target_pairs={{0,2},{2,0},{1,3},{3,1},{4,6},{6,4},{5,7},{7,5},{8,10},{10,8},{9,1... | collective-permute-start | bytes 2359304 | tf_op jit(solution)/shard_map/ppermute | solution.py:266
  30.0 34.0 %collective-permute-start.4 = (bf16[768,512]{1,0:T(8,128)(2,1)S(1)}, bf16[768,512]{1,0:T(8,128)(2,1)S(1)}, u32[]{:S(2)}, u32[]{:S(2)}) collective-permute-start(bf16[768,512]{1,0:T(8,128)(2,1)S(1)} %bitcast.17), channel_id=1, source_target_pairs={{0,2},{2,0},{1,3},{3,1},{4,6},{6,4},{5,7},{7,5},{8,10},{10,8},{9,1... | collective-permute-start | bytes 2359304 | tf_op jit(solution)/shard_map/ppermute | solution.py:266
  32.1 35.5 %collective-permute-start = (bf16[512,768]{1,0:T(8,128)(2,1)}, bf16[512,768]{1,0:T(8,128)(2,1)}, u32[]{:S(2)}, u32[]{:S(2)}) collective-permute-start(bf16[512,768]{1,0:T(8,128)(2,1)} %bitcast.5.refs_0_), channel_id=1, source_target_pairs={{0,1},{1,0},{2,3},{3,2},{4,5},{5,4},{6,7},{7,6},{8,9},{9,8},{10,11... | collective-permute-start | bytes 2359304 | tf_op jit(solution)/shard_map/ppermute | solution.py:267
  35.5 32.1 %collective-permute-start.3 = (bf16[768,512]{1,0:T(8,128)(2,1)S(1)}, bf16[768,512]{1,0:T(8,128)(2,1)S(1)}, u32[]{:S(2)}, u32[]{:S(2)}) collective-permute-start(bf16[768,512]{1,0:T(8,128)(2,1)S(1)} %bitcast.18), channel_id=1, source_target_pairs={{0,1},{1,0},{2,3},{3,2},{4,5},{5,4},{6,7},{7,6},{8,9},{9,8},{10,11... | collective-permute-start | bytes 2359304 | tf_op jit(solution)/shard_map/ppermute | solution.py:267
  47.1 20.6 %collective-permute-start.2 = (bf16[512,768]{1,0:T(8,128)(2,1)}, bf16[512,768]{1,0:T(8,128)(2,1)}, u32[]{:S(2)}, u32[]{:S(2)}) collective-permute-start(bf16[512,768]{1,0:T(8,128)(2,1)} %collective-permute-done.1.refs_2_), channel_id=1, source_target_pairs={{0,1},{1,0},{2,3},{3,2},{4,5},{5,4},{6,7},{7,6},{8,9},{9,8},{10,11... | collective-permute-start | bytes 2359304 | tf_op jit(solution)/shard_map/ppermute | solution.py:268
  63.9 22.4 %copy-start.4 = (bf16[768,512]{1,0:T(8,128)(2,1)}, bf16[768,512]{1,0:T(8,128)(2,1)S(1)}, u32[]{:S(2)}) copy-start(bf16[768,512]{1,0:T(8,128)(2,1)S(1)} %collective-permute-done.4.refs_6_.refs_2_) | copy-start | bytes 2359300
  63.9 5.7 %collective-permute-start.5 = (bf16[768,512]{1,0:T(8,128)(2,1)S(1)}, bf16[768,512]{1,0:T(8,128)(2,1)}, u32[]{:S(2)}, u32[]{:S(2)}) collective-permute-start(bf16[768,512]{1,0:T(8,128)(2,1)S(1)} %collective-permute-done.4.refs_6_.refs_2_), channel_id=1, source_target_pairs={{0,1},{1,0},{2,3},{3,2},{4,5},{5,4},{6,7},{7,6},{8,9},{9,8},{10,11... | collective-permute-start | bytes 2359304 | tf_op jit(solution)/shard_map/ppermute | solution.py:268
  67.6 2.0 copy-start.5
  123.7 2.0 copy-start.2
  125.7 48.4 %all-to-all-start.2 = ((bf16[4,16,16,1024]{3,2,1,0:T(8,128)(2,1)}), bf16[4,16,16,1024]{3,2,1,0:T(8,128)(2,1)}, u32[]{:S(2)}, u32[]{:S(2)}) async-start(bf16[4,16,16,1024]{3,2,1,0:T(8,128)(2,1)} %bitcast.14), calls=%async_computation.2 | async-start | bytes 4194304 | tf_op jit(solution)/shard_map/all_to_all | solution.py:283
  139.4 34.6 %collective-permute-start.7 = (bf16[256,1536]{1,0:T(8,128)(2,1)}, bf16[256,1536]{1,0:T(8,128)(2,1)S(1)}, u32[]{:S(2)}, u32[]{:S(2)}) collective-permute-start(bf16[256,1536]{1,0:T(8,128)(2,1)} %forward.1.acts_ref.a0), channel_id=1, source_target_pairs={{0,2},{2,0},{1,3},{3,1},{4,6},{6,4},{5,7},{7,5},{8,10},{10,8},{9,1... | collective-permute-start | bytes 2359304 | tf_op jit(solution)/shard_map/ppermute | solution.py:300
  142.7 31.3 %collective-permute-start.6 = (bf16[256,1536]{1,0:T(8,128)(2,1)}, bf16[256,1536]{1,0:T(8,128)(2,1)S(1)}, u32[]{:S(2)}, u32[]{:S(2)}) collective-permute-start(bf16[256,1536]{1,0:T(8,128)(2,1)} %forward.1.acts_ref.a0), channel_id=1, source_target_pairs={{0,1},{1,0},{2,3},{3,2},{4,5},{5,4},{6,7},{7,6},{8,9},{9,8},{10,11... | collective-permute-start | bytes 2359304 | tf_op jit(solution)/shard_map/ppermute | solution.py:301
  174.0 10.1 %copy-start.6 = (bf16[256,1536]{1,0:T(8,128)(2,1)}, bf16[256,1536]{1,0:T(8,128)(2,1)S(1)}, u32[]{:S(2)}) copy-start(bf16[256,1536]{1,0:T(8,128)(2,1)S(1)} %collective-permute-done.7.a2) | copy-start | bytes 2359300
  174.0 0.9 copy-start.7
  174.9 21.1 %all-to-all-start.4 = ((bf16[16,4,16,512]{3,2,1,0:T(8,128)(2,1)}), bf16[16,4,16,512]{3,2,1,0:T(8,128)(2,1)S(1)}, u32[]{:S(2)}, u32[]{:S(2)}) async-start(bf16[16,4,16,512]{3,2,1,0:T(8,128)(2,1)} %expert_out.1), calls=%async_computation.4 | async-start | bytes 2097152 | tf_op jit(solution)/shard_map/all_to_all | solution.py:317
  178.6 4.7 %collective-permute-start.8 = (bf16[256,1536]{1,0:T(8,128)(2,1)S(1)}, bf16[256,1536]{1,0:T(8,128)(2,1)S(1)}, u32[]{:S(2)}, u32[]{:S(2)}) collective-permute-start(bf16[256,1536]{1,0:T(8,128)(2,1)S(1)} %collective-permute-done.7.a2), channel_id=1, source_target_pairs={{0,1},{1,0},{2,3},{3,2},{4,5},{5,4},{6,7},{7,6},{8,9},{9,8},{10,11... | collective-permute-start | bytes 2359304 | tf_op jit(solution)/shard_map/ppermute | solution.py:316
  183.3 0.9 copy-start.8
  190.1 13.7 %copy-start.1 = (f32[192,256]{1,0:T(8,128)S(1)}, f32[192,256]{1,0:T(8,128)}, u32[]{:S(2)}) copy-start(f32[192,256]{1,0:T(8,128)} %get-tuple-element.41.share_ref) | copy-start | bytes 589828
  196.0 98.0 %all-to-all-start.3 = ((bf16[128,48,128]{2,1,0:T(8,128)(2,1)}), bf16[128,48,128]{2,1,0:T(8,128)(2,1)S(1)}, u32[]{:S(2)}, u32[]{:S(2)}) async-start(bf16[128,48,128]{2,1,0:T(8,128)(2,1)} %moments.1), calls=%async_computation.3 | async-start | bytes 3145728 | tf_op jit(solution)/shard_map/all_to_all | solution.py:337
  203.5 90.5 %copy-start = (s32[128]{0:T(128)S(1)}, s32[128]{0:T(128)}, u32[]{:S(2)}) copy-start(s32[128]{0:T(128)} %partner_ref.1) | copy-start | bytes 1540
  203.6 79.2 %reduce-scatter.2.cloned.1.call-start = ((), (), s32[]{:S(2)}) async-start(), calls=%async_computation.8 | async-start | bytes 884736 | tf_op jit(solution)/shard_map/reduce_scatter | solution.py:335
Sparse Core Ops, SparseCore 0:
  11.2 70.2 all-gather.1
  207.8 74.9 reduce-scatter.1

commit v9 on v4

--- a/solution.py
+++ b/solution.py
@@ -125,9 +125,10 @@
 
 
 def forward_kernel(me_ref, rows_ref, *refs):
-    sources, out_ref, ups, downs, sems = refs[:8], refs[8], refs[9], refs[10], refs[11]
+    sources, out_ref, sent_ref, ups, downs, sems = refs[:8], *refs[8:]
     copies = fetch(
-        [(sources[j + 4 * kind], held.at[j]) for j in range(4) for kind, held in ((0, ups), (1, downs))],
+        [(sources[j], ups.at[j]) for j in range(4)]
+        + [(sources[4 + j], downs.at[j]) for j in range(4)],
         sems,
     )
     targets, _, per_target, double = rows_ref.shape
@@ -136,30 +137,25 @@
     hidden_count = ups.shape[2]
     me = me_ref[0]
     preact = jnp.zeros((count, hidden_count), F32)
+    for j in range(4):
+        tok = rows_ref[:, me ^ j, :, :quarter].reshape(count, quarter)
+        copies[j].wait()
+        preact = preact + jnp.dot(tok, ups[j], preferred_element_type=F32)
+    sigmoid = 1.0 / (1.0 + jnp.exp(-preact))
+    hidden = (preact * sigmoid).astype(BF16)
+    slope = sigmoid * (1.0 + preact * (1.0 - sigmoid))
+    out_ref[:, :hidden_count] = hidden
     back = jnp.zeros((count, hidden_count), F32)
     for j in range(4):
-        both = rows_ref[:, me ^ j].reshape(count, double)
-        copies[2 * j].wait()
-        preact = preact + jnp.dot(both[:, :quarter], ups[j], preferred_element_type=F32)
-        copies[2 * j + 1].wait()
+        grad = rows_ref[:, me ^ j, :, quarter:].reshape(count, quarter)
+        copies[4 + j].wait()
         back = back + lax.dot_general(
-            both[:, quarter:], downs[j], (((1,), (1,)), ((), ())), preferred_element_type=F32
-        )
-    sigmoid = 1.0 / (1.0 + jnp.exp(-preact))
-    out_ref[:, :hidden_count] = (preact * sigmoid).astype(BF16)
-    out_ref[:, hidden_count:] = (back * sigmoid * (1.0 + preact * (1.0 - sigmoid))).astype(BF16)
-
-
-def expert_out_kernel(me_ref, acts_ref, *refs):
-    sources, out_ref, downs, sems = refs[:4], refs[4], refs[5], refs[6]
-    copies = fetch([(sources[j], downs.at[j]) for j in range(4)], sems)
-    targets, _, per_target, quarter = out_ref.shape
-    hidden = acts_ref[:, : downs.shape[1]]
-    me = me_ref[0]
-    for j in range(4):
-        copies[j].wait()
+            grad, downs[j], (((1,), (1,)), ((), ())), preferred_element_type=F32
+        )
+    out_ref[:, hidden_count:] = (back * slope).astype(BF16)
+    for j in range(4):
         part = jnp.dot(hidden, downs[j], preferred_element_type=F32).astype(BF16)
-        out_ref[:, me ^ j] = part.reshape(targets, per_target, quarter)
+        sent_ref[:, me ^ j] = part.reshape(targets, per_target, quarter)
 
 
 def combine_kernel(share_ref, returned_ref, out_ref):
@@ -271,17 +267,14 @@
         4 * 10**6,
     )(plane, gathered)
     rows = lax.all_to_all(outgoing, GROUP_AXES, split_axis=0, concat_axis=0, tiled=True)
-    by_feature = lax.all_to_all(
-        rows.transpose(1, 0, 2, 3), DP_AXES, split_axis=0, concat_axis=0, tiled=True
-    )
-
-    acts = call(
+
+    acts, expert_out = call(
         forward_kernel,
         "forward",
-        shape_of((256, 1536)),
+        (shape_of((256, 1536)), shape_of((16, 4, 16, 512))),
         [SMEM, VMEM] + [HBM] * 8,
-        16 * 10**8,
-        9 * 10**6,
+        24 * 10**8,
+        10**7,
         (
             pltpu.VMEM((4, 512, 768), BF16),
             pltpu.VMEM((4, 768, 512), BF16),
@@ -291,24 +284,17 @@
     acts2 = lax.ppermute(acts, "yl", FLIP)
     acts1 = lax.ppermute(acts, "core", FLIP)
 
-    expert_out = call(
-        expert_out_kernel,
-        "expert_out",
-        shape_of((16, 4, 16, 512)),
-        [SMEM, VMEM] + [HBM] * 4,
-        8 * 10**8,
-        5 * 10**6,
-        (pltpu.VMEM((4, 768, 512), BF16), pltpu.SemaphoreType.DMA((4,))),
-    )(me, acts, *downs)
-
-    by_feature, acts1, acts2, expert_out = lax.optimization_barrier(
-        (by_feature, acts1, acts2, expert_out)
-    )
+    returned = lax.all_to_all(expert_out, GROUP_AXES, split_axis=0, concat_axis=0, tiled=True)
+    turned_rows, returned, acts1 = lax.optimization_barrier(
+        (rows.transpose(1, 0, 2, 3), returned, acts1)
+    )
+    by_feature = lax.all_to_all(turned_rows, DP_AXES, split_axis=0, concat_axis=0, tiled=True)
     acts3 = lax.ppermute(acts2, "core", FLIP)
-    returned = lax.all_to_all(expert_out, GROUP_AXES, split_axis=0, concat_axis=0, tiled=True)
     partial = call(
         combine_kernel, "combine", shape_of((192, 2048)), [VMEM, VMEM], 6 * 10**8, 2 * 10**6, (), 12
     )(share, returned)
+    layer_out = lax.psum_scatter(partial, "zh", scatter_dimension=0, tiled=True)
+
     pieces = call(
         moment_kernel,
         "moments",
@@ -323,10 +309,9 @@
         ),
     )(me, by_feature, acts, acts1, acts2, acts3, up_moment[0], down_moment[0])
 
-    layer_out = lax.psum_scatter(partial, "zh", scatter_dimension=0, tiled=True)
-
+
+    pieces, layer_out = lax.optimization_barrier((pieces, layer_out))
     spread = lax.all_to_all(pieces, SLOT_AXES, split_axis=0, concat_axis=0, tiled=True)
-    spread, layer_out = lax.optimization_barrier((spread, layer_out))
     chosen = call(
         pick_kernel, "pick", shape_of((128, 48, 128)), [SMEM, VMEM], 0, 3 * 10**6, (), 12
     )(partner, spread)

time: 384 us -> 378 us (0.984)
  waiting for transfers between devices: 143 us -> 87.9 us
  blocking collectives: 118 us -> 173 us
    reduce_scatter x1, waiting for transfers between devices: 78.3 us -> 7.86 us  [body(): layer_out = lax.psum_scatter(partial, 'zh', scatter_dimension=0, tiled=True)]
    all_to_all x1, blocking collectives: 33.7 us -> 89.1 us  [body(): lax.all_to_all(pieces, SLOT_AXES, split_axis=0, concat_axis=0, tiled=True)]
    all_to_all x2, waiting for transfers between devices: 10.6 us -> 45.7 us  [the longest x1 28 us: body(): lax.all_to_all(outgoing, GROUP_AXES, split_axis=0, concat_axis=0, tiled=T...]
    ppermute x1, waiting for transfers between devices: 24 us -> 4.34 us  [body(): acts2 = lax.ppermute(acts, 'yl', FLIP)]
    pallas_call x2 -> x1, Pallas kernels: 11.8 us -> 8.5 us  [body(): call(forward_kernel, 'forward', (shape_of((256, 1536)), shape_of((16, 4,...]
  transfers between devices with their start and end apart: 14 -> 14, of which waited for: 9 -> 10; matrix products, arithmetic and copies ran while one was open for 0% -> 1% of each run, Pallas kernels for 5% -> 2%
where the time goes in v9:
time: 378 us; the launch traced here: 372 us
  blocking collectives  173 us (46%)
  waiting for transfers between devices  87.9 us (23%)
  starting transfers between devices  68.9 us (18%)
  Pallas kernels  25.2 us (7%)
  between operations  14.2 us (4%)
    all_to_all x1, blocking collectives, body(): lax.all_to_all(pieces, SLOT_AXES, split_axis=0, concat_axis=0, tiled=True)  89.1 us
    all_to_all x1, blocking collectives, body(): lax.all_to_all(chosen, SLOT_AXES, split_axis=0, concat_axis=0, tiled=True)  83.5 us
    all_to_all x1, waiting for transfers between devices, body(): lax.all_to_all(outgoing, GROUP_AXES, split_axis=0, concat_axis=0, tiled=T...  28 us
    all_gather x1, waiting for transfers between devices, body(): gathered = lax.all_gather(packed, 'zh', axis=0, tiled=True)  19.2 us
    all_to_all x1, waiting for transfers between devices, body(): lax.all_to_all(turned_rows, DP_AXES, split_axis=0, concat_axis=0, tiled=T...  17.7 us
    ppermute x1, starting transfers between devices, body(): lax.ppermute(up2, 'core', FLIP)  14.7 us
    all_to_all x1, starting transfers between devices, body(): lax.all_to_all(turned_rows, DP_AXES, split_axis=0, concat_axis=0, tiled=T...  9.02 us
    ppermute x1, starting transfers between devices, body(): lax.ppermute(up0, 'core', FLIP)  8.68 us
  transfers between devices with their start and end apart: 14, of which 10 were waited for; matrix products, arithmetic and copies ran while one was open for 1% of the time, Pallas kernels for 2%

profile of v9, /device:TPU:1, one launch (start us, length us, event | category | flops | bytes accessed | tf_op | source)
XLA Modules:
  0.0 372.0 jit_solution(8314851219014062535)
XLA Ops:
  7.2 2.1 pack.1
  9.4 4.0 %collective-permute-start.1 = (bf16[512,768]{1,0:T(8,128)(2,1)}, bf16[512,768]{1,0:T(8,128)(2,1)S(1)}, u32[]{:S(2)}, u32[]{:S(2)}) collective-permute-start(bf16[512,768]{1,0:T(8,128)(2,1)} %bitcast.17), channel_id=1, source_target_pairs={{0,2},{2,0},{1,3},{3,1},{4,6},{6,4},{5,7},{7,5},{8,10},{10,8},{9,1... | collective-permute-start | bytes 2359304 | tf_op jit(solution)/shard_map/ppermute | solution.py:253
  13.4 1.9 collective-permute-start.4
  15.3 8.7 %collective-permute-start = (bf16[512,768]{1,0:T(8,128)(2,1)}, bf16[512,768]{1,0:T(8,128)(2,1)S(1)}, u32[]{:S(2)}, u32[]{:S(2)}) collective-permute-start(bf16[512,768]{1,0:T(8,128)(2,1)} %bitcast.18), channel_id=1, source_target_pairs={{0,1},{1,0},{2,3},{3,2},{4,5},{5,4},{6,7},{7,6},{8,9},{9,8},{10,11... | collective-permute-start | bytes 2359304 | tf_op jit(solution)/shard_map/ppermute | solution.py:254
  24.0 1.9 collective-permute-start.3
  25.9 0.1 collective-permute-done.1.refs_2_
  26.0 14.7 %collective-permute-start.2 = (bf16[512,768]{1,0:T(8,128)(2,1)S(1)}, bf16[512,768]{1,0:T(8,128)(2,1)}, u32[]{:S(2)}, u32[]{:S(2)}) collective-permute-start(bf16[512,768]{1,0:T(8,128)(2,1)S(1)} %collective-permute-done.1.refs_2_), channel_id=1, source_target_pairs={{0,1},{1,0},{2,3},{3,2},{4,5},{5,4},{6,7},{7,6},{8,9},{9,8},{10,11... | collective-permute-start | bytes 2359304 | tf_op jit(solution)/shard_map/ppermute | solution.py:255
  40.7 2.2 collective-permute-done.4.refs_6_
  42.9 7.9 %collective-permute-start.5 = (bf16[768,512]{1,0:T(8,128)(2,1)S(1)}, bf16[768,512]{1,0:T(8,128)(2,1)}, u32[]{:S(2)}, u32[]{:S(2)}) collective-permute-start(bf16[768,512]{1,0:T(8,128)(2,1)S(1)} %collective-permute-done.4.refs_6_), channel_id=1, source_target_pairs={{0,1},{1,0},{2,3},{3,2},{4,5},{5,4},{6,7},{7,6},{8,9},{9,8},{10,11... | collective-permute-start | bytes 2359304 | tf_op jit(solution)/shard_map/ppermute | solution.py:255
  50.9 2.0 collective-permute-done.5.refs_7_
  52.9 19.2 %all-gather.2.cloned.1.call-done.gathered_ref = bf16[192,4224]{1,0:T(8,128)(2,1)} async-done(((bf16[24,4224]{1,0:T(8,128)(2,1)}), bf16[192,4224]{1,0:T(8,128)(2,1)}) %all-gather.2.cloned.1.call-update) | async-done | bytes 1622032 | tf_op jit(solution)/shard_map/all_gather | solution.py:250
  72.0 4.8 %select.1 = (bf16[16,4,16,1024]{3,2,1,0:T(8,128)(2,1)}, f32[192,256]{1,0:T(8,128)}) custom-call(s32[1]{0:T(128)} %bitcast.1.plane_ref, bf16[192,4224]{1,0:T(8,128)(2,1)} %all-gather.2.cloned.1.call-done.gathered_ref), custom_call_target="tpu_custom_call" | custom-call | flops 1000000000 | bytes 4000000 | tf_op jit(solution)/shard_map/select/pallas_call | solution.py:261
  76.8 7.1 %all-to-all-start = ((bf16[16,4,16,1024]{3,2,1,0:T(8,128)(2,1)}), bf16[16,4,16,1024]{3,2,1,0:T(8,128)(2,1)}, u32[]{:S(2)}, u32[]{:S(2)}) async-start(bf16[16,4,16,1024]{3,2,1,0:T(8,128)(2,1)} %get-tuple-element.22), calls=%async_computation | async-start | bytes 4194304 | tf_op jit(solution)/shard_map/all_to_all | solution.py:269
  83.9 28.0 %all-to-all-done.rows_ref = bf16[16,4,16,1024]{3,2,1,0:T(8,128)(2,1)} async-done(((bf16[16,4,16,1024]{3,2,1,0:T(8,128)(2,1)}), bf16[16,4,16,1024]{3,2,1,0:T(8,128)(2,1)}, u32[]{:S(2)}, u32[]{:S(2)}) %all-to-all-start) | async-done | bytes 2097184 | tf_op jit(solution)/shard_map/all_to_all | solution.py:269
  111.8 8.5 %forward.1 = (bf16[256,1536]{1,0:T(8,128)(2,1)}, bf16[16,4,16,512]{3,2,1,0:T(8,128)(2,1)}) custom-call(s32[1]{0:T(128)} %bitcast.me_ref, bf16[16,4,16,1024]{3,2,1,0:T(8,128)(2,1)} %all-to-all-done.rows_ref, bf16[512,768]{1,0:T(8,128)(2,1)} %bitcast.19, bf16[512,768]{1,0:T(8,128)(2,1)} %copy-done.4, bf16[512,768]{1,0:T(8,128)(2,1)} %copy-done.2, ...), custom_call_target="tpu_custom_call" | custom-call | flops 2400000000 | bytes 10000000 | tf_op jit(solution)/shard_map/forward/pallas_call | solution.py:271
  120.4 3.8 %all-to-all-start.1 = ((bf16[16,4,16,512]{3,2,1,0:T(8,128)(2,1)}), bf16[16,4,16,512]{3,2,1,0:T(8,128)(2,1)S(1)}, u32[]{:S(2)}, u32[]{:S(2)}) async-start(bf16[16,4,16,512]{3,2,1,0:T(8,128)(2,1)} %get-tuple-element.29), calls=%async_computation.1 | async-start | bytes 2097152 | tf_op jit(solution)/shard_map/all_to_all | solution.py:287
  124.2 5.3 %collective-permute-start.6 = (bf16[256,1536]{1,0:T(8,128)(2,1)S(1)}, bf16[256,1536]{1,0:T(8,128)(2,1)S(1)}, u32[]{:S(2)}, u32[]{:S(2)}) collective-permute-start(bf16[256,1536]{1,0:T(8,128)(2,1)S(1)} %copy-done.5), channel_id=1, source_target_pairs={{0,1},{1,0},{2,3},{3,2},{4,5},{5,4},{6,7},{7,6},{8,9},{9,8},{10,11... | collective-permute-start | bytes 2359304 | tf_op jit(solution)/shard_map/ppermute | solution.py:285
  129.5 1.9 collective-permute-start.7
  131.4 3.2 copy.17
  134.6 4.5 %all-to-all-done.1.returned_ref = bf16[16,4,16,512]{3,2,1,0:T(8,128)(2,1)S(1)} async-done(((bf16[16,4,16,512]{3,2,1,0:T(8,128)(2,1)}), bf16[16,4,16,512]{3,2,1,0:T(8,128)(2,1)S(1)}, u32[]{:S(2)}, u32[]{:S(2)}) %all-to-all-start.1) | async-done | bytes 1048608 | tf_op jit(solution)/shard_map/all_to_all | solution.py:287
  139.1 9.0 %all-to-all-start.2 = ((bf16[4,16,16,1024]{3,2,1,0:T(8,128)(2,1)}), bf16[4,16,16,1024]{3,2,1,0:T(8,128)(2,1)}, u32[]{:S(2)}, u32[]{:S(2)}) async-start(bf16[4,16,16,1024]{3,2,1,0:T(8,128)(2,1)} %bitcast.13), calls=%async_computation.2 | async-start | bytes 4194304 | tf_op jit(solution)/shard_map/all_to_all | solution.py:291
  148.1 1.7 combine.1
  149.8 4.3 %collective-permute-done.7.a2 = bf16[256,1536]{1,0:T(8,128)(2,1)} collective-permute-done((bf16[256,1536]{1,0:T(8,128)(2,1)S(1)}, bf16[256,1536]{1,0:T(8,128)(2,1)}, u32[]{:S(2)}, u32[]{:S(2)}) %collective-permute-start.7) | collective-permute-done | bytes 786464 | tf_op jit(solution)/shard_map/ppermute | solution.py:284
  154.1 2.6 collective-permute-start.8
  156.8 2.1 collective-permute-done.8.a3
  158.9 17.7 %all-to-all-done.2.rows_ref = bf16[4,16,16,1024]{3,2,1,0:T(8,128)(2,1)} async-done(((bf16[4,16,16,1024]{3,2,1,0:T(8,128)(2,1)}), bf16[4,16,16,1024]{3,2,1,0:T(8,128)(2,1)}, u32[]{:S(2)}, u32[]{:S(2)}) %all-to-all-start.2) | async-done | bytes 2097184 | tf_op jit(solution)/shard_map/all_to_all | solution.py:291
  176.6 6.0 %moments.1 = bf16[128,48,128]{2,1,0:T(8,128)(2,1)} custom-call(s32[1]{0:T(128)} %bitcast.me_ref, bf16[4,16,16,1024]{3,2,1,0:T(8,128)(2,1)} %all-to-all-done.2.rows_ref, bf16[256,1536]{1,0:T(8,128)(2,1)} %get-tuple-element.30.a0, bf16[256,1536]{1,0:T(8,128)(2,1)} %copy-done.6, bf16[256,1536]{1,0:T(8,128)(2,1)} %collective-permute-done.7.a2, ...), custom_call_target="tpu_custom_call" | custom-call | flops 3200000000 | bytes 9000000 | tf_op jit(solution)/shard_map/moments/pallas_call | solution.py:298
  182.6 7.9 %reduce-scatter.2.cloned.1.call-done = bf16[24,2048]{1,0:T(8,128)(2,1)} async-done(((bf16[192,2048]{1,0:T(8,128)(2,1)}), bf16[24,2048]{1,0:T(8,128)(2,1)}) %reduce-scatter.2.cloned.1.call-update) | async-done | bytes 98320 | tf_op jit(solution)/shard_map/reduce_scatter | solution.py:296
  190.5 89.1 %all_to_all.25.spread_ref = bf16[128,48,128]{2,1,0:T(8,128)(2,1)S(1)} all-to-all(bf16[128,48,128]{2,1,0:T(8,128)(2,1)} %moments.1), channel_id=1, replica_groups=mesh['yh'=2,'zh'=8,'zp'=2,'x'=4,'yl'=2,'core'=2] {'yh','zh','zp','x'}, dimensions={0} | all-to-all | bytes 3145728 | tf_op jit(solution)/shard_map/all_to_all | solution.py:314
  279.5 0.8 pick.1
  280.3 83.5 %all_to_all.26.pieces_ref = bf16[128,48,128]{2,1,0:T(8,128)(2,1)S(1)} all-to-all(bf16[128,48,128]{2,1,0:T(8,128)(2,1)S(1)} %pick.1), channel_id=1, replica_groups=mesh['yh'=2,'zh'=8,'zp'=2,'x'=4,'yl'=2,'core'=2] {'yh','zh','zp','x'}, dimensions={0} | all-to-all | bytes 3145728 | tf_op jit(solution)/shard_map/all_to_all | solution.py:318
  363.8 1.4 unpack.1
  (24 shorter events, 0.1 us)
Async XLA Ops:
  7.2 64.9 %all-gather.2.cloned.1.call-start = ((), (), s32[]{:S(2)}) async-start(), calls=%async_computation.6 | async-start | bytes 1824768 | tf_op jit(solution)/shard_map/all_gather | solution.py:250
  9.4 16.7 %collective-permute-start.1 = (bf16[512,768]{1,0:T(8,128)(2,1)}, bf16[512,768]{1,0:T(8,128)(2,1)S(1)}, u32[]{:S(2)}, u32[]{:S(2)}) collective-permute-start(bf16[512,768]{1,0:T(8,128)(2,1)} %bitcast.17), channel_id=1, source_target_pairs={{0,2},{2,0},{1,3},{3,1},{4,6},{6,4},{5,7},{7,5},{8,10},{10,8},{9,1... | collective-permute-start | bytes 2359304 | tf_op jit(solution)/shard_map/ppermute | solution.py:253
  13.4 29.5 %collective-permute-start.4 = (bf16[768,512]{1,0:T(8,128)(2,1)}, bf16[768,512]{1,0:T(8,128)(2,1)S(1)}, u32[]{:S(2)}, u32[]{:S(2)}) collective-permute-start(bf16[768,512]{1,0:T(8,128)(2,1)} %bitcast.20), channel_id=1, source_target_pairs={{0,2},{2,0},{1,3},{3,1},{4,6},{6,4},{5,7},{7,5},{8,10},{10,8},{9,1... | collective-permute-start | bytes 2359304 | tf_op jit(solution)/shard_map/ppermute | solution.py:253
  15.3 35.5 %collective-permute-start = (bf16[512,768]{1,0:T(8,128)(2,1)}, bf16[512,768]{1,0:T(8,128)(2,1)S(1)}, u32[]{:S(2)}, u32[]{:S(2)}) collective-permute-start(bf16[512,768]{1,0:T(8,128)(2,1)} %bitcast.18), channel_id=1, source_target_pairs={{0,1},{1,0},{2,3},{3,2},{4,5},{5,4},{6,7},{7,6},{8,9},{9,8},{10,11... | collective-permute-start | bytes 2359304 | tf_op jit(solution)/shard_map/ppermute | solution.py:254
  24.0 26.9 %collective-permute-start.3 = (bf16[768,512]{1,0:T(8,128)(2,1)}, bf16[768,512]{1,0:T(8,128)(2,1)}, u32[]{:S(2)}, u32[]{:S(2)}) collective-permute-start(bf16[768,512]{1,0:T(8,128)(2,1)} %bitcast.21), channel_id=1, source_target_pairs={{0,1},{1,0},{2,3},{3,2},{4,5},{5,4},{6,7},{7,6},{8,9},{9,8},{10,11... | collective-permute-start | bytes 2359304 | tf_op jit(solution)/shard_map/ppermute | solution.py:254
  26.0 50.8 %copy-start.2 = (bf16[512,768]{1,0:T(8,128)(2,1)}, bf16[512,768]{1,0:T(8,128)(2,1)S(1)}, u32[]{:S(2)}) copy-start(bf16[512,768]{1,0:T(8,128)(2,1)S(1)} %collective-permute-done.1.refs_2_) | copy-start | bytes 2359300
  26.0 24.9 %collective-permute-start.2 = (bf16[512,768]{1,0:T(8,128)(2,1)S(1)}, bf16[512,768]{1,0:T(8,128)(2,1)}, u32[]{:S(2)}, u32[]{:S(2)}) collective-permute-start(bf16[512,768]{1,0:T(8,128)(2,1)S(1)} %collective-permute-done.1.refs_2_), channel_id=1, source_target_pairs={{0,1},{1,0},{2,3},{3,2},{4,5},{5,4},{6,7},{7,6},{8,9},{9,8},{10,11... | collective-permute-start | bytes 2359304 | tf_op jit(solution)/shard_map/ppermute | solution.py:255
  42.9 33.9 %copy-start.3 = (bf16[768,512]{1,0:T(8,128)(2,1)}, bf16[768,512]{1,0:T(8,128)(2,1)S(1)}, u32[]{:S(2)}) copy-start(bf16[768,512]{1,0:T(8,128)(2,1)S(1)} %collective-permute-done.4.refs_6_) | copy-start | bytes 2359300
  42.9 10.0 %collective-permute-start.5 = (bf16[768,512]{1,0:T(8,128)(2,1)S(1)}, bf16[768,512]{1,0:T(8,128)(2,1)}, u32[]{:S(2)}, u32[]{:S(2)}) collective-permute-start(bf16[768,512]{1,0:T(8,128)(2,1)S(1)} %collective-permute-done.4.refs_6_), channel_id=1, source_target_pairs={{0,1},{1,0},{2,3},{3,2},{4,5},{5,4},{6,7},{7,6},{8,9},{9,8},{10,11... | collective-permute-start | bytes 2359304 | tf_op jit(solution)/shard_map/ppermute | solution.py:255
  50.9 2.0 copy-start.4
  76.8 35.0 %all-to-all-start = ((bf16[16,4,16,1024]{3,2,1,0:T(8,128)(2,1)}), bf16[16,4,16,1024]{3,2,1,0:T(8,128)(2,1)}, u32[]{:S(2)}, u32[]{:S(2)}) async-start(bf16[16,4,16,1024]{3,2,1,0:T(8,128)(2,1)} %get-tuple-element.22), calls=%async_computation | async-start | bytes 4194304 | tf_op jit(solution)/shard_map/all_to_all | solution.py:269
  120.4 3.8 %copy-start.5 = (bf16[256,1536]{1,0:T(8,128)(2,1)S(1)}, bf16[256,1536]{1,0:T(8,128)(2,1)}, u32[]{:S(2)}) copy-start(bf16[256,1536]{1,0:T(8,128)(2,1)} %get-tuple-element.30.a0) | copy-start | bytes 2359300
  120.4 18.7 %all-to-all-start.1 = ((bf16[16,4,16,512]{3,2,1,0:T(8,128)(2,1)}), bf16[16,4,16,512]{3,2,1,0:T(8,128)(2,1)S(1)}, u32[]{:S(2)}, u32[]{:S(2)}) async-start(bf16[16,4,16,512]{3,2,1,0:T(8,128)(2,1)} %get-tuple-element.29), calls=%async_computation.1 | async-start | bytes 2097152 | tf_op jit(solution)/shard_map/all_to_all | solution.py:287
  124.2 10.4 %collective-permute-start.6 = (bf16[256,1536]{1,0:T(8,128)(2,1)S(1)}, bf16[256,1536]{1,0:T(8,128)(2,1)S(1)}, u32[]{:S(2)}, u32[]{:S(2)}) collective-permute-start(bf16[256,1536]{1,0:T(8,128)(2,1)S(1)} %copy-done.5), channel_id=1, source_target_pairs={{0,1},{1,0},{2,3},{3,2},{4,5},{5,4},{6,7},{7,6},{8,9},{9,8},{10,11... | collective-permute-start | bytes 2359304 | tf_op jit(solution)/shard_map/ppermute | solution.py:285
  129.5 24.7 %collective-permute-start.7 = (bf16[256,1536]{1,0:T(8,128)(2,1)S(1)}, bf16[256,1536]{1,0:T(8,128)(2,1)}, u32[]{:S(2)}, u32[]{:S(2)}) collective-permute-start(bf16[256,1536]{1,0:T(8,128)(2,1)S(1)} %copy-done.5), channel_id=1, source_target_pairs={{0,2},{2,0},{1,3},{3,1},{4,6},{6,4},{5,7},{7,5},{8,10},{10,8},{9,1... | collective-permute-start | bytes 2359304 | tf_op jit(solution)/shard_map/ppermute | solution.py:284
  134.6 4.5 %copy-start.6 = (bf16[256,1536]{1,0:T(8,128)(2,1)}, bf16[256,1536]{1,0:T(8,128)(2,1)S(1)}, u32[]{:S(2)}) copy-start(bf16[256,1536]{1,0:T(8,128)(2,1)S(1)} %collective-permute-done.6.a1) | copy-start | bytes 2359300
  139.1 9.0 %copy-start.1 = (f32[192,256]{1,0:T(8,128)S(1)}, f32[192,256]{1,0:T(8,128)}, u32[]{:S(2)}) copy-start(f32[192,256]{1,0:T(8,128)} %get-tuple-element.33.share_ref) | copy-start | bytes 589828
  139.1 37.5 %all-to-all-start.2 = ((bf16[4,16,16,1024]{3,2,1,0:T(8,128)(2,1)}), bf16[4,16,16,1024]{3,2,1,0:T(8,128)(2,1)}, u32[]{:S(2)}, u32[]{:S(2)}) async-start(bf16[4,16,16,1024]{3,2,1,0:T(8,128)(2,1)} %bitcast.13), calls=%async_computation.2 | async-start | bytes 4194304 | tf_op jit(solution)/shard_map/all_to_all | solution.py:291
  148.1 42.4 %reduce-scatter.2.cloned.1.call-start = ((), (), s32[]{:S(2)}) async-start(), calls=%async_computation.7 | async-start | bytes 884736 | tf_op jit(solution)/shard_map/reduce_scatter | solution.py:296
  154.1 4.7 %collective-permute-start.8 = (bf16[256,1536]{1,0:T(8,128)(2,1)}, bf16[256,1536]{1,0:T(8,128)(2,1)S(1)}, u32[]{:S(2)}, u32[]{:S(2)}) collective-permute-start(bf16[256,1536]{1,0:T(8,128)(2,1)} %collective-permute-done.7.a2), channel_id=1, source_target_pairs={{0,1},{1,0},{2,3},{3,2},{4,5},{5,4},{6,7},{7,6},{8,9},{9,8},{10,11... | collective-permute-start | bytes 2359304 | tf_op jit(solution)/shard_map/ppermute | solution.py:292
  158.9 17.7 %copy-start.7 = (bf16[256,1536]{1,0:T(8,128)(2,1)}, bf16[256,1536]{1,0:T(8,128)(2,1)S(1)}, u32[]{:S(2)}) copy-start(bf16[256,1536]{1,0:T(8,128)(2,1)S(1)} %collective-permute-done.8.a3) | copy-start | bytes 2359300
  182.6 96.9 %copy-start = (s32[128]{0:T(128)S(1)}, s32[128]{0:T(128)}, u32[]{:S(2)}) copy-start(s32[128]{0:T(128)} %partner_ref.1) | copy-start | bytes 1540
Sparse Core Ops, SparseCore 0:
  10.1 61.9 all-gather.1
  152.3 38.0 reduce-scatter.1

commit v10 on v9

--- a/solution.py
+++ b/solution.py
@@ -125,7 +125,7 @@
 
 
 def forward_kernel(me_ref, rows_ref, *refs):
-    sources, out_ref, sent_ref, ups, downs, sems = refs[:8], *refs[8:]
+    sources, hidden_ref, slope_ref, sent_ref, ups, downs, sems = refs[:8], *refs[8:]
     copies = fetch(
         [(sources[j], ups.at[j]) for j in range(4)]
         + [(sources[4 + j], downs.at[j]) for j in range(4)],
@@ -134,28 +134,38 @@
     targets, _, per_target, double = rows_ref.shape
     quarter = double // 2
     count = targets * per_target
-    hidden_count = ups.shape[2]
     me = me_ref[0]
-    preact = jnp.zeros((count, hidden_count), F32)
+    preact = jnp.zeros((count, ups.shape[2]), F32)
     for j in range(4):
         tok = rows_ref[:, me ^ j, :, :quarter].reshape(count, quarter)
         copies[j].wait()
         preact = preact + jnp.dot(tok, ups[j], preferred_element_type=F32)
     sigmoid = 1.0 / (1.0 + jnp.exp(-preact))
     hidden = (preact * sigmoid).astype(BF16)
-    slope = sigmoid * (1.0 + preact * (1.0 - sigmoid))
-    out_ref[:, :hidden_count] = hidden
+    hidden_ref[...] = hidden
+    slope_ref[...] = sigmoid * (1.0 + preact * (1.0 - sigmoid))
+    for j in range(4):
+        copies[4 + j].wait()
+        part = jnp.dot(hidden, downs[j], preferred_element_type=F32).astype(BF16)
+        sent_ref[:, me ^ j] = part.reshape(targets, per_target, quarter)
+
+
+def back_kernel(me_ref, rows_ref, hidden_ref, slope_ref, *refs):
+    sources, out_ref, downs, sems = refs[:4], *refs[4:]
+    copies = fetch([(sources[j], downs.at[j]) for j in range(4)], sems)
+    targets, _, per_target, double = rows_ref.shape
+    quarter = double // 2
+    count, hidden_count = slope_ref.shape
+    me = me_ref[0]
     back = jnp.zeros((count, hidden_count), F32)
     for j in range(4):
         grad = rows_ref[:, me ^ j, :, quarter:].reshape(count, quarter)
-        copies[4 + j].wait()
+        copies[j].wait()
         back = back + lax.dot_general(
             grad, downs[j], (((1,), (1,)), ((), ())), preferred_element_type=F32
         )
-    out_ref[:, hidden_count:] = (back * slope).astype(BF16)
-    for j in range(4):
-        part = jnp.dot(hidden, downs[j], preferred_element_type=F32).astype(BF16)
-        sent_ref[:, me ^ j] = part.reshape(targets, per_target, quarter)
+    out_ref[:, :hidden_count] = hidden_ref[...]
+    out_ref[:, hidden_count:] = (back * slope_ref[...]).astype(BF16)
 
 
 def combine_kernel(share_ref, returned_ref, out_ref):
@@ -268,12 +278,12 @@
     )(plane, gathered)
     rows = lax.all_to_all(outgoing, GROUP_AXES, split_axis=0, concat_axis=0, tiled=True)
 
-    acts, expert_out = call(
+    hidden, slope, expert_out = call(
         forward_kernel,
         "forward",
-        (shape_of((256, 1536)), shape_of((16, 4, 16, 512))),
+        (shape_of((256, 768)), shape_of((256, 768), F32), shape_of((16, 4, 16, 512))),
         [SMEM, VMEM] + [HBM] * 8,
-        24 * 10**8,
+        16 * 10**8,
         10**7,
         (
             pltpu.VMEM((4, 512, 768), BF16),
@@ -281,6 +291,15 @@
             pltpu.SemaphoreType.DMA((8,)),
         ),
     )(me, rows, *ups, *downs)
+    acts = call(
+        back_kernel,
+        "back",
+        shape_of((256, 1536)),
+        [SMEM, VMEM, VMEM, VMEM] + [HBM] * 4,
+        8 * 10**8,
+        6 * 10**6,
+        (pltpu.VMEM((4, 768, 512), BF16), pltpu.SemaphoreType.DMA((4,))),
+    )(me, rows, hidden, slope, *downs)
     acts2 = lax.ppermute(acts, "yl", FLIP)
     acts1 = lax.ppermute(acts, "core", FLIP)
 

time: 378 us -> 379 us (level)
  Pallas kernels: 25.2 us -> 29.5 us
    all_to_all x1, waiting for transfers between devices: 4.47 us -> 0.01 us  [body(): lax.all_to_all(expert_out, GROUP_AXES, split_axis=0, concat_axis=0, tiled...]
    pallas_call x1 -> x2, Pallas kernels: 8.5 us -> 12.8 us  [the longest x1 7.16 us: body(): call(forward_kernel, 'forward', (shape_of((256, 768)), shape_of((256, 768...]
  transfers between devices with their start and end apart: 14 -> 14, of which waited for: 10 -> 9; matrix products, arithmetic and copies ran while one was open for 1% -> 1% of each run, Pallas kernels for 2% -> 4%
where the time goes in v10:
time: 379 us; the launch traced here: 372 us
  blocking collectives  170 us (45%)
  waiting for transfers between devices  85.9 us (23%)
  starting transfers between devices  67 us (18%)
  Pallas kernels  29.5 us (8%)
  between operations  14.2 us (4%)
  local copies, waits for them, and re-layouts  4.98 us (1%)
    all_to_all x1, blocking collectives, body(): lax.all_to_all(pieces, SLOT_AXES, split_axis=0, concat_axis=0, tiled=True)  86.8 us
    all_to_all x1, blocking collectives, body(): lax.all_to_all(chosen, SLOT_AXES, split_axis=0, concat_axis=0, tiled=True)  83.1 us
    all_to_all x1, waiting for transfers between devices, body(): lax.all_to_all(outgoing, GROUP_AXES, split_axis=0, concat_axis=0, tiled=T...  27.9 us
    all_gather x1, waiting for transfers between devices, body(): gathered = lax.all_gather(packed, 'zh', axis=0, tiled=True)  18.4 us
    all_to_all x1, waiting for transfers between devices, body(): lax.all_to_all(turned_rows, DP_AXES, split_axis=0, concat_axis=0, tiled=T...  17.5 us
    ppermute x1, starting transfers between devices, body(): lax.ppermute(up2, 'core', FLIP)  14.8 us
    reduce_scatter x1, waiting for transfers between devices, body(): layer_out = lax.psum_scatter(partial, 'zh', scatter_dimension=0, tiled=True)  8.85 us
    ppermute x1, starting transfers between devices, body(): lax.ppermute(up0, 'core', FLIP)  8.68 us
  transfers between devices with their start and end apart: 14, of which 9 were waited for; matrix products, arithmetic and copies ran while one was open for 1% of the time, Pallas kernels for 4%

profile of v10, /device:TPU:1, one launch (start us, length us, event | category | flops | bytes accessed | tf_op | source)
XLA Modules:
  0.0 371.6 jit_solution(10312829732021808077)
XLA Ops:
  7.2 2.1 pack.1
  9.3 4.0 %collective-permute-start.1 = (bf16[512,768]{1,0:T(8,128)(2,1)}, bf16[512,768]{1,0:T(8,128)(2,1)}, u32[]{:S(2)}, u32[]{:S(2)}) collective-permute-start(bf16[512,768]{1,0:T(8,128)(2,1)} %bitcast.19), channel_id=1, source_target_pairs={{0,2},{2,0},{1,3},{3,1},{4,6},{6,4},{5,7},{7,5},{8,10},{10,8},{9,1... | collective-permute-start | bytes 2359304 | tf_op jit(solution)/shard_map/ppermute | solution.py:263
  13.4 1.9 collective-permute-start.4
  15.3 8.7 %collective-permute-start = (bf16[512,768]{1,0:T(8,128)(2,1)}, bf16[512,768]{1,0:T(8,128)(2,1)}, u32[]{:S(2)}, u32[]{:S(2)}) collective-permute-start(bf16[512,768]{1,0:T(8,128)(2,1)} %bitcast.20), channel_id=1, source_target_pairs={{0,1},{1,0},{2,3},{3,2},{4,5},{5,4},{6,7},{7,6},{8,9},{9,8},{10,11... | collective-permute-start | bytes 2359304 | tf_op jit(solution)/shard_map/ppermute | solution.py:264
  24.0 1.9 collective-permute-start.3
  26.0 14.8 %collective-permute-start.2 = (bf16[512,768]{1,0:T(8,128)(2,1)}, bf16[512,768]{1,0:T(8,128)(2,1)}, u32[]{:S(2)}, u32[]{:S(2)}) collective-permute-start(bf16[512,768]{1,0:T(8,128)(2,1)} %collective-permute-done.1.refs_2_), channel_id=1, source_target_pairs={{0,1},{1,0},{2,3},{3,2},{4,5},{5,4},{6,7},{7,6},{8,9},{9,8},{10,11... | collective-permute-start | bytes 2359304 | tf_op jit(solution)/shard_map/ppermute | solution.py:265
  40.8 2.1 collective-permute-done.4.refs_6_.refs_2_
  42.9 7.9 %collective-permute-start.5 = (bf16[768,512]{1,0:T(8,128)(2,1)S(1)}, bf16[768,512]{1,0:T(8,128)(2,1)S(1)}, u32[]{:S(2)}, u32[]{:S(2)}) collective-permute-start(bf16[768,512]{1,0:T(8,128)(2,1)S(1)} %collective-permute-done.4.refs_6_.refs_2_), channel_id=1, source_target_pairs={{0,1},{1,0},{2,3},{3,2},{4,5},{5,4},{6,7},{7,6},{8,9},{9,8},{10,11... | collective-permute-start | bytes 2359304 | tf_op jit(solution)/shard_map/ppermute | solution.py:265
  50.9 1.8 collective-permute-done.5.refs_7_.refs_3_
  52.7 0.9 copy-done.4
  53.6 18.4 %all-gather.2.cloned.1.call-done.gathered_ref = bf16[192,4224]{1,0:T(8,128)(2,1)} async-done(((bf16[24,4224]{1,0:T(8,128)(2,1)}), bf16[192,4224]{1,0:T(8,128)(2,1)}) %all-gather.2.cloned.1.call-update) | async-done | bytes 1622032 | tf_op jit(solution)/shard_map/all_gather | solution.py:260
  72.0 4.8 %select.1 = (bf16[16,4,16,1024]{3,2,1,0:T(8,128)(2,1)}, f32[192,256]{1,0:T(8,128)}) custom-call(s32[1]{0:T(128)} %bitcast.1.plane_ref, bf16[192,4224]{1,0:T(8,128)(2,1)} %all-gather.2.cloned.1.call-done.gathered_ref), custom_call_target="tpu_custom_call" | custom-call | flops 1000000000 | bytes 4000000 | tf_op jit(solution)/shard_map/select/pallas_call | solution.py:271
  76.8 7.0 %all-to-all-start = ((bf16[16,4,16,1024]{3,2,1,0:T(8,128)(2,1)}), bf16[16,4,16,1024]{3,2,1,0:T(8,128)(2,1)}, u32[]{:S(2)}, u32[]{:S(2)}) async-start(bf16[16,4,16,1024]{3,2,1,0:T(8,128)(2,1)} %get-tuple-element.23), calls=%async_computation | async-start | bytes 4194304 | tf_op jit(solution)/shard_map/all_to_all | solution.py:279
  83.9 27.9 %all-to-all-done.rows_ref = bf16[16,4,16,1024]{3,2,1,0:T(8,128)(2,1)} async-done(((bf16[16,4,16,1024]{3,2,1,0:T(8,128)(2,1)}), bf16[16,4,16,1024]{3,2,1,0:T(8,128)(2,1)}, u32[]{:S(2)}, u32[]{:S(2)}) %all-to-all-start) | async-done | bytes 2097184 | tf_op jit(solution)/shard_map/all_to_all | solution.py:279
  111.8 7.2 %forward.1 = (bf16[256,768]{1,0:T(8,128)(2,1)}, f32[256,768]{1,0:T(8,128)}, bf16[16,4,16,512]{3,2,1,0:T(8,128)(2,1)}) custom-call(s32[1]{0:T(128)} %bitcast.me_ref, bf16[16,4,16,1024]{3,2,1,0:T(8,128)(2,1)} %all-to-all-done.rows_ref, bf16[512,768]{1,0:T(8,128)(2,1)} %bitcast.21, bf16[512,768]{1,0:T(8,128)(2,1)} %collective-permute-done.refs_1_, ...), custom_call_target="tpu_custom_call" | custom-call | flops 1600000000 | bytes 10000000 | tf_op jit(solution)/shard_map/forward/pallas_call | solution.py:281
  119.0 3.7 all-to-all-start.1
  122.6 5.7 %back.1.a0 = bf16[256,1536]{1,0:T(8,128)(2,1)} custom-call(s32[1]{0:T(128)} %bitcast.me_ref, bf16[16,4,16,1024]{3,2,1,0:T(8,128)(2,1)} %all-to-all-done.rows_ref, bf16[256,768]{1,0:T(8,128)(2,1)} %get-tuple-element.31.hidden_ref, f32[256,768]{1,0:T(8,128)} %get-tuple-element.32.slope_ref, bf16[768,512]{1,0:T(8,128)(2,1)} %bitcast.18, ...), custom_call_target="tpu_custom_call" | custom-call | flops 800000000 | bytes 6000000 | tf_op jit(solution)/shard_map/back/pallas_call | solution.py:294
  128.3 5.3 %collective-permute-start.6 = (bf16[256,1536]{1,0:T(8,128)(2,1)}, bf16[256,1536]{1,0:T(8,128)(2,1)S(1)}, u32[]{:S(2)}, u32[]{:S(2)}) collective-permute-start(bf16[256,1536]{1,0:T(8,128)(2,1)} %back.1.a0), channel_id=1, source_target_pairs={{0,1},{1,0},{2,3},{3,2},{4,5},{5,4},{6,7},{7,6},{8,9},{9,8},{10,11... | collective-permute-start | bytes 2359304 | tf_op jit(solution)/shard_map/ppermute | solution.py:304
  133.6 1.9 collective-permute-start.7
  135.5 3.2 copy.18
  138.8 0.9 copy-done.5
  139.6 6.9 %all-to-all-start.2 = ((bf16[4,16,16,1024]{3,2,1,0:T(8,128)(2,1)}), bf16[4,16,16,1024]{3,2,1,0:T(8,128)(2,1)}, u32[]{:S(2)}, u32[]{:S(2)}) async-start(bf16[4,16,16,1024]{3,2,1,0:T(8,128)(2,1)} %bitcast.14), calls=%async_computation.2 | async-start | bytes 4194304 | tf_op jit(solution)/shard_map/all_to_all | solution.py:310
  146.6 1.7 combine.1
  148.3 7.0 %collective-permute-done.7.a2 = bf16[256,1536]{1,0:T(8,128)(2,1)} collective-permute-done((bf16[256,1536]{1,0:T(8,128)(2,1)}, bf16[256,1536]{1,0:T(8,128)(2,1)}, u32[]{:S(2)}, u32[]{:S(2)}) %collective-permute-start.7) | collective-permute-done | bytes 786464 | tf_op jit(solution)/shard_map/ppermute | solution.py:303
  155.3 2.8 collective-permute-start.8
  158.1 2.1 collective-permute-done.8.a3
  160.2 17.5 %all-to-all-done.2.rows_ref = bf16[4,16,16,1024]{3,2,1,0:T(8,128)(2,1)} async-done(((bf16[4,16,16,1024]{3,2,1,0:T(8,128)(2,1)}), bf16[4,16,16,1024]{3,2,1,0:T(8,128)(2,1)}, u32[]{:S(2)}, u32[]{:S(2)}) %all-to-all-start.2) | async-done | bytes 2097184 | tf_op jit(solution)/shard_map/all_to_all | solution.py:310
  177.8 6.0 %moments.1 = bf16[128,48,128]{2,1,0:T(8,128)(2,1)} custom-call(s32[1]{0:T(128)} %bitcast.me_ref, bf16[4,16,16,1024]{3,2,1,0:T(8,128)(2,1)} %all-to-all-done.2.rows_ref, bf16[256,1536]{1,0:T(8,128)(2,1)} %back.1.a0, bf16[256,1536]{1,0:T(8,128)(2,1)} %copy-done.5, bf16[256,1536]{1,0:T(8,128)(2,1)} %collective-permute-done.7.a2, bf16[256,1536]{1,0:T(8,128)(2,1)} %copy-done.6, ...), custom_call_target="tpu_custom_call" | custom-call | flops 3200000000 | bytes 9000000 | tf_op jit(solution)/shard_map/moments/pallas_call | solution.py:317
  183.8 8.8 %reduce-scatter.2.cloned.1.call-done = bf16[24,2048]{1,0:T(8,128)(2,1)} async-done(((bf16[192,2048]{1,0:T(8,128)(2,1)}), bf16[24,2048]{1,0:T(8,128)(2,1)}) %reduce-scatter.2.cloned.1.call-update) | async-done | bytes 98320 | tf_op jit(solution)/shard_map/reduce_scatter | solution.py:315
  192.6 86.8 %all_to_all.25.spread_ref = bf16[128,48,128]{2,1,0:T(8,128)(2,1)S(1)} all-to-all(bf16[128,48,128]{2,1,0:T(8,128)(2,1)} %moments.1), channel_id=1, replica_groups=mesh['yh'=2,'zh'=8,'zp'=2,'x'=4,'yl'=2,'core'=2] {'yh','zh','zp','x'}, dimensions={0} | all-to-all | bytes 3145728 | tf_op jit(solution)/shard_map/all_to_all | solution.py:333
  280.2 83.1 %all_to_all.26.pieces_ref = bf16[128,48,128]{2,1,0:T(8,128)(2,1)S(1)} all-to-all(bf16[128,48,128]{2,1,0:T(8,128)(2,1)S(1)} %pick.1), channel_id=1, replica_groups=mesh['yh'=2,'zh'=8,'zp'=2,'x'=4,'yl'=2,'core'=2] {'yh','zh','zp','x'}, dimensions={0} | all-to-all | bytes 3145728 | tf_op jit(solution)/shard_map/all_to_all | solution.py:337
  363.3 1.4 unpack.1
  (23 shorter events, 1.0 us)
Async XLA Ops:
  7.2 64.9 %all-gather.2.cloned.1.call-start = ((), (), s32[]{:S(2)}) async-start(), calls=%async_computation.6 | async-start | bytes 1824768 | tf_op jit(solution)/shard_map/all_gather | solution.py:260
  9.3 16.7 %collective-permute-start.1 = (bf16[512,768]{1,0:T(8,128)(2,1)}, bf16[512,768]{1,0:T(8,128)(2,1)}, u32[]{:S(2)}, u32[]{:S(2)}) collective-permute-start(bf16[512,768]{1,0:T(8,128)(2,1)} %bitcast.19), channel_id=1, source_target_pairs={{0,2},{2,0},{1,3},{3,1},{4,6},{6,4},{5,7},{7,5},{8,10},{10,8},{9,1... | collective-permute-start | bytes 2359304 | tf_op jit(solution)/shard_map/ppermute | solution.py:263
  13.4 29.5 %collective-permute-start.4 = (bf16[768,512]{1,0:T(8,128)(2,1)}, bf16[768,512]{1,0:T(8,128)(2,1)S(1)}, u32[]{:S(2)}, u32[]{:S(2)}) collective-permute-start(bf16[768,512]{1,0:T(8,128)(2,1)} %bitcast.15), channel_id=1, source_target_pairs={{0,2},{2,0},{1,3},{3,1},{4,6},{6,4},{5,7},{7,5},{8,10},{10,8},{9,1... | collective-permute-start | bytes 2359304 | tf_op jit(solution)/shard_map/ppermute | solution.py:263
  15.3 35.5 %collective-permute-start = (bf16[512,768]{1,0:T(8,128)(2,1)}, bf16[512,768]{1,0:T(8,128)(2,1)}, u32[]{:S(2)}, u32[]{:S(2)}) collective-permute-start(bf16[512,768]{1,0:T(8,128)(2,1)} %bitcast.20), channel_id=1, source_target_pairs={{0,1},{1,0},{2,3},{3,2},{4,5},{5,4},{6,7},{7,6},{8,9},{9,8},{10,11... | collective-permute-start | bytes 2359304 | tf_op jit(solution)/shard_map/ppermute | solution.py:264
  24.0 26.9 %collective-permute-start.3 = (bf16[768,512]{1,0:T(8,128)(2,1)}, bf16[768,512]{1,0:T(8,128)(2,1)S(1)}, u32[]{:S(2)}, u32[]{:S(2)}) collective-permute-start(bf16[768,512]{1,0:T(8,128)(2,1)} %bitcast.16), channel_id=1, source_target_pairs={{0,1},{1,0},{2,3},{3,2},{4,5},{5,4},{6,7},{7,6},{8,9},{9,8},{10,11... | collective-permute-start | bytes 2359304 | tf_op jit(solution)/shard_map/ppermute | solution.py:264
  26.0 24.9 %collective-permute-start.2 = (bf16[512,768]{1,0:T(8,128)(2,1)}, bf16[512,768]{1,0:T(8,128)(2,1)}, u32[]{:S(2)}, u32[]{:S(2)}) collective-permute-start(bf16[512,768]{1,0:T(8,128)(2,1)} %collective-permute-done.1.refs_2_), channel_id=1, source_target_pairs={{0,1},{1,0},{2,3},{3,2},{4,5},{5,4},{6,7},{7,6},{8,9},{9,8},{10,11... | collective-permute-start | bytes 2359304 | tf_op jit(solution)/shard_map/ppermute | solution.py:265
  42.9 33.9 %copy-start.2 = (bf16[768,512]{1,0:T(8,128)(2,1)}, bf16[768,512]{1,0:T(8,128)(2,1)S(1)}, u32[]{:S(2)}) copy-start(bf16[768,512]{1,0:T(8,128)(2,1)S(1)} %collective-permute-done.4.refs_6_.refs_2_) | copy-start | bytes 2359300
  42.9 9.8 %collective-permute-start.5 = (bf16[768,512]{1,0:T(8,128)(2,1)S(1)}, bf16[768,512]{1,0:T(8,128)(2,1)S(1)}, u32[]{:S(2)}, u32[]{:S(2)}) collective-permute-start(bf16[768,512]{1,0:T(8,128)(2,1)S(1)} %collective-permute-done.4.refs_6_.refs_2_), channel_id=1, source_target_pairs={{0,1},{1,0},{2,3},{3,2},{4,5},{5,4},{6,7},{7,6},{8,9},{9,8},{10,11... | collective-permute-start | bytes 2359304 | tf_op jit(solution)/shard_map/ppermute | solution.py:265
  50.9 26.0 %copy-start.3 = (bf16[768,512]{1,0:T(8,128)(2,1)}, bf16[768,512]{1,0:T(8,128)(2,1)S(1)}, u32[]{:S(2)}) copy-start(bf16[768,512]{1,0:T(8,128)(2,1)S(1)} %collective-permute-done.3.refs_5_.refs_1_) | copy-start | bytes 2359300
  52.7 0.9 copy-start.4
  76.8 35.0 %all-to-all-start = ((bf16[16,4,16,1024]{3,2,1,0:T(8,128)(2,1)}), bf16[16,4,16,1024]{3,2,1,0:T(8,128)(2,1)}, u32[]{:S(2)}, u32[]{:S(2)}) async-start(bf16[16,4,16,1024]{3,2,1,0:T(8,128)(2,1)} %get-tuple-element.23), calls=%async_computation | async-start | bytes 4194304 | tf_op jit(solution)/shard_map/all_to_all | solution.py:279
  119.0 19.8 %all-to-all-start.1 = ((bf16[16,4,16,512]{3,2,1,0:T(8,128)(2,1)}), bf16[16,4,16,512]{3,2,1,0:T(8,128)(2,1)S(1)}, u32[]{:S(2)}, u32[]{:S(2)}) async-start(bf16[16,4,16,512]{3,2,1,0:T(8,128)(2,1)} %get-tuple-element.30), calls=%async_computation.1 | async-start | bytes 2097152 | tf_op jit(solution)/shard_map/all_to_all | solution.py:306
  128.3 10.4 %collective-permute-start.6 = (bf16[256,1536]{1,0:T(8,128)(2,1)}, bf16[256,1536]{1,0:T(8,128)(2,1)S(1)}, u32[]{:S(2)}, u32[]{:S(2)}) collective-permute-start(bf16[256,1536]{1,0:T(8,128)(2,1)} %back.1.a0), channel_id=1, source_target_pairs={{0,1},{1,0},{2,3},{3,2},{4,5},{5,4},{6,7},{7,6},{8,9},{9,8},{10,11... | collective-permute-start | bytes 2359304 | tf_op jit(solution)/shard_map/ppermute | solution.py:304
  133.6 21.7 %collective-permute-start.7 = (bf16[256,1536]{1,0:T(8,128)(2,1)}, bf16[256,1536]{1,0:T(8,128)(2,1)}, u32[]{:S(2)}, u32[]{:S(2)}) collective-permute-start(bf16[256,1536]{1,0:T(8,128)(2,1)} %back.1.a0), channel_id=1, source_target_pairs={{0,2},{2,0},{1,3},{3,1},{4,6},{6,4},{5,7},{7,5},{8,10},{10,8},{9,1... | collective-permute-start | bytes 2359304 | tf_op jit(solution)/shard_map/ppermute | solution.py:303
  138.7 0.9 copy-start.5
  138.8 7.8 %copy-start.1 = (f32[192,256]{1,0:T(8,128)S(1)}, f32[192,256]{1,0:T(8,128)}, u32[]{:S(2)}) copy-start(f32[192,256]{1,0:T(8,128)} %get-tuple-element.35.share_ref) | copy-start | bytes 589828
  139.6 38.1 %all-to-all-start.2 = ((bf16[4,16,16,1024]{3,2,1,0:T(8,128)(2,1)}), bf16[4,16,16,1024]{3,2,1,0:T(8,128)(2,1)}, u32[]{:S(2)}, u32[]{:S(2)}) async-start(bf16[4,16,16,1024]{3,2,1,0:T(8,128)(2,1)} %bitcast.14), calls=%async_computation.2 | async-start | bytes 4194304 | tf_op jit(solution)/shard_map/all_to_all | solution.py:310
  146.6 46.0 %reduce-scatter.2.cloned.1.call-start = ((), (), s32[]{:S(2)}) async-start(), calls=%async_computation.7 | async-start | bytes 884736 | tf_op jit(solution)/shard_map/reduce_scatter | solution.py:315
  155.3 5.0 %collective-permute-start.8 = (bf16[256,1536]{1,0:T(8,128)(2,1)}, bf16[256,1536]{1,0:T(8,128)(2,1)S(1)}, u32[]{:S(2)}, u32[]{:S(2)}) collective-permute-start(bf16[256,1536]{1,0:T(8,128)(2,1)} %collective-permute-done.7.a2), channel_id=1, source_target_pairs={{0,1},{1,0},{2,3},{3,2},{4,5},{5,4},{6,7},{7,6},{8,9},{9,8},{10,11... | collective-permute-start | bytes 2359304 | tf_op jit(solution)/shard_map/ppermute | solution.py:311
  160.2 17.5 %copy-start.6 = (bf16[256,1536]{1,0:T(8,128)(2,1)}, bf16[256,1536]{1,0:T(8,128)(2,1)S(1)}, u32[]{:S(2)}) copy-start(bf16[256,1536]{1,0:T(8,128)(2,1)S(1)} %collective-permute-done.8.a3) | copy-start | bytes 2359300
  183.7 95.7 %copy-start = (s32[128]{0:T(128)S(1)}, s32[128]{0:T(128)}, u32[]{:S(2)}) copy-start(s32[128]{0:T(128)} %partner_ref.1) | copy-start | bytes 1540
Sparse Core Ops, SparseCore 0:
  10.1 61.9 all-gather.1
  150.8 41.7 reduce-scatter.1
